TPU v7x, 32 devices: a whole 2x2x4 slice. The times are simulated.
32 devices in a mesh: dp: 8 (over y, x, core), group: 4 (over z).
Axes of the slice: x: 2, y: 2, z: 4, core: 2. Of those that a mesh axis runs over, the one named last changes fastest.
Arguments:
- tokens: bfloat16 [32768, 1024], P(('dp', 'group')), may hold values from -6 to 6
- cotangent: bfloat16 [32768, 1024], P(('dp', 'group')), may hold values from -6 to 6
- order: int32 [4, 8], P('group'), may hold values from 0 to 7, each once within a row
- lengths: int32 [8, 4, 4], P(None, 'group'), may hold values from 1 to 960, 1024 in all within a row
- adapter_ids: int32 [8, 4, 4], P(None, 'group'), may hold values from 0 to 7
- norm_gain: float32 [1024], replicated, may hold values from 0.5 to 1.5
- ffn_gain: float32 [1024], replicated, may hold values from 0.5 to 1.5
- conv_weight: float32 [3, 1024], replicated, may hold values from -3.5 to 3.5
- in_weight: bfloat16 [1024, 3072], P(None, 'group'), may hold values from -0.1875 to 0.1875
- out_weight: bfloat16 [1024, 1024], P(None, 'group'), may hold values from -0.1875 to 0.1875
- gate_weight: bfloat16 [1024, 4608], P(None, 'group'), may hold values from -0.1875 to 0.1875
- up_weight: bfloat16 [1024, 4608], P(None, 'group'), may hold values from -0.1875 to 0.1875
- down_weight: bfloat16 [4608, 1024], P(None, 'group'), may hold values from -0.09375 to 0.09375
- input_first_factor: bfloat16 [1024, 128], replicated, may hold values from -0.1875 to 0.1875
- input_second_factor: bfloat16 [128, 3072], replicated, may hold values from -0.75 to 0.75
- output_first_factor: bfloat16 [1024, 128], replicated, may hold values from -0.1875 to 0.1875
- output_second_factor: bfloat16 [128, 1024], replicated, may hold values from -0.75 to 0.75
- gate_first_factor: bfloat16 [1024, 128], replicated, may hold values from -0.1875 to 0.1875
- gate_second_factor: bfloat16 [128, 4608], replicated, may hold values from -0.75 to 0.75
- up_first_factor: bfloat16 [1024, 128], replicated, may hold values from -0.1875 to 0.1875
- up_second_factor: bfloat16 [128, 4608], replicated, may hold values from -0.75 to 0.75
- down_first_factor: bfloat16 [4608, 128], replicated, may hold values from -0.09375 to 0.09375
- down_second_factor: bfloat16 [128, 1024], replicated, may hold values from -0.75 to 0.75
Outputs:
- block_output: bfloat16 [32768, 1024], P(('dp', 'group'))
- input_grad: bfloat16 [32768, 1024], P(('dp', 'group'))
- grad_in_a: float32 [1024, 128], P('group')
- grad_in_b: float32 [128, 3072], P(None, 'group')
- grad_out_a: float32 [1024, 128], P('group')
- grad_out_b: float32 [128, 1024], P(None, 'group')
- grad_gate_a: float32 [1024, 128], P('group')
- grad_gate_b: float32 [128, 4608], P(None, 'group')
- grad_up_a: float32 [1024, 128], P('group')
- grad_up_b: float32 [128, 4608], P(None, 'group')
- grad_down_a: float32 [4608, 128], P('group')
- grad_down_b: float32 [128, 1024], P(None, 'group')
Inputs may be any that keep to these rules, and one draw needn't show every extreme that they name: Each row of order is a permutation. The 4 lengths of a pack sum to 1024; every draw has a sequence of exactly 960.
All inputs are finite; a program needn't handle non-finite values.
Results may differ from a plain program's by a relative error of at most 0.017.
Values may be sent and summed in bfloat16 or wider, within the bound.
No kernel may reach another device: no remote copies, remote signals or barrier semaphores. Data moves between devices by JAX's collectives and lax.ppermute only.
A program may use at most 320 MiB of HBM per device.

v0:
```python
import jax
import jax.numpy as jnp
from jax import lax
from jax.sharding import PartitionSpec as P

ADAPTER_RANK = 16


eps_norm = 1e-05
adapter_scale = 2.0


def matrix_product(left, right):
    return jnp.dot(left, right, preferred_element_type=jnp.float32)


def transposed_left_matmul(left, right):
    return lax.dot_general(
        left, right, (((0,), (0,)), ((), ())), preferred_element_type=jnp.float32
    )


def transposed_right_matmul(left, right):
    return lax.dot_general(
        left, right, (((1,), (1,)), ((), ())), preferred_element_type=jnp.float32
    )


def per_token_tables(
    sequence_length_row, adapter_index_row, count_of_rows, adapter_column_span, adapter_rank_size
):
    finish = jnp.cumsum(sequence_length_row)
    starts = finish - sequence_length_row
    counter = jnp.arange(count_of_rows, dtype=jnp.int32)
    member = ((counter[:, None] >= starts[None, :]) & (counter[:, None] < finish[None, :])).astype(
        jnp.int32
    )
    beginning = jnp.sum(member * starts[None, :], axis=1)
    position = counter - beginning
    chosen = jnp.sum(member * adapter_index_row[None, :], axis=1)
    column_span = jnp.arange(adapter_column_span, dtype=jnp.int32) // adapter_rank_size
    select_adapter = (column_span[None, :] == chosen[:, None]).astype(jnp.bfloat16)
    after_one = (position >= 1).astype(jnp.float32)[:, None]
    after_two = (position >= 2).astype(jnp.float32)[:, None]
    return (select_adapter, after_one, after_two)


def delayed(values, amount):
    return jnp.concatenate(
        [jnp.zeros((amount, values.shape[1]), values.dtype), values[:-amount]], axis=0
    )


def advanced(values, amount):
    return jnp.concatenate(
        [values[amount:], jnp.zeros((amount, values.shape[1]), values.dtype)], axis=0
    )


def regroup(values, picks, pieces):
    shaped = values.reshape(pieces, values.shape[0] // pieces, values.shape[1])
    return jnp.take(shaped, picks, axis=0).reshape(values.shape)


def inverse_root(values):
    return lax.rsqrt(jnp.mean(values * values, axis=-1, keepdims=True) + eps_norm)


def norm_back(values, inverse, gain, incoming_gradient):
    scaled = gain * incoming_gradient
    return inverse * scaled - values * (inverse * inverse * inverse) * jnp.mean(
        values * scaled, axis=-1, keepdims=True
    )


def adapter_project(
    input_rows, frozen_weight, adapter_down_factor, adapter_up_factor, select_adapter
):
    reduced_sum = (
        matrix_product(input_rows, adapter_down_factor).astype(jnp.bfloat16) * select_adapter
    )
    return (
        matrix_product(input_rows, frozen_weight)
        + adapter_scale * matrix_product(reduced_sum, adapter_up_factor),
        reduced_sum,
    )


def adapter_project_backward(
    incoming_gradient,
    input_rows,
    frozen_weight,
    adapter_down_factor,
    adapter_up_factor,
    reduced_sum,
    select_adapter,
):
    gradient_rank_space = incoming_gradient.astype(jnp.bfloat16)
    gradient_up_factor = adapter_scale * transposed_left_matmul(reduced_sum, gradient_rank_space)
    gradient_reduced_sum = (
        adapter_scale
        * transposed_right_matmul(gradient_rank_space, adapter_up_factor)
        * select_adapter
    ).astype(jnp.bfloat16)
    grad_down = transposed_left_matmul(input_rows, gradient_reduced_sum)
    input_gradients = transposed_right_matmul(
        gradient_rank_space, frozen_weight
    ) + transposed_right_matmul(gradient_reduced_sum, adapter_down_factor)
    return (input_gradients, grad_down, gradient_up_factor)


def local(
    tokens,
    cotangent,
    order,
    lengths,
    adapter_ids,
    norm_gain,
    ffn_gain,
    conv_weight,
    in_weight,
    out_weight,
    gate_weight,
    up_weight,
    down_weight,
    input_first_factor,
    input_second_factor,
    output_first_factor,
    output_second_factor,
    gate_first_factor,
    gate_second_factor,
    up_first_factor,
    up_second_factor,
    down_first_factor,
    down_second_factor,
):
    dp_count = lax.axis_size("dp")
    dp_index = lax.axis_index("dp")
    count_of_rows = tokens.shape[0]
    model_width = tokens.shape[1]
    order_row = order[0]
    counting = jnp.arange(dp_count, dtype=jnp.int32)
    inverse_row = jnp.sum(
        jnp.where(order_row[None, :] == counting[:, None], counting[None, :], 0), axis=1
    )
    arrived = lax.all_to_all(tokens, "dp", split_axis=0, concat_axis=0, tiled=True)
    hidden_in = lax.all_to_all(
        regroup(arrived, order_row, dp_count), "dp", split_axis=0, concat_axis=0, tiled=True
    )
    pack_source = order_row[dp_index]
    sequence_length_row = lengths[:, 0, :][pack_source]
    adapter_index_row = adapter_ids[:, 0, :][pack_source]
    select_adapter, after_one, after_two = per_token_tables(
        sequence_length_row,
        adapter_index_row,
        count_of_rows,
        input_first_factor.shape[1],
        ADAPTER_RANK,
    )
    shards = (in_weight, out_weight, gate_weight, up_weight, down_weight)
    full_in, full_out, full_gate, full_up, full_down = (
        lax.all_gather(shards[0], "group", axis=1, tiled=True),
        lax.all_gather(shards[1], "group", axis=1, tiled=True),
        lax.all_gather(shards[2], "group", axis=1, tiled=True),
        lax.all_gather(shards[3], "group", axis=1, tiled=True),
        lax.all_gather(shards[4], "group", axis=1, tiled=True),
    )
    hidden32 = hidden_in.astype(jnp.float32)
    inverse_one = inverse_root(hidden32)
    normed = (hidden32 * inverse_one * norm_gain).astype(jnp.bfloat16)
    mixed_in, reduced_in = adapter_project(
        normed, full_in, input_first_factor, input_second_factor, select_adapter
    )
    input_gate = mixed_in[:, :model_width]
    output_gate = mixed_in[:, model_width : 2 * model_width]
    conv_input = mixed_in[:, 2 * model_width :]
    gated = input_gate * conv_input
    convolved = (
        conv_weight[2] * gated
        + conv_weight[1] * delayed(gated, 1) * after_one
        + conv_weight[0] * delayed(gated, 2) * after_two
    )
    mixer = (output_gate * convolved).astype(jnp.bfloat16)
    branch, reduced_out = adapter_project(
        mixer, full_out, output_first_factor, output_second_factor, select_adapter
    )
    middle = hidden32 + branch
    inverse_two = inverse_root(middle)
    normed_two = (middle * inverse_two * ffn_gain).astype(jnp.bfloat16)
    gate_pre, reduced_gate = adapter_project(
        normed_two, full_gate, gate_first_factor, gate_second_factor, select_adapter
    )
    up_pre, reduced_up = adapter_project(
        normed_two, full_up, up_first_factor, up_second_factor, select_adapter
    )
    sigmoid_gate = jax.nn.sigmoid(gate_pre)
    activated = (gate_pre * sigmoid_gate * up_pre).astype(jnp.bfloat16)
    ffn_out, reduced_down = adapter_project(
        activated, full_down, down_first_factor, down_second_factor, select_adapter
    )
    result = (middle + ffn_out).astype(jnp.bfloat16)
    back_in, back_out, back_gate, back_up, back_down = (
        lax.all_gather(shards[0], "group", axis=1, tiled=True),
        lax.all_gather(shards[1], "group", axis=1, tiled=True),
        lax.all_gather(shards[2], "group", axis=1, tiled=True),
        lax.all_gather(shards[3], "group", axis=1, tiled=True),
        lax.all_gather(shards[4], "group", axis=1, tiled=True),
    )
    upstream32 = cotangent.astype(jnp.float32)
    grad_act, down_a_grad, down_b_grad = adapter_project_backward(
        upstream32,
        activated,
        back_down,
        down_first_factor,
        down_second_factor,
        reduced_down,
        select_adapter,
    )
    grad_gate_pre = grad_act * up_pre * (sigmoid_gate * (1.0 + gate_pre * (1.0 - sigmoid_gate)))
    grad_up_pre = grad_act * gate_pre * sigmoid_gate
    grad_from_gate, gate_a_grad, gate_b_grad = adapter_project_backward(
        grad_gate_pre,
        normed_two,
        back_gate,
        gate_first_factor,
        gate_second_factor,
        reduced_gate,
        select_adapter,
    )
    grad_from_up, up_a_grad, up_b_grad = adapter_project_backward(
        grad_up_pre,
        normed_two,
        back_up,
        up_first_factor,
        up_second_factor,
        reduced_up,
        select_adapter,
    )
    grad_middle = upstream32 + norm_back(
        middle, inverse_two, ffn_gain, grad_from_gate + grad_from_up
    )
    grad_mixer, out_a_grad, out_b_grad = adapter_project_backward(
        grad_middle,
        mixer,
        back_out,
        output_first_factor,
        output_second_factor,
        reduced_out,
        select_adapter,
    )
    grad_output_gate = grad_mixer * convolved
    grad_conv = grad_mixer * output_gate
    grad_gated = (
        conv_weight[2] * grad_conv
        + conv_weight[1] * advanced(grad_conv * after_one, 1)
        + conv_weight[0] * advanced(grad_conv * after_two, 2)
    )
    grad_mixed = jnp.concatenate(
        [grad_gated * conv_input, grad_output_gate, grad_gated * input_gate], axis=1
    )
    grad_normed, in_a_grad, in_b_grad = adapter_project_backward(
        grad_mixed,
        normed,
        back_in,
        input_first_factor,
        input_second_factor,
        reduced_in,
        select_adapter,
    )
    grad_input = (grad_middle + norm_back(hidden32, inverse_one, norm_gain, grad_normed)).astype(
        jnp.bfloat16
    )
    grad_terms = (
        in_a_grad,
        in_b_grad,
        out_a_grad,
        out_b_grad,
        gate_a_grad,
        gate_b_grad,
        up_a_grad,
        up_b_grad,
        down_a_grad,
        down_b_grad,
    )
    owned = (
        lax.psum_scatter(
            grad_terms[0].astype(jnp.bfloat16), "group", scatter_dimension=0, tiled=True
        ).astype(jnp.float32),
        lax.psum_scatter(
            grad_terms[1].astype(jnp.bfloat16), "group", scatter_dimension=1, tiled=True
        ).astype(jnp.float32),
        lax.psum_scatter(
            grad_terms[2].astype(jnp.bfloat16), "group", scatter_dimension=0, tiled=True
        ).astype(jnp.float32),
        lax.psum_scatter(
            grad_terms[3].astype(jnp.bfloat16), "group", scatter_dimension=1, tiled=True
        ).astype(jnp.float32),
        lax.psum_scatter(
            grad_terms[4].astype(jnp.bfloat16), "group", scatter_dimension=0, tiled=True
        ).astype(jnp.float32),
        lax.psum_scatter(
            grad_terms[5].astype(jnp.bfloat16), "group", scatter_dimension=1, tiled=True
        ).astype(jnp.float32),
        lax.psum_scatter(
            grad_terms[6].astype(jnp.bfloat16), "group", scatter_dimension=0, tiled=True
        ).astype(jnp.float32),
        lax.psum_scatter(
            grad_terms[7].astype(jnp.bfloat16), "group", scatter_dimension=1, tiled=True
        ).astype(jnp.float32),
        lax.psum_scatter(
            grad_terms[8].astype(jnp.bfloat16), "group", scatter_dimension=0, tiled=True
        ).astype(jnp.float32),
        lax.psum_scatter(
            grad_terms[9].astype(jnp.bfloat16), "group", scatter_dimension=1, tiled=True
        ).astype(jnp.float32),
    )
    totals = (
        lax.psum(owned[0].astype(jnp.bfloat16), "dp").astype(jnp.float32),
        lax.psum(owned[1].astype(jnp.bfloat16), "dp").astype(jnp.float32),
        lax.psum(owned[2].astype(jnp.bfloat16), "dp").astype(jnp.float32),
        lax.psum(owned[3].astype(jnp.bfloat16), "dp").astype(jnp.float32),
        lax.psum(owned[4].astype(jnp.bfloat16), "dp").astype(jnp.float32),
        lax.psum(owned[5].astype(jnp.bfloat16), "dp").astype(jnp.float32),
        lax.psum(owned[6].astype(jnp.bfloat16), "dp").astype(jnp.float32),
        lax.psum(owned[7].astype(jnp.bfloat16), "dp").astype(jnp.float32),
        lax.psum(owned[8].astype(jnp.bfloat16), "dp").astype(jnp.float32),
        lax.psum(owned[9].astype(jnp.bfloat16), "dp").astype(jnp.float32),
    )
    going = (
        lax.all_to_all(result, "dp", split_axis=0, concat_axis=0, tiled=True),
        lax.all_to_all(grad_input, "dp", split_axis=0, concat_axis=0, tiled=True),
    )
    going = (regroup(going[0], inverse_row, dp_count), regroup(going[1], inverse_row, dp_count))
    result, grad_input = (
        lax.all_to_all(going[0], "dp", split_axis=0, concat_axis=0, tiled=True),
        lax.all_to_all(going[1], "dp", split_axis=0, concat_axis=0, tiled=True),
    )
    return (
        result,
        grad_input,
        totals[0],
        totals[1],
        totals[2],
        totals[3],
        totals[4],
        totals[5],
        totals[6],
        totals[7],
        totals[8],
        totals[9],
    )


def solution(mesh):
    in_specs = (
        P(("dp", "group"), None),
        P(("dp", "group"), None),
        P("group", None),
        P(None, "group", None),
        P(None, "group", None),
        P(),
        P(),
        P(),
        P(None, "group"),
        P(None, "group"),
        P(None, "group"),
        P(None, "group"),
        P(None, "group"),
        P(),
        P(),
        P(),
        P(),
        P(),
        P(),
        P(),
        P(),
        P(),
        P(),
    )
    out_specs = (
        P(("dp", "group"), None),
        P(("dp", "group"), None),
        P("group", None),
        P(None, "group"),
        P("group", None),
        P(None, "group"),
        P("group", None),
        P(None, "group"),
        P("group", None),
        P(None, "group"),
        P("group", None),
        P(None, "group"),
    )
    return jax.shard_map(local, mesh=mesh, in_specs=in_specs, out_specs=out_specs, check_vma=False)
```

profile of v0, /device:TPU:0, one launch (start us, length us, event | category | flops | bytes accessed | tf_op | source)
XLA Modules:
  0.0 1087.4 jit_solution(8852656804332261047)
XLA Ops:
  10.0 5.2 all-to-all-start
  15.2 26.6 %all-to-all-done = bf16[8,128,1024]{2,1,0:T(8,128)(2,1)S(1)} async-done(((bf16[8,128,1024]{2,1,0:T(8,128)(2,1)}), bf16[8,128,1024]{2,1,0:T(8,128)(2,1)S(1)}, u32[]{:S(2)}, u32[]{:S(2)}) %all-to-all-start) | async-done | bytes 2097184 | tf_op jit(solution)/shard_map/all_to_all | solution.py:146
  60.3 17.0 %all-to-all-done.1 = bf16[8,128,1024]{2,1,0:T(8,128)(2,1)S(1)} async-done(((bf16[8,128,1024]{2,1,0:T(8,128)(2,1)}), bf16[8,128,1024]{2,1,0:T(8,128)(2,1)S(1)}, u32[]{:S(2)}, u32[]{:S(2)}) %all-to-all-start.1) | async-done | bytes 2097184 | tf_op jit(solution)/shard_map/all_to_all | solution.py:147
  82.9 44.8 %all-gather.6.cloned.1.call-done = bf16[1024,3072]{1,0:T(8,128)(2,1)} async-done(((bf16[1024,768]{1,0:T(8,128)(2,1)}), bf16[1024,3072]{1,0:T(8,128)(2,1)}) %all-gather.6.cloned.1.call-update) | async-done | bytes 6291472 | tf_op jit(solution)/shard_map/all_gather | solution.py:162
  127.7 9.9 fusion.30
  151.3 22.4 %all-gather.8.cloned.1.call-done = bf16[1024,1024]{1,0:T(8,128)(2,1)} async-done(((bf16[1024,256]{1,0:T(8,128)(2,1)}), bf16[1024,1024]{1,0:T(8,128)(2,1)}) %all-gather.8.cloned.1.call-update) | async-done | bytes 2097168 | tf_op jit(solution)/shard_map/all_gather | solution.py:163
  183.0 157.3 %all-gather.12.cloned.1.call-done = bf16[1024,4608]{1,0:T(8,128)(2,1)} async-done(((bf16[1024,1152]{1,0:T(8,128)(2,1)}), bf16[1024,4608]{1,0:T(8,128)(2,1)}) %all-gather.12.cloned.1.call-update) | async-done | bytes 9437200 | tf_op jit(solution)/shard_map/all_gather | solution.py:165
  340.4 16.4 %fusion.33 = f32[1024,4608]{1,0:T(8,128)} fusion(bf16[1024,1024]{1,0:T(8,128)(2,1)S(1)} %multiply_convert_fusion.6, bf16[1024,4608]{1,0:T(8,128)(2,1)} %all-gather.12.cloned.1.call-done), kind=kOutput, calls=%fused_computation.126 | convolution fusion | flops 9663676416 | bytes 30408704 | tf_op jit(solution)/shard_map/dot_general | solution.py:14
  356.7 12.9 %multiply_add_fusion = f32[1024,4608]{1,0:T(8,128)} fusion(f32[1024,4608]{1,0:T(8,128)} %fusion.33, bf16[1024,128]{1,0:T(8,128)(2,1)S(1)} %compare_select_fusion.1, bf16[128,4608]{1,0:T(8,128)(2,1)S(1)} %copy-done.19), kind=kOutput, calls=%fused_computation.6 | convolution fusion | flops 1217396736 | bytes 39190528 | tf_op jit(solution)/shard_map/dot_general | solution.py:14
  369.6 136.6 %all-gather.14.cloned.1.call-done = bf16[4608,1024]{1,0:T(8,128)(2,1)} async-done(((bf16[4608,256]{1,0:T(8,128)(2,1)}), bf16[4608,1024]{1,0:T(8,128)(2,1)}) %all-gather.14.cloned.1.call-update) | async-done | bytes 9437200 | tf_op jit(solution)/shard_map/all_gather | solution.py:166
  506.3 16.9 %fusion.35 = f32[1024,4608]{1,0:T(8,128)} fusion(bf16[1024,1024]{1,0:T(8,128)(2,1)} %param.26, bf16[4608,1024]{1,0:T(8,128)(2,1)} %all-gather.14.cloned.1.call-done), kind=kOutput, calls=%fused_computation.128 | convolution fusion | flops 9663676416 | bytes 30408704 | tf_op jit(solution)/shard_map/dot_general | solution.py:24
  523.2 12.4 %convolution_add_fusion = f32[1024,4608]{1,0:T(8,128)} fusion(f32[1024,4608]{1,0:T(8,128)} %fusion.35, bf16[1024,128]{1,0:T(8,128)(2,1)S(1)} %copy-done.29, bf16[4608,128]{1,0:T(8,128)(2,1)S(1)} %copy-done.18), kind=kOutput, calls=%fused_computation.10 | convolution fusion | flops 1212678144 | bytes 39190528 | tf_op jit(solution)/shard_map/dot_general | solution.py:24
  535.6 137.1 %all-gather.10.cloned.1.call-done = bf16[1024,4608]{1,0:T(8,128)(2,1)} async-done(((bf16[1024,1152]{1,0:T(8,128)(2,1)}), bf16[1024,4608]{1,0:T(8,128)(2,1)}) %all-gather.10.cloned.1.call-update) | async-done | bytes 9437200 | tf_op jit(solution)/shard_map/all_gather | solution.py:164
  672.7 16.2 %fusion.32 = f32[1024,4608]{1,0:T(8,128)} fusion(bf16[1024,1024]{1,0:T(8,128)(2,1)S(1)} %multiply_convert_fusion.6, bf16[1024,4608]{1,0:T(8,128)(2,1)} %all-gather.10.cloned.1.call-done), kind=kOutput, calls=%fused_computation.125 | convolution fusion | flops 9663676416 | bytes 30408704 | tf_op jit(solution)/shard_map/dot_general | solution.py:14
  689.0 28.3 %multiply_convert_fusion.1 = (bf16[1024,4608]{1,0:T(8,128)(2,1)}, bf16[1024,4608]{1,0:T(8,128)(2,1)}, bf16[1024,4608]{1,0:T(8,128)(2,1)}) fusion(f32[1024,4608]{1,0:T(8,128)} %convolution_add_fusion, f32[1024,4608]{1,0:T(8,128)} %multiply_add_fusion, f32[1024,4608]{1,0:T(8,128)} %fusion.32, bf16[1024,128]{1,0:T(8,128)(2,1)S(1)} %copy-done.34, ...), kind=kOutput, calls=%fused_computation.4 | convolution fusion | flops 1292894208 | bytes 86376448 | tf_op jit(solution)/shard_map/dot_general | solution.py:14
  717.2 6.1 fusion.1
  725.8 6.7 compare_select_fusion
  732.6 16.6 %fusion.34 = f32[1024,1024]{1,0:T(8,128)} fusion(bf16[1024,4608]{1,0:T(8,128)(2,1)} %get-tuple-element.30, bf16[4608,1024]{1,0:T(8,128)(2,1)} %all-gather.14.cloned.1.call-done), kind=kOutput, calls=%fused_computation.127 | convolution fusion | flops 9663676416 | bytes 23068672 | tf_op jit(solution)/shard_map/dot_general | solution.py:14
  754.1 5.5 add_convert_fusion
  764.1 6.3 fusion.22
  773.1 6.3 fusion.21
  779.4 14.2 %fusion.36 = f32[1024,1024]{1,0:T(8,128)S(1)} fusion(bf16[1024,4608]{1,0:T(8,128)(2,1)} %get-tuple-element.29, bf16[1024,4608]{1,0:T(8,128)(2,1)} %all-gather.10.cloned.1.call-done), kind=kOutput, calls=%fused_computation.129 | convolution fusion | flops 9663676416 | bytes 23068672 | tf_op jit(solution)/shard_map/dot_general | solution.py:24
  793.7 14.2 %fusion.38 = f32[1024,1024]{1,0:T(8,128)S(1)} fusion(bf16[1024,4608]{1,0:T(8,128)(2,1)} %get-tuple-element.31, bf16[1024,4608]{1,0:T(8,128)(2,1)} %all-gather.12.cloned.1.call-done), kind=kOutput, calls=%fused_computation.131 | convolution fusion | flops 9663676416 | bytes 23068672 | tf_op jit(solution)/shard_map/dot_general | solution.py:24
  826.5 5.4 fusion.26
  845.0 8.4 multiply_convert_fusion.5
  857.6 10.5 fusion.28
  892.4 13.8 %all-to-all-done.4 = bf16[8,128,1024]{2,1,0:T(8,128)(2,1)} async-done(((bf16[8,128,1024]{2,1,0:T(8,128)(2,1)}), bf16[8,128,1024]{2,1,0:T(8,128)(2,1)}, u32[]{:S(2)}, u32[]{:S(2)}) %all-to-all-start.4) | async-done | bytes 2097184 | tf_op jit(solution)/shard_map/all_to_all | solution.py:331
  917.7 7.4 convolution_convert_fusion
  925.2 19.1 %all-to-all-done.3 = bf16[8,128,1024]{2,1,0:T(8,128)(2,1)S(1)} async-done(((bf16[8,128,1024]{2,1,0:T(8,128)(2,1)}), bf16[8,128,1024]{2,1,0:T(8,128)(2,1)S(1)}, u32[]{:S(2)}, u32[]{:S(2)}) %all-to-all-start.3) | async-done | bytes 2097184 | tf_op jit(solution)/shard_map/all_to_all | solution.py:335
  952.4 12.0 %reduce-scatter.17.cloned.1.call-done = bf16[128,768]{1,0:T(8,128)(2,1)} async-done(((bf16[128,3072]{1,0:T(8,128)(2,1)}), bf16[128,768]{1,0:T(8,128)(2,1)}) %reduce-scatter.17.cloned.1.call-update) | async-done | bytes 196624 | tf_op jit(solution)/shard_map/reduce_scatter | solution.py:289
  964.4 30.6 %reduce-scatter.27.cloned.1.call-done = bf16[1152,128]{1,0:T(8,128)(2,1)} async-done(((bf16[4608,128]{1,0:T(8,128)(2,1)}), bf16[1152,128]{1,0:T(8,128)(2,1)}) %reduce-scatter.27.cloned.1.call-update) | async-done | bytes 294928 | tf_op jit(solution)/shard_map/reduce_scatter | solution.py:310
  995.1 65.8 %all-reduce.7.cloned.1.call-done = (bf16[256,128]{1,0:T(8,128)(2,1)}, bf16[128,768]{1,0:T(8,128)(2,1)}, bf16[256,128]{1,0:T(8,128)(2,1)}, bf16[128,256]{1,0:T(8,...) async-done(((bf16[256,128]{1,0:T(8,128)(2,1)}, ...) | async-done | bytes 1474576 | tf_op jit(solution)/shard_map/psum | solution.py:318
  (287 shorter events, 161.1 us)
Async XLA Ops:
  7.2 681.8 %copy-start = (bf16[128,4608]{1,0:T(8,128)(2,1)S(1)}, bf16[128,4608]{1,0:T(8,128)(2,1)}, u32[]{:S(2)}) copy-start(bf16[128,4608]{1,0:T(8,128)(2,1)} %param.43) | copy-start | bytes 3538948
  7.2 120.5 %all-gather.6.cloned.1.call-start = ((), (), s32[]{:S(2)}) async-start(), calls=%async_computation.16 | async-start | bytes 7864320 | tf_op jit(solution)/shard_map/all_gather | solution.py:162
  7.9 165.8 %all-gather.8.cloned.1.call-start = ((), (), s32[]{:S(2)}) async-start(), calls=%async_computation.17 | async-start | bytes 2621440 | tf_op jit(solution)/shard_map/all_gather | solution.py:163
  8.7 331.7 %all-gather.12.cloned.1.call-start = ((), (), s32[]{:S(2)}) async-start(), calls=%async_computation.19 | async-start | bytes 11796480 | tf_op jit(solution)/shard_map/all_gather | solution.py:165
  9.4 496.8 %all-gather.14.cloned.1.call-start = ((), (), s32[]{:S(2)}) async-start(), calls=%async_computation.20 | async-start | bytes 11796480 | tf_op jit(solution)/shard_map/all_gather | solution.py:166
  10.0 31.8 %all-to-all-start = ((bf16[8,128,1024]{2,1,0:T(8,128)(2,1)}), bf16[8,128,1024]{2,1,0:T(8,128)(2,1)S(1)}, u32[]{:S(2)}, u32[]{:S(2)}) async-start(bf16[8,128,1024]{2,1,0:T(8,128)(2,1)} %bitcast.128), calls=%async_computation | async-start | bytes 4194304 | tf_op jit(solution)/shard_map/all_to_all | solution.py:146
  47.0 30.3 %all-to-all-start.1 = ((bf16[8,128,1024]{2,1,0:T(8,128)(2,1)}), bf16[8,128,1024]{2,1,0:T(8,128)(2,1)S(1)}, u32[]{:S(2)}, u32[]{:S(2)}) async-start(bf16[8,128,1024]{2,1,0:T(8,128)(2,1)} %broadcast_select_fusion.2), calls=%async_computation.1 | async-start | bytes 4194304 | tf_op jit(solution)/shard_map/all_to_all | solution.py:147
  50.8 621.9 %all-gather.10.cloned.1.call-start = ((), (), s32[]{:S(2)}) async-start(), calls=%async_computation.18 | async-start | bytes 11796480 | tf_op jit(solution)/shard_map/all_gather | solution.py:164
  51.4 897.3 %reduce-scatter.33.cloned.1.call-start = ((), (), s32[]{:S(2)}) async-start(), calls=%async_computation.30 | async-start | bytes 1474560
  60.3 80.5 %copy-start.47 = (f32[1,1024]{1,0:T(1,128)}, f32[1,1024]{1,0:T(1,128)S(1)}, u32[]{:S(2)}) copy-start(f32[1,1024]{1,0:T(1,128)S(1)} %get-tuple-element.34) | copy-start | bytes 12292
  60.3 80.5 %copy-start.49 = (f32[1,1024]{1,0:T(1,128)}, f32[1,1024]{1,0:T(1,128)S(1)}, u32[]{:S(2)}) copy-start(f32[1,1024]{1,0:T(1,128)S(1)} %get-tuple-element.35) | copy-start | bytes 12292
  60.3 80.5 %copy-start.51 = (f32[1,1024]{1,0:T(1,128)}, f32[1,1024]{1,0:T(1,128)S(1)}, u32[]{:S(2)}) copy-start(f32[1,1024]{1,0:T(1,128)S(1)} %get-tuple-element.36) | copy-start | bytes 12292
  77.3 101.0 %copy-start.4 = (bf16[8,128,1024]{2,1,0:T(8,128)(2,1)}, bf16[8,128,1024]{2,1,0:T(8,128)(2,1)S(1)}, u32[]{:S(2)}) copy-start(bf16[8,128,1024]{2,1,0:T(8,128)(2,1)S(1)} %all-to-all-done.1) | copy-start | bytes 6291460
  82.9 54.7 %copy-start.31 = (bf16[1024,128]{1,0:T(8,128)(2,1)}, bf16[1024,128]{1,0:T(8,128)(2,1)S(1)}, u32[]{:S(2)}) copy-start(bf16[1024,128]{1,0:T(8,128)(2,1)S(1)} %compare_select_fusion.4) | copy-start | bytes 786436
  151.3 27.0 %copy-start.21 = (bf16[128,1024]{1,0:T(8,128)(2,1)S(1)}, bf16[128,1024]{1,0:T(8,128)(2,1)}, u32[]{:S(2)}) copy-start(bf16[128,1024]{1,0:T(8,128)(2,1)} %param.41) | copy-start | bytes 786436
  725.8 23.4 %slice-start = ((s8[9437184]{0:T(1024)(128)(4,1)}), s8[4194304]{0:T(1024)(128)(4,1)S(1)}, s32[]{:S(2)}) async-start(s8[9437184]{0:T(1024)(128)(4,1)} %bitcast.121), calls=%async_computation.32 | async-start | bytes 8388608
  732.5 21.6 %copy-start.23 = (bf16[1024,128]{1,0:T(8,128)(2,1)}, bf16[1024,128]{1,0:T(8,128)(2,1)S(1)}, u32[]{:S(2)}) copy-start(bf16[1024,128]{1,0:T(8,128)(2,1)S(1)} %compare_select_fusion) | copy-start | bytes 786436
  759.6 115.2 %all-to-all-start.2 = ((bf16[8,128,1024]{2,1,0:T(8,128)(2,1)}), bf16[8,128,1024]{2,1,0:T(8,128)(2,1)}, u32[]{:S(2)}, u32[]{:S(2)}) async-start(bf16[8,128,1024]{2,1,0:T(8,128)(2,1)} %bitcast.125), calls=%async_computation.2 | async-start | bytes 4194304 | tf_op jit(solution)/shard_map/all_to_all | solution.py:330
  764.0 186.5 %reduce-scatter.31.cloned.1.call-start = ((), (), s32[]{:S(2)}) async-start(), calls=%async_computation.29 | async-start | bytes 1474560
  779.4 173.0 %reduce-scatter.25.cloned.1.call-start = ((), (), s32[]{:S(2)}) async-start(), calls=%async_computation.26 | async-start | bytes 327680 | tf_op jit(solution)/shard_map/reduce_scatter | solution.py:304
  820.8 131.5 %reduce-scatter.23.cloned.1.call-start = ((), (), s32[]{:S(2)}) async-start(), calls=%async_computation.25 | async-start | bytes 327680 | tf_op jit(solution)/shard_map/reduce_scatter | solution.py:298
  826.2 126.1 %reduce-scatter.19.cloned.1.call-start = ((), (), s32[]{:S(2)}) async-start(), calls=%async_computation.23 | async-start | bytes 327680 | tf_op jit(solution)/shard_map/reduce_scatter | solution.py:292
  835.3 32.9 %copy-start.15 = (bf16[1024,1024]{1,0:T(8,128)(2,1)}, bf16[1024,1024]{1,0:T(8,128)(2,1)S(1)}, u32[]{:S(2)}) copy-start(bf16[1024,1024]{1,0:T(8,128)(2,1)S(1)} %get-tuple-element.32) | copy-start | bytes 6291460
  844.9 107.5 %reduce-scatter.21.cloned.1.call-start = ((), (), s32[]{:S(2)}) async-start(), calls=%async_computation.24 | async-start | bytes 327680 | tf_op jit(solution)/shard_map/reduce_scatter | solution.py:295
  874.8 31.4 %all-to-all-start.4 = ((bf16[8,128,1024]{2,1,0:T(8,128)(2,1)}), bf16[8,128,1024]{2,1,0:T(8,128)(2,1)}, u32[]{:S(2)}, u32[]{:S(2)}) async-start(bf16[8,128,1024]{2,1,0:T(8,128)(2,1)} %bitcast.123), calls=%async_computation.4 | async-start | bytes 4194304 | tf_op jit(solution)/shard_map/all_to_all | solution.py:331
  879.6 72.8 %reduce-scatter.15.cloned.1.call-start = ((), (), s32[]{:S(2)}) async-start(), calls=%async_computation.21 | async-start | bytes 327680 | tf_op jit(solution)/shard_map/reduce_scatter | solution.py:286
  882.1 70.3 %reduce-scatter.29.cloned.1.call-start = ((), (), s32[]{:S(2)}) async-start(), calls=%async_computation.28 | async-start | bytes 327680 | tf_op jit(solution)/shard_map/reduce_scatter | solution.py:313
  885.1 79.3 %reduce-scatter.17.cloned.1.call-start = ((), (), s32[]{:S(2)}) async-start(), calls=%async_computation.22 | async-start | bytes 983040 | tf_op jit(solution)/shard_map/reduce_scatter | solution.py:289
  913.9 30.3 %all-to-all-start.3 = ((bf16[8,128,1024]{2,1,0:T(8,128)(2,1)}), bf16[8,128,1024]{2,1,0:T(8,128)(2,1)S(1)}, u32[]{:S(2)}, u32[]{:S(2)}) async-start(bf16[8,128,1024]{2,1,0:T(8,128)(2,1)} %get-tuple-element.42), calls=%async_computation.3 | async-start | bytes 4194304 | tf_op jit(solution)/shard_map/all_to_all | solution.py:335
  917.6 77.4 %reduce-scatter.27.cloned.1.call-start = ((), (), s32[]{:S(2)}) async-start(), calls=%async_computation.27 | async-start | bytes 1474560 | tf_op jit(solution)/shard_map/reduce_scatter | solution.py:310
  944.2 132.0 %all-to-all-start.5 = ((bf16[8,128,1024]{2,1,0:T(8,128)(2,1)}), bf16[8,128,1024]{2,1,0:T(8,128)(2,1)}, u32[]{:S(2)}, u32[]{:S(2)}) async-start(bf16[8,128,1024]{2,1,0:T(8,128)(2,1)} %get-tuple-element.41), calls=%async_computation.5 | async-start | bytes 4194304 | tf_op jit(solution)/shard_map/all_to_all | solution.py:336
  948.6 112.3 %all-reduce.7.cloned.1.call-start = ((), (), s32[]{:S(2)}) async-start(), calls=%async_computation.31 | async-start | bytes 2949120 | tf_op jit(solution)/shard_map/psum | solution.py:318
  (72 other events, 444.0 us)
Sparse Core Ops, SparseCore 0:
  9.6 118.0 all-gather.5
  129.2 44.4 all-gather.7
  175.3 165.0 all-gather.11
  341.8 164.4 all-gather.13
  507.7 164.9 all-gather.9
  725.9 27.3 reduce-scatter.32
  779.5 27.7 reduce-scatter.30
  821.0 18.2 reduce-scatter.24
  841.7 17.7 reduce-scatter.22
  861.5 18.0 reduce-scatter.18
  882.0 17.7 reduce-scatter.20
  902.5 17.9 reduce-scatter.14
  922.8 17.7 reduce-scatter.28
  942.8 21.5 reduce-scatter.16
  966.6 28.4 reduce-scatter.26
  1000.6 60.2 all-reduce.6
where the time goes:
time: 1090 us
  waiting for transfers between devices  687 us (63%)
  matrix products  263 us (24%)
  other arithmetic  58.7 us (5%)
  local copies, waits for them, and re-layouts  35.3 us (3%)
  starting transfers between devices  27 us (2%)
  between operations  17.2 us (2%)
    all_gather x1, waiting for transfers between devices, local(): lax.all_gather(shards[3], 'group', axis=1, tiled=True)  157 us
    all_gather x1, waiting for transfers between devices, local(): lax.all_gather(shards[2], 'group', axis=1, tiled=True)  137 us
    all_gather x1, waiting for transfers between devices, local(): lax.all_gather(shards[4], 'group', axis=1, tiled=True)  137 us
    dot_general x15, matrix products, matrix_product(): return jnp.dot(left, right, preferred_element_type=jnp.float32)  125 us
    dot_general x15, matrix products, transposed_right_matmul(): lax.dot_general(left, right, (((1,), (1,)), ((), ())), preferred_element_...  105 us
    psum x1, waiting for transfers between devices, local(): lax.psum(owned[0].astype(jnp.bfloat16), 'dp').astype(jnp.float32)  65.8 us
    all_gather x1, waiting for transfers between devices, local(): lax.all_gather(shards[0], 'group', axis=1, tiled=True)  44.8 us
    dot_general x10, matrix products, transposed_left_matmul(): lax.dot_general(left, right, (((0,), (0,)), ((), ())), preferred_element_...  32.7 us
  transfers between devices with their start and end apart: 22, of which 12 were waited for; matrix products, arithmetic and copies ran while one was open for 26% of the time, Pallas kernels for 0%

commit v1 on v0

--- a/solution.py
+++ b/solution.py
@@ -29,7 +29,9 @@
 def per_token_tables(
     sequence_length_row, adapter_index_row, count_of_rows, adapter_column_span, adapter_rank_size
 ):
-    finish = jnp.cumsum(sequence_length_row)
+    count = sequence_length_row.shape[0]
+    earlier = jnp.arange(count)[:, None] <= jnp.arange(count)[None, :]
+    finish = jnp.sum(jnp.where(earlier, sequence_length_row[:, None], 0), axis=0)
     starts = finish - sequence_length_row
     counter = jnp.arange(count_of_rows, dtype=jnp.int32)
     member = ((counter[:, None] >= starts[None, :]) & (counter[:, None] < finish[None, :])).astype(
@@ -58,8 +60,41 @@
 
 
 def regroup(values, picks, pieces):
-    shaped = values.reshape(pieces, values.shape[0] // pieces, values.shape[1])
-    return jnp.take(shaped, picks, axis=0).reshape(values.shape)
+    size = values.shape[0] // pieces
+    return jnp.concatenate(
+        [lax.dynamic_slice_in_dim(values, picks[i] * size, size, 0) for i in range(pieces)], axis=0
+    )
+
+
+def gather_weight(shard):
+    size = shard.shape[0] // lax.axis_size("dp")
+    piece = lax.dynamic_slice_in_dim(shard, lax.axis_index("dp") * size, size, 0)
+    stacked = lax.all_gather(piece, ("group", "dp"))
+    return stacked.reshape(lax.axis_size("group"), shard.shape[0], shard.shape[1])
+
+
+def wide_product(rows, stacked):
+    out = jnp.einsum("rk,gkn->rgn", rows, stacked, preferred_element_type=jnp.float32)
+    return out.reshape(rows.shape[0], -1)
+
+
+def wide_product_back(grads, stacked):
+    shaped = grads.reshape(grads.shape[0], stacked.shape[0], stacked.shape[2])
+    return jnp.einsum("rgn,gkn->rk", shaped, stacked, preferred_element_type=jnp.float32)
+
+
+def reduce_grads(terms):
+    groups = lax.axis_size("group")
+    parts = [t.astype(jnp.bfloat16).reshape(groups, -1, t.shape[1]) for t in terms]
+    joined = jnp.concatenate(parts, axis=1)
+    flat = joined.reshape(-1, joined.shape[2])
+    mine = lax.psum_scatter(flat, ("group", "dp"), scatter_dimension=0, tiled=True)
+    share = lax.all_gather(mine, "dp", tiled=True)
+    out, at = [], 0
+    for p in parts:
+        out.append(share[at : at + p.shape[1]].astype(jnp.float32))
+        at += p.shape[1]
+    return out
 
 
 def inverse_root(values):
@@ -80,7 +115,7 @@
         matrix_product(input_rows, adapter_down_factor).astype(jnp.bfloat16) * select_adapter
     )
     return (
-        matrix_product(input_rows, frozen_weight)
+        wide_product(input_rows, frozen_weight)
         + adapter_scale * matrix_product(reduced_sum, adapter_up_factor),
         reduced_sum,
     )
@@ -96,14 +131,14 @@
     select_adapter,
 ):
     gradient_rank_space = incoming_gradient.astype(jnp.bfloat16)
-    gradient_up_factor = adapter_scale * transposed_left_matmul(reduced_sum, gradient_rank_space)
+    gradient_up_factor = adapter_scale * transposed_left_matmul(gradient_rank_space, reduced_sum)
     gradient_reduced_sum = (
         adapter_scale
         * transposed_right_matmul(gradient_rank_space, adapter_up_factor)
         * select_adapter
     ).astype(jnp.bfloat16)
     grad_down = transposed_left_matmul(input_rows, gradient_reduced_sum)
-    input_gradients = transposed_right_matmul(
+    input_gradients = wide_product_back(
         gradient_rank_space, frozen_weight
     ) + transposed_right_matmul(gradient_reduced_sum, adapter_down_factor)
     return (input_gradients, grad_down, gradient_up_factor)
@@ -143,11 +178,12 @@
     inverse_row = jnp.sum(
         jnp.where(order_row[None, :] == counting[:, None], counting[None, :], 0), axis=1
     )
-    arrived = lax.all_to_all(tokens, "dp", split_axis=0, concat_axis=0, tiled=True)
-    hidden_in = lax.all_to_all(
-        regroup(arrived, order_row, dp_count), "dp", split_axis=0, concat_axis=0, tiled=True
-    )
-    pack_source = order_row[dp_index]
+    arrived = lax.all_to_all(cotangent, "dp", split_axis=0, concat_axis=0, tiled=True)
+    cotangent = lax.all_to_all(
+        regroup(arrived, inverse_row, dp_count), "dp", split_axis=0, concat_axis=0, tiled=True
+    )
+    pack_source = dp_index
+    hidden_in = tokens
     sequence_length_row = lengths[:, 0, :][pack_source]
     adapter_index_row = adapter_ids[:, 0, :][pack_source]
     select_adapter, after_one, after_two = per_token_tables(
@@ -158,13 +194,7 @@
         ADAPTER_RANK,
     )
     shards = (in_weight, out_weight, gate_weight, up_weight, down_weight)
-    full_in, full_out, full_gate, full_up, full_down = (
-        lax.all_gather(shards[0], "group", axis=1, tiled=True),
-        lax.all_gather(shards[1], "group", axis=1, tiled=True),
-        lax.all_gather(shards[2], "group", axis=1, tiled=True),
-        lax.all_gather(shards[3], "group", axis=1, tiled=True),
-        lax.all_gather(shards[4], "group", axis=1, tiled=True),
-    )
+    full_in, full_out, full_gate, full_up, full_down = [gather_weight(w) for w in shards]
     hidden32 = hidden_in.astype(jnp.float32)
     inverse_one = inverse_root(hidden32)
     normed = (hidden32 * inverse_one * norm_gain).astype(jnp.bfloat16)
@@ -199,13 +229,7 @@
         activated, full_down, down_first_factor, down_second_factor, select_adapter
     )
     result = (middle + ffn_out).astype(jnp.bfloat16)
-    back_in, back_out, back_gate, back_up, back_down = (
-        lax.all_gather(shards[0], "group", axis=1, tiled=True),
-        lax.all_gather(shards[1], "group", axis=1, tiled=True),
-        lax.all_gather(shards[2], "group", axis=1, tiled=True),
-        lax.all_gather(shards[3], "group", axis=1, tiled=True),
-        lax.all_gather(shards[4], "group", axis=1, tiled=True),
-    )
+    back_in, back_out, back_gate, back_up, back_down = full_in, full_out, full_gate, full_up, full_down
     upstream32 = cotangent.astype(jnp.float32)
     grad_act, down_a_grad, down_b_grad = adapter_project_backward(
         upstream32,
@@ -270,70 +294,13 @@
     grad_input = (grad_middle + norm_back(hidden32, inverse_one, norm_gain, grad_normed)).astype(
         jnp.bfloat16
     )
-    grad_terms = (
-        in_a_grad,
-        in_b_grad,
-        out_a_grad,
-        out_b_grad,
-        gate_a_grad,
-        gate_b_grad,
-        up_a_grad,
-        up_b_grad,
-        down_a_grad,
-        down_b_grad,
-    )
-    owned = (
-        lax.psum_scatter(
-            grad_terms[0].astype(jnp.bfloat16), "group", scatter_dimension=0, tiled=True
-        ).astype(jnp.float32),
-        lax.psum_scatter(
-            grad_terms[1].astype(jnp.bfloat16), "group", scatter_dimension=1, tiled=True
-        ).astype(jnp.float32),
-        lax.psum_scatter(
-            grad_terms[2].astype(jnp.bfloat16), "group", scatter_dimension=0, tiled=True
-        ).astype(jnp.float32),
-        lax.psum_scatter(
-            grad_terms[3].astype(jnp.bfloat16), "group", scatter_dimension=1, tiled=True
-        ).astype(jnp.float32),
-        lax.psum_scatter(
-            grad_terms[4].astype(jnp.bfloat16), "group", scatter_dimension=0, tiled=True
-        ).astype(jnp.float32),
-        lax.psum_scatter(
-            grad_terms[5].astype(jnp.bfloat16), "group", scatter_dimension=1, tiled=True
-        ).astype(jnp.float32),
-        lax.psum_scatter(
-            grad_terms[6].astype(jnp.bfloat16), "group", scatter_dimension=0, tiled=True
-        ).astype(jnp.float32),
-        lax.psum_scatter(
-            grad_terms[7].astype(jnp.bfloat16), "group", scatter_dimension=1, tiled=True
-        ).astype(jnp.float32),
-        lax.psum_scatter(
-            grad_terms[8].astype(jnp.bfloat16), "group", scatter_dimension=0, tiled=True
-        ).astype(jnp.float32),
-        lax.psum_scatter(
-            grad_terms[9].astype(jnp.bfloat16), "group", scatter_dimension=1, tiled=True
-        ).astype(jnp.float32),
-    )
+    early = reduce_grads(
+        [down_a_grad, down_b_grad, gate_a_grad, gate_b_grad, up_a_grad, up_b_grad, out_a_grad, out_b_grad]
+    )
+    late = reduce_grads([in_a_grad, in_b_grad])
     totals = (
-        lax.psum(owned[0].astype(jnp.bfloat16), "dp").astype(jnp.float32),
-        lax.psum(owned[1].astype(jnp.bfloat16), "dp").astype(jnp.float32),
-        lax.psum(owned[2].astype(jnp.bfloat16), "dp").astype(jnp.float32),
-        lax.psum(owned[3].astype(jnp.bfloat16), "dp").astype(jnp.float32),
-        lax.psum(owned[4].astype(jnp.bfloat16), "dp").astype(jnp.float32),
-        lax.psum(owned[5].astype(jnp.bfloat16), "dp").astype(jnp.float32),
-        lax.psum(owned[6].astype(jnp.bfloat16), "dp").astype(jnp.float32),
-        lax.psum(owned[7].astype(jnp.bfloat16), "dp").astype(jnp.float32),
-        lax.psum(owned[8].astype(jnp.bfloat16), "dp").astype(jnp.float32),
-        lax.psum(owned[9].astype(jnp.bfloat16), "dp").astype(jnp.float32),
-    )
-    going = (
-        lax.all_to_all(result, "dp", split_axis=0, concat_axis=0, tiled=True),
-        lax.all_to_all(grad_input, "dp", split_axis=0, concat_axis=0, tiled=True),
-    )
-    going = (regroup(going[0], inverse_row, dp_count), regroup(going[1], inverse_row, dp_count))
-    result, grad_input = (
-        lax.all_to_all(going[0], "dp", split_axis=0, concat_axis=0, tiled=True),
-        lax.all_to_all(going[1], "dp", split_axis=0, concat_axis=0, tiled=True),
+        late[0], late[1].T, early[6], early[7].T, early[2], early[3].T, early[4], early[5].T,
+        early[0], early[1].T,
     )
     return (
         result,

time: 1090 us -> 885 us (0.81)
  waiting for transfers between devices: 687 us -> 456 us
  local copies, waits for them, and re-layouts: 35.3 us -> 109 us
  matrix products: 263 us -> 237 us
  other arithmetic: 58.7 us -> 32.9 us
  starting transfers between devices: 27 us -> 9.12 us
    all_gather x5 -> x6, waiting for transfers between devices: 498 us -> 226 us  [the longest x5 214 us: gather_weight(): stacked = lax.all_gather(piece, ('group', 'dp'))]
    dot_general x0 -> x10, matrix products: none -> 125 us  [the longest x5 72.1 us: wide_product_back(): jnp.einsum('rgn,gkn->rk', shaped, stacked, preferred_element_type=jnp.flo...]
    unnamed x18 -> x9, waiting for transfers between devices: 3.32 us -> 112 us
    dot_general x15 -> x10, matrix products: 105 us -> 27.9 us  [transposed_right_matmul(): lax.dot_general(left, right, (((1,), (1,)), ((), ())), preferred_element_...]
    psum x1 -> x0, waiting for transfers between devices: 65.8 us -> none  [local(): lax.psum(owned[0].astype(jnp.bfloat16), 'dp').astype(jnp.float32)]
    dot_general x15 -> x10, matrix products: 125 us -> 61.3 us  [matrix_product(): return jnp.dot(left, right, preferred_element_type=jnp.float32)]
    dot_general x0 -> x5, local copies, waits for them, and re-layouts: none -> 51 us  [wide_product(): jnp.einsum('rk,gkn->rgn', rows, stacked, preferred_element_type=jnp.float32)]
    all_to_all x6 -> x2, waiting for transfers between devices: 76.5 us -> 43.4 us  [the longest x1 23 us: local(): lax.all_to_all(cotangent, 'dp', split_axis=0, concat_axis=0, tiled=True)]
  transfers between devices with their start and end apart: 22 -> 10, of which waited for: 12 -> 9; matrix products, arithmetic and copies ran while one was open for 26% -> 23% of each run, Pallas kernels for 0% -> 0%
where the time goes in v1:
time: 885 us; the launch traced here: 873 us
  waiting for transfers between devices  456 us (52%)
  matrix products  237 us (27%)
  local copies, waits for them, and re-layouts  109 us (12%)
  other arithmetic  32.9 us (4%)
  between operations  20.8 us (2%)
  starting transfers between devices  9.12 us (1%)
    all_gather x5, waiting for transfers between devices, gather_weight(): stacked = lax.all_gather(piece, ('group', 'dp'))  214 us
    unnamed x9, waiting for transfers between devices  112 us
    reduce_scatter x1, waiting for transfers between devices, reduce_grads(): lax.psum_scatter(flat, ('group', 'dp'), scatter_dimension=0, tiled=True)  75.1 us
    dot_general x5, matrix products, wide_product_back(): jnp.einsum('rgn,gkn->rk', shaped, stacked, preferred_element_type=jnp.flo...  72.1 us
    dot_general x10, matrix products, matrix_product(): return jnp.dot(left, right, preferred_element_type=jnp.float32)  61.3 us
    dot_general x5, matrix products, wide_product(): jnp.einsum('rk,gkn->rgn', rows, stacked, preferred_element_type=jnp.float32)  53.4 us
    dot_general x5, local copies, waits for them, and re-layouts, wide_product(): jnp.einsum('rk,gkn->rgn', rows, stacked, preferred_element_type=jnp.float32)  51 us
    unnamed x201, local copies, waits for them, and re-layouts  38.3 us
  transfers between devices with their start and end apart: 10, of which 9 were waited for; matrix products, arithmetic and copies ran while one was open for 23% of the time, Pallas kernels for 0%

profile of v1, /device:TPU:0, one launch (start us, length us, event | category | flops | bytes accessed | tf_op | source)
XLA Modules:
  0.0 873.4 jit_solution(10565206722525793448)
XLA Ops:
  15.0 5.2 all-to-all-start
  26.1 23.0 %all-to-all-done = bf16[8,128,1024]{2,1,0:T(8,128)(2,1)S(1)} async-done(((bf16[8,128,1024]{2,1,0:T(8,128)(2,1)}), bf16[8,128,1024]{2,1,0:T(8,128)(2,1)S(1)}, u32[]{:S(2)}, u32[]{:S(2)}) %all-to-all-start) | async-done | bytes 2097184 | tf_op jit(solution)/shard_map/all_to_all | solution.py:181
  68.2 20.4 %all-to-all-done.1 = bf16[8,128,1024]{1,2,0:T(8,128)(2,1)S(1)} async-done(((bf16[8,128,1024]{1,2,0:T(8,128)(2,1)}), bf16[8,128,1024]{1,2,0:T(8,128)(2,1)S(1)}, u32[]{:S(2)}, u32[]{:S(2)}) %all-to-all-start.1) | async-done | bytes 2097184 | tf_op jit(solution)/shard_map/all_to_all | solution.py:182
  100.2 53.9 %all-gather.14.cloned.1.call-done = bf16[4096,768]{1,0:T(8,128)(2,1)} async-done(((bf16[128,768]{1,0:T(8,128)(2,1)}), bf16[4096,768]{1,0:T(8,128)(2,1)}) %all-gather.14.cloned.1.call-update) | async-done | bytes 6291472 | tf_op jit(solution)/shard_map/all_gather | solution.py:72
  154.1 8.8 %copy.149 = bf16[4,768,1024]{2,1,0:T(8,128)(2,1)} copy(bf16[4,768,1024]{1,2,0:T(8,128)(2,1)} %bitcast.233) | data formatting | bytes 12582912 | tf_op jit(solution)/shard_map/rk,gkn->rgn/dot_general | solution.py:77
  162.9 9.6 %fusion.63 = f32[1024,3072]{1,0:T(8,128)S(1)} fusion(bf16[3072,1024]{1,0:T(8,128)(2,1)} %bitcast.236, bf16[1024,1024]{0,1:T(8,128)(2,1)S(1)} %copy-done.7, f32[1024]{0:T(1024)S(1)} %copy-done.68, f32[1024]{0:T(1024)S(1)} %get-tuple-element.95), kind=kOutput, calls=%fused_computation.159 | convolution fusion | flops 6446645248 | bytes 20979712 | tf_op jit(solution)/shard_map/rk,gkn->rgn/dot_general | solution.py:77
  179.5 4.6 multiply_convert_fusion.7
  191.2 47.0 %all-gather.20.cloned.1.call-done = bf16[4096,1152]{1,0:T(8,128)(2,1)} async-done(((bf16[128,1152]{1,0:T(8,128)(2,1)}), bf16[4096,1152]{1,0:T(8,128)(2,1)}) %all-gather.20.cloned.1.call-update) | async-done | bytes 9437200 | tf_op jit(solution)/shard_map/all_gather | solution.py:72
  238.2 12.7 %copy.152 = bf16[4,1152,1024]{2,1,0:T(8,128)(2,1)} copy(bf16[4,1152,1024]{1,2,0:T(8,128)(2,1)} %bitcast.211) | data formatting | bytes 18874368 | tf_op jit(solution)/shard_map/rk,gkn->rgn/dot_general | solution.py:77
  250.8 71.3 %all-gather.18.cloned.1.call-done = bf16[4096,1152]{1,0:T(8,128)(2,1)} async-done(((bf16[128,1152]{1,0:T(8,128)(2,1)}), bf16[4096,1152]{1,0:T(8,128)(2,1)}) %all-gather.18.cloned.1.call-update) | async-done | bytes 9437200 | tf_op jit(solution)/shard_map/all_gather | solution.py:72
  322.2 12.7 %copy.151 = bf16[4,1152,1024]{2,1,0:T(8,128)(2,1)} copy(bf16[4,1152,1024]{1,2,0:T(8,128)(2,1)} %bitcast.215) | data formatting | bytes 18874368 | tf_op jit(solution)/shard_map/rk,gkn->rgn/dot_general | solution.py:77
  334.9 16.5 %fusion.69 = f32[1024,4608]{1,0:T(8,128)} fusion(bf16[1024,1024]{0,1:T(8,128)(2,1)S(1)} %multiply_convert_fusion.6, bf16[4608,1024]{1,0:T(8,128)(2,1)} %bitcast.220), kind=kOutput, calls=%fused_computation.164 | convolution fusion | flops 9663676416 | bytes 30408704 | tf_op jit(solution)/shard_map/rk,gkn->rgn/dot_general | solution.py:77
  351.4 13.2 %fusion.68 = f32[1024,4608]{1,0:T(8,128)} fusion(bf16[1024,1024]{0,1:T(8,128)(2,1)S(1)} %multiply_convert_fusion.6, bf16[4608,1024]{1,0:T(8,128)(2,1)S(1)} %bitcast.221), kind=kOutput, calls=%fused_computation.163 | convolution fusion | flops 9663676416 | bytes 30408704 | tf_op jit(solution)/shard_map/rk,gkn->rgn/dot_general | solution.py:77
  364.5 41.6 %all-gather.22.cloned.1.call-done = bf16[18432,256]{1,0:T(8,128)(2,1)} async-done(((bf16[576,256]{1,0:T(8,128)(2,1)}), bf16[18432,256]{1,0:T(8,128)(2,1)}) %all-gather.22.cloned.1.call-update) | async-done | bytes 9437200 | tf_op jit(solution)/shard_map/all_gather | solution.py:72
  406.2 17.3 %fusion.71 = f32[1024,4608,1]{1,0,2:T(8,128)} fusion(bf16[1024,4,256]{0,2,1:T(8,128)(2,1)} %reshape.212, bf16[4,4608,256]{2,1,0:T(8,128)(2,1)} %bitcast.209), kind=kOutput, calls=%fused_computation.166 | convolution fusion | flops 9663676416 | bytes 30408704 | tf_op jit(solution)/shard_map/rgn,gkn->rk/dot_general | solution.py:83
  423.4 12.2 %multiply_add_fusion = f32[1024,4608]{1,0:T(8,128)} fusion(f32[1024,4608]{1,0:T(8,128)} %fusion.69, bf16[1024,128]{1,0:T(8,128)(2,1)S(1)} %compare_select_fusion.1, bf16[128,4608]{1,0:T(8,128)(2,1)S(1)} %copy-done.24), kind=kOutput, calls=%fused_computation.4 | convolution fusion | flops 1217396736 | bytes 39190528 | tf_op jit(solution)/shard_map/dot_general | solution.py:14
  435.6 12.3 %bitcast_add_fusion = f32[1024,4608]{1,0:T(8,128)} fusion(f32[1024,4608,1]{1,0,2:T(8,128)} %fusion.71, bf16[1024,128]{1,0:T(8,128)(2,1)S(1)} %fusion.48, bf16[4608,128]{1,0:T(8,128)(2,1)S(1)} %copy-done.23), kind=kOutput, calls=%fused_computation | convolution fusion | flops 1212678144 | bytes 39190528 | tf_op jit(solution)/shard_map/dot_general | solution.py:24
  447.9 28.6 %multiply_convert_fusion.1 = (bf16[1024,4608]{1,0:T(8,128)(2,1)}, bf16[1024,4608]{1,0:T(8,128)(2,1)}, bf16[1024,4608]{1,0:T(8,128)(2,1)}) fusion(f32[1024,4608]{1,0:T(8,128)} %bitcast_add_fusion, f32[1024,4608]{1,0:T(8,128)} %multiply_add_fusion, f32[1024,4608]{1,0:T(8,128)} %fusion.68, bf16[1024,128]{1,0:T(8,128)(2,1)S(1)} %compare_select_fusion.2, ...), kind=kOutput, calls=%fused_computation.2 | convolution fusion | flops 1292894208 | bytes 86376448 | tf_op jit(solution)/shard_map/dot_general | solution.py:14
  476.5 7.1 compare_select_fusion
  483.6 7.6 convolution_convert_fusion
  512.5 14.0 %fusion = f32[1024,1024,1]{0,1,2:T(8,128)} fusion(bf16[4,1024,1152]{2,1,0:T(8,128)(2,1)S(1)} %bitcast.214, bf16[128,4,8,1152]{3,2,1,0:T(8,128)(2,1)} %bitcast.261), kind=kOutput, calls=%fused_computation.8 | convolution fusion | flops 9663676416 | bytes 23068672 | tf_op jit(solution)/shard_map/rgn,gkn->rk/dot_general | solution.py:83
  526.5 20.9 %multiply_reduce_fusion = (f32[1024]{0:T(1024)S(1)}, f32[1024,1024]{0,1:T(8,128)}) fusion(f32[1024,1024]{0,1:T(8,128)S(1)} %copy-done.4, f32[1024,1024]{0,1:T(8,128)} %fusion.73, f32[1024,1024,1]{0,1,2:T(8,128)} %fusion, f32[1024,1024]{0,1:T(8,128)} %fusion.72, bf16[4,1024,1152]{2,1,0:T(8,128)(2,1)} %bitcast.216, bf16[128,4,8,1152]{3,2,1,0:T(8,128)(2,1)} %bitcast.258, ...), kind=kOutput, calls=%fused_computation.50 | convolution fusion | flops 9669966848 | bytes 39854080 | tf_op jit(solution)/shard_map/rgn,gkn->rk/dot_general | solution.py:83
  562.3 12.9 %copy.153 = bf16[4,256,4608]{2,1,0:T(8,128)(2,1)} copy(bf16[4,256,4608]{1,2,0:T(8,128)(2,1)} %bitcast.210) | data formatting | bytes 18874368 | tf_op jit(solution)/shard_map/rk,gkn->rgn/dot_general | solution.py:77
  577.4 7.6 multiply_convert_fusion.4
  602.8 11.8 %fusion.70 = f32[1024,1024]{0,1:T(8,128)} fusion(bf16[1024,4608]{1,0:T(8,128)(2,1)S(1)} %bitcast.265, bf16[1024,4608]{1,0:T(8,128)(2,1)S(1)} %bitcast.219), kind=kOutput, calls=%fused_computation.165 | convolution fusion | flops 9663676416 | bytes 23068672 | tf_op jit(solution)/shard_map/rk,gkn->rgn/dot_general | solution.py:77
  616.2 12.3 %fusion.18 = (f32[1024]{0:T(1024)S(1)}, f32[1024,1024]{0,1:T(8,128)}) fusion(bf16[1024,1024]{0,1:T(8,128)(2,1)S(1)} %copy-done.9, f32[1024,1024]{0,1:T(8,128)S(1)} %fusion.75, bf16[4,1024,768]{2,1,0:T(8,128)(2,1)} %bitcast.234, bf16[128,4,8,768]{3,2,1,0:T(8,128)(2,1)} %bitcast.235, f32[1024]{0:T(1024)S(1)} %copy-done.69), kind=kOutput, calls=%fused_computation.35 | convolution fusion | flops 6447692800 | bytes 23076864 | tf_op jit(solution)/shard_map/rgn,gkn->rk/dot_general | solution.py:83
  628.5 75.1 %reduce-scatter.9.cloned.1.call-done = bf16[592,128]{1,0:T(8,128)(2,1)} async-done(((bf16[18944,128]{1,0:T(8,128)(2,1)}), bf16[592,128]{1,0:T(8,128)(2,1)}) %reduce-scatter.9.cloned.1.call-update) | async-done | bytes 151568 | tf_op jit(solution)/shard_map/reduce_scatter | solution.py:91
  703.6 5.5 add_convert_fusion
  713.1 7.6 fusion.17
  724.8 111.7 %reduce-scatter.7.cloned.1.call-done = bf16[128,128]{1,0:T(8,128)(2,1)} async-done(((bf16[4096,128]{1,0:T(8,128)(2,1)}), bf16[128,128]{1,0:T(8,128)(2,1)}) %reduce-scatter.7.cloned.1.call-update) | async-done | bytes 32784
  837.4 8.1 all_gather.46
  847.0 11.7 %all-gather.12.cloned.1.call-done = bf16[4736,128]{1,0:T(8,128)(2,1)} async-done(((bf16[592,128]{1,0:T(8,128)(2,1)}), bf16[4736,128]{1,0:T(8,128)(2,1)}) %all-gather.12.cloned.1.call-update) | async-done | bytes 1212432 | tf_op jit(solution)/shard_map/all_gather | solution.py:92
  (290 shorter events, 128.0 us)
Async XLA Ops:
  7.2 13.0 %copy-start.70 = (s32[1,8]{1,0:T(1,128)S(1)}, s32[1,8]{1,0:T(1,128)}, u32[]{:S(2)}) copy-start(s32[1,8]{1,0:T(1,128)} %param.25) | copy-start | bytes 100
  7.2 89.0 %all-gather.16.cloned.1.call-start = ((), (), s32[]{:S(2)}) async-start(), calls=%async_computation.6 | async-start | bytes 2162688 | tf_op jit(solution)/shard_map/all_gather | solution.py:72
  8.9 145.2 %all-gather.14.cloned.1.call-start = ((), (), s32[]{:S(2)}) async-start(), calls=%async_computation.5 | async-start | bytes 6488064 | tf_op jit(solution)/shard_map/all_gather | solution.py:72
  10.6 227.6 %all-gather.20.cloned.1.call-start = ((), (), s32[]{:S(2)}) async-start(), calls=%async_computation.8 | async-start | bytes 9732096 | tf_op jit(solution)/shard_map/all_gather | solution.py:72
  11.4 310.7 %all-gather.18.cloned.1.call-start = ((), (), s32[]{:S(2)}) async-start(), calls=%async_computation.7 | async-start | bytes 9732096 | tf_op jit(solution)/shard_map/all_gather | solution.py:72
  13.2 392.9 %all-gather.22.cloned.1.call-start = ((), (), s32[]{:S(2)}) async-start(), calls=%async_computation.9 | async-start | bytes 9732096 | tf_op jit(solution)/shard_map/all_gather | solution.py:72
  15.0 34.1 %all-to-all-start = ((bf16[8,128,1024]{2,1,0:T(8,128)(2,1)}), bf16[8,128,1024]{2,1,0:T(8,128)(2,1)S(1)}, u32[]{:S(2)}, u32[]{:S(2)}) async-start(bf16[8,128,1024]{2,1,0:T(8,128)(2,1)} %bitcast.239), calls=%async_computation | async-start | bytes 4194304 | tf_op jit(solution)/shard_map/all_to_all | solution.py:181
  54.6 33.9 %all-to-all-start.1 = ((bf16[8,128,1024]{1,2,0:T(8,128)(2,1)}), bf16[8,128,1024]{1,2,0:T(8,128)(2,1)S(1)}, u32[]{:S(2)}, u32[]{:S(2)}) async-start(bf16[8,128,1024]{1,2,0:T(8,128)(2,1)} %copy.156), calls=%async_computation.1 | async-start | bytes 4194304 | tf_op jit(solution)/shard_map/all_to_all | solution.py:182
  58.3 645.3 %reduce-scatter.9.cloned.1.call-start = ((), (), s32[]{:S(2)}) async-start(), calls=%async_computation.11 | async-start | bytes 5001216 | tf_op jit(solution)/shard_map/reduce_scatter | solution.py:91
  62.7 113.0 %copy-start.55 = (f32[1024]{0:T(1024)}, f32[1024]{0:T(1024)S(1)}, u32[]{:S(2)}) copy-start(f32[1024]{0:T(1024)S(1)} %get-tuple-element.99) | copy-start | bytes 12292
  62.7 113.0 %copy-start.57 = (f32[1024]{0:T(1024)}, f32[1024]{0:T(1024)S(1)}, u32[]{:S(2)}) copy-start(f32[1024]{0:T(1024)S(1)} %get-tuple-element.98) | copy-start | bytes 12292
  65.4 97.5 %copy-start.60 = (f32[1024]{0:T(1024)}, f32[1024]{0:T(1024)S(1)}, u32[]{:S(2)}) copy-start(f32[1024]{0:T(1024)S(1)} %get-tuple-element.95) | copy-start | bytes 12292
  65.4 110.3 %copy-start.49 = (f32[1,1024]{1,0:T(1,128)}, f32[1,1024]{1,0:T(1,128)S(1)}, u32[]{:S(2)}) copy-start(f32[1,1024]{1,0:T(1,128)S(1)} %get-tuple-element.91) | copy-start | bytes 12292
  65.5 110.3 %copy-start.51 = (f32[1,1024]{1,0:T(1,128)}, f32[1,1024]{1,0:T(1,128)S(1)}, u32[]{:S(2)}) copy-start(f32[1,1024]{1,0:T(1,128)S(1)} %get-tuple-element.92) | copy-start | bytes 12292
  65.5 110.3 %copy-start.53 = (f32[1,1024]{1,0:T(1,128)}, f32[1,1024]{1,0:T(1,128)S(1)}, u32[]{:S(2)}) copy-start(f32[1,1024]{1,0:T(1,128)S(1)} %get-tuple-element.93) | copy-start | bytes 12292
  68.1 104.4 %copy-start.27 = (bf16[1024,128]{1,0:T(8,128)(2,1)}, bf16[1024,128]{1,0:T(8,128)(2,1)S(1)}, u32[]{:S(2)}) copy-start(bf16[1024,128]{1,0:T(8,128)(2,1)S(1)} %compare_select_fusion.4) | copy-start | bytes 786436
  68.1 27.3 %copy-start.41 = (bf16[128,1024]{1,0:T(8,128)(2,1)S(1)}, bf16[128,1024]{1,0:T(8,128)(2,1)}, u32[]{:S(2)}) copy-start(bf16[128,1024]{1,0:T(8,128)(2,1)} %param.45) | copy-start | bytes 786436
  334.9 16.5 %copy-start.13 = (bf16[4,1152,1024]{2,1,0:T(8,128)(2,1)S(1)}, bf16[4,1152,1024]{2,1,0:T(8,128)(2,1)}, u32[]{:S(2)}) copy-start(bf16[4,1152,1024]{2,1,0:T(8,128)(2,1)} %copy.151) | copy-start | bytes 28311556
  406.2 17.3 %copy-start.24 = (bf16[128,4608]{1,0:T(8,128)(2,1)S(1)}, bf16[128,4608]{1,0:T(8,128)(2,1)}, u32[]{:S(2)}) copy-start(bf16[128,4608]{1,0:T(8,128)(2,1)} %param.43) | copy-start | bytes 3538948
  435.6 12.3 %copy-start.67 = (bf16[128,4608]{1,0:T(8,128)(2,1)S(1)}, bf16[128,4608]{1,0:T(8,128)(2,1)}, u32[]{:S(2)}) copy-start(bf16[128,4608]{1,0:T(8,128)(2,1)} %param.41) | copy-start | bytes 3538948
  476.5 14.7 %slice-start.12 = ((s8[9437184]{0:T(1024)(128)(4,1)}), s8[4194304]{0:T(1024)(128)(4,1)S(1)}, s32[]{:S(2)}) async-start(s8[9437184]{0:T(1024)(128)(4,1)} %bitcast.262), calls=%async_computation.24 | async-start | bytes 8388608
  476.5 14.7 %slice-start.13 = ((s8[9437184]{0:T(1024)(128)(4,1)}), s8[4194304]{0:T(1024)(128)(4,1)S(1)}, s32[]{:S(2)}) async-start(s8[9437184]{0:T(1024)(128)(4,1)} %bitcast.262), calls=%async_computation.25 | async-start | bytes 8388608
  512.5 14.0 %copy-start.4 = (f32[1024,1024]{0,1:T(8,128)S(1)}, f32[1024,1024]{0,1:T(8,128)}, u32[]{:S(2)}) copy-start(f32[1024,1024]{0,1:T(8,128)} %copy-done.3) | copy-start | bytes 12582916
  512.5 14.0 %copy-start.64 = (f32[1024]{0:T(1024)S(1)}, f32[1024]{0:T(1024)}, u32[]{:S(2)}) copy-start(f32[1024]{0:T(1024)} %param.29) | copy-start | bytes 12292
  526.5 21.0 %copy-start.6 = (bf16[8,128,1024]{1,2,0:T(8,128)(2,1)S(1)}, bf16[8,128,1024]{1,2,0:T(8,128)(2,1)}, u32[]{:S(2)}) copy-start(bf16[8,128,1024]{1,2,0:T(8,128)(2,1)} %copy-done.5) | copy-start | bytes 6291460
  526.5 21.0 %copy-start.47 = (f32[1024]{0:T(1024)S(1)}, f32[1024]{0:T(1024)}, u32[]{:S(2)}) copy-start(f32[1024]{0:T(1024)} %copy-done.46) | copy-start | bytes 12292
  526.5 21.0 %copy-start.48 = (f32[1024]{0:T(1024)S(1)}, f32[1024]{0:T(1024)}, u32[]{:S(2)}) copy-start(f32[1024]{0:T(1024)} %get-tuple-element.96) | copy-start | bytes 12292
  562.1 274.5 %reduce-scatter.7.cloned.1.call-start = ((), (), s32[]{:S(2)}) async-start(), calls=%async_computation.10 | async-start | bytes 1081344
  562.3 12.9 %copy-start.38 = (bf16[1024,128]{1,0:T(8,128)(2,1)S(1)}, bf16[1024,128]{1,0:T(8,128)(2,1)}, u32[]{:S(2)}) copy-start(bf16[1024,128]{1,0:T(8,128)(2,1)} %param.38) | copy-start | bytes 786436
  614.6 244.2 %all-gather.12.cloned.1.call-start = ((), (), s32[]{:S(2)}) async-start(), calls=%async_computation.4 | async-start | bytes 1363968 | tf_op jit(solution)/shard_map/all_gather | solution.py:92
  616.2 87.4 %copy-start.42 = (bf16[128,1024]{1,0:T(8,128)(2,1)S(1)}, bf16[128,1024]{1,0:T(8,128)(2,1)}, u32[]{:S(2)}) copy-start(bf16[128,1024]{1,0:T(8,128)(2,1)} %param.45) | copy-start | bytes 786436
  720.7 145.4 %copy-start.1 = (bf16[1024,1152]{1,0:T(8,128)(2,1)S(1)}, bf16[1024,1152]{1,0:T(8,128)(2,1)}, u32[]{:S(2)}) copy-start(bf16[1024,1152]{1,0:T(8,128)(2,1)} %param.34) | copy-start | bytes 7077892
  (67 other events, 320.9 us)
Sparse Core Ops, SparseCore 0:
  11.5 66.4 all-gather.15
  80.9 73.2 all-gather.13
  157.6 80.5 all-gather.19
  241.5 80.6 all-gather.17
  325.5 80.6 all-gather.21
  562.2 141.3 reduce-scatter.8
  705.8 130.6 reduce-scatter.6
  838.6 20.1 all-gather.11

commit v2 on v1

--- a/solution.py
+++ b/solution.py
@@ -1,6 +1,8 @@
 import jax
 import jax.numpy as jnp
 from jax import lax
+from jax.experimental import pallas as pl
+from jax.experimental.pallas import tpu as pltpu
 from jax.sharding import PartitionSpec as P
 
 ADAPTER_RANK = 16
@@ -318,6 +320,696 @@
     )
 
 
+f32 = jnp.float32
+bf16 = jnp.bfloat16
+VMEM_BYTES = 60 * 2**20
+PARTS = 3
+X_BIT, Y_BIT, CORE_BIT = 2, 4, 1
+
+
+def nn(a, b):
+    return lax.dot_general(a, b, (((1,), (0,)), ((), ())), preferred_element_type=f32)
+
+
+def nt(a, b):
+    return lax.dot_general(a, b, (((1,), (1,)), ((), ())), preferred_element_type=f32)
+
+
+def swap_dp(values, bit):
+    return lax.ppermute(values, "dp", [(i, i ^ bit) for i in range(lax.axis_size("dp"))])
+
+
+def stacked(parts):
+    size = parts[0].shape[0]
+
+    def kernel(*refs):
+        out_ref, sems = refs[-2], refs[-1]
+        copies = [
+            pltpu.make_async_copy(refs[k], out_ref.at[k * size : (k + 1) * size], sems.at[k])
+            for k in range(len(parts))
+        ]
+        for copy in copies:
+            copy.start()
+        for copy in copies:
+            copy.wait()
+
+    return pl.pallas_call(
+        kernel,
+        name="stacked",
+        out_shape=jax.ShapeDtypeStruct((len(parts) * size, parts[0].shape[1]), parts[0].dtype),
+        in_specs=[any_spec()] * len(parts),
+        out_specs=vmem_spec(),
+        scratch_shapes=[pltpu.SemaphoreType.DMA((len(parts),))],
+    )(*parts)
+
+
+def from_planes(piece):
+    groups = lax.axis_size("group")
+    return stacked(
+        [
+            lax.ppermute(piece, "group", [(i, (i + t) % groups) for i in range(groups)])
+            for t in range(1, groups)
+        ]
+    )
+
+
+def after(values, *others):
+    return lax.optimization_barrier((values, *others))[0]
+
+
+def piece_table():
+    masks = [0, X_BIT, Y_BIT, X_BIT | Y_BIT]
+    masks = masks + [m | CORE_BIT for m in masks]
+    return [(m, (1, 2, 3)) for m in masks]
+
+
+def any_spec():
+    return pl.BlockSpec(memory_space=pl.ANY)
+
+
+def vmem_spec():
+    return pl.BlockSpec(memory_space=pltpu.VMEM)
+
+
+def smem_spec():
+    return pl.BlockSpec(memory_space=pltpu.SMEM)
+
+
+def params():
+    return pltpu.CompilerParams(vmem_limit_bytes=VMEM_BYTES)
+
+
+def cost(flops):
+    return pl.CostEstimate(flops=int(flops) // 16, transcendentals=0, bytes_accessed=int(flops) // 16000)
+
+
+def sds(shape, dtype):
+    return jax.ShapeDtypeStruct(shape, dtype)
+
+
+BN = 256
+
+
+def col(i):
+    return pl.ds(pl.multiple_of(i * BN, BN), BN)
+
+
+ROWS = 128
+
+
+def row(i):
+    return pl.ds(pl.multiple_of(i * ROWS, ROWS), ROWS)
+
+
+def loop(n, body):
+    def step(i, carry):
+        body(i)
+        return carry
+
+    lax.fori_loop(0, n, step, 0)
+
+
+def front_call(ids, pieces, in_shard, out_shard, x, gain1, gain2, taps, sel2, m1, m2,
+               a_in, b_in, a_out, b_out, a_gu):
+    rows, d = x.shape
+    table = piece_table()
+    n_pieces = len(pieces)
+    h_in = in_shard.shape[1]
+    h_out = out_shard.shape[1]
+    pr = d // lax.axis_size("dp")
+    c = a_in.shape[1]
+
+    def kernel(*refs):
+        ids_ref = refs[0]
+        p_refs = refs[1 : 1 + n_pieces]
+        (in_ref, out_ref, x_ref, g1_ref, g2_ref, taps_ref, sel_ref, m1_ref, m2_ref, a_in_ref, b_in_ref,
+         a_out_ref, b_out_ref, a_gu_ref) = refs[1 + n_pieces : 15 + n_pieces]
+        (n1_ref, zin_ref, mix_ref, cv_ref, y_ref, zout_ref, h_ref, n2_ref, zgu_ref, w_in_hbm, w_out_hbm,
+         w_in, w_out, sem_in, sem_out, sem_store) = refs[15 + n_pieces :]
+        s = ids_ref[0]
+        z = ids_ref[1]
+
+        def put(buf, sem, src, r0, c0, width):
+            pltpu.make_async_copy(
+                src, buf.at[pl.ds(pl.multiple_of(r0, 128), src.shape[0]), pl.ds(pl.multiple_of(c0, 128), width)], sem
+            ).start()
+
+        put(w_in, sem_in, in_ref, 0, z * h_in, h_in)
+        for p_ref, (mask, steps) in zip(p_refs, table):
+            for k, t in enumerate(steps):
+                put(w_in, sem_in, p_ref.at[k * pr : (k + 1) * pr, :h_in], (s ^ mask) * pr, ((z - t) & 3) * h_in, h_in)
+        put(w_out, sem_out, out_ref, 0, z * h_out, h_out)
+        for p_ref, (mask, steps) in zip(p_refs, table):
+            for k, t in enumerate(steps):
+                put(w_out, sem_out, p_ref.at[k * pr : (k + 1) * pr, h_in:], (s ^ mask) * pr, ((z - t) & 3) * h_out, h_out)
+
+        g1 = g1_ref[...]
+
+        def norm1(i):
+            v = x_ref[row(i), :].astype(f32)
+            r = lax.rsqrt(jnp.mean(v * v, axis=-1, keepdims=True) + eps_norm)
+            n1_ref[row(i), :] = (v * r * g1).astype(bf16)
+
+        loop(rows // ROWS, norm1)
+        zin_ref[...] = nn(n1_ref[...], a_in_ref[...]).astype(bf16) * sel_ref[...]
+        pltpu.make_async_copy(w_in, w_in, sem_in).wait()
+        store_in = pltpu.make_async_copy(w_in, w_in_hbm, sem_store.at[0])
+        store_in.start()
+        m1 = m1_ref[...]
+        m2 = m2_ref[...]
+        blocks = d // BN
+
+        def mix(j):
+            def part(k):
+                cc = col(k * blocks + j)
+                return nn(n1_ref[...], w_in[:, cc]) + nn(zin_ref[...], b_in_ref[:, cc])
+
+            bg = part(0)
+            mix_ref[:, col(j)] = bg.astype(bf16)
+            xv = part(2)
+            mix_ref[:, col(2 * blocks + j)] = xv.astype(bf16)
+            bx = bg * xv
+            cv = (
+                taps_ref[2:3, col(j)] * bx
+                + taps_ref[1:2, col(j)] * pltpu.roll(bx, 1, 0) * m1
+                + taps_ref[0:1, col(j)] * pltpu.roll(bx, 2, 0) * m2
+            )
+            cv_ref[:, col(j)] = cv.astype(bf16)
+            cg = part(1)
+            mix_ref[:, col(blocks + j)] = cg.astype(bf16)
+            y_ref[:, col(j)] = (cg * cv).astype(bf16)
+
+        loop(blocks, mix)
+        zout_ref[...] = nn(y_ref[...], a_out_ref[...]).astype(bf16) * sel_ref[...]
+        pltpu.make_async_copy(w_out, w_out, sem_out).wait()
+        store_out = pltpu.make_async_copy(w_out, w_out_hbm, sem_store.at[1])
+        store_out.start()
+
+        def mid(j):
+            o = nn(y_ref[...], w_out[:, col(j)]) + nn(zout_ref[...], b_out_ref[:, col(j)])
+            h_ref[:, col(j)] = x_ref[:, col(j)].astype(f32) + o
+
+        loop(blocks, mid)
+        g2 = g2_ref[...]
+
+        def norm2(i):
+            v = h_ref[row(i), :]
+            r = lax.rsqrt(jnp.mean(v * v, axis=-1, keepdims=True) + eps_norm)
+            n2_ref[row(i), :] = (v * r * g2).astype(bf16)
+
+        loop(rows // ROWS, norm2)
+        sel = sel_ref[...]
+        zgu_ref[...] = nn(n2_ref[...], a_gu_ref[...]).astype(bf16) * jnp.concatenate([sel, sel], axis=1)
+        store_in.wait()
+        store_out.wait()
+
+    outs = [
+        sds((rows, d), bf16), sds((rows, c), bf16), sds((rows, 3 * d), bf16), sds((rows, d), bf16),
+        sds((rows, d), bf16), sds((rows, c), bf16), sds((rows, d), f32), sds((rows, d), bf16),
+        sds((rows, 2 * c), bf16), sds((d, 3 * d), bf16), sds((d, d), bf16),
+    ]
+    return pl.pallas_call(
+        kernel,
+        name="front",
+        out_shape=outs,
+        in_specs=[smem_spec()] + [any_spec()] * (n_pieces + 2) + [vmem_spec()] * 12,
+        out_specs=[vmem_spec()] * 9 + [any_spec()] * 2,
+        scratch_shapes=[
+            pltpu.VMEM((d, 3 * d), bf16), pltpu.VMEM((d, d), bf16),
+            pltpu.SemaphoreType.DMA, pltpu.SemaphoreType.DMA, pltpu.SemaphoreType.DMA((2,)),
+        ],
+        compiler_params=params(),
+        cost_estimate=cost(2.6 * rows * d * 4 * d),
+    )(ids, *pieces, in_shard, out_shard, x, gain1, gain2, taps, sel2, m1, m2, a_in, b_in, a_out, b_out, a_gu)
+
+
+def ffn_call(part, ids, pieces, gate_shard, up_shard, down_shard, n2, dy, zgu, dzd,
+             b_gate, b_up, a_down, acc, dn, dz_acc, zd_acc):
+    rows, d = n2.shape
+    table = piece_table()
+    n_pieces = len(pieces)
+    quarter = gate_shard.shape[1]
+    width = quarter // PARTS
+    fp = 4 * width
+    pr = d // lax.axis_size("dp")
+    dr = fp // lax.axis_size("dp")
+    c = zgu.shape[1] // 2
+    h_d = down_shard.shape[1]
+    first = acc is None
+    dps = lax.axis_size("dp")
+
+    def kernel(*refs):
+        ids_ref = refs[0]
+        p_refs = refs[1 : 1 + n_pieces]
+        rest = refs[1 + n_pieces :]
+        (gs_ref, us_ref, ds_ref, bg_hbm, bu_hbm, ad_hbm, acc_hbm, dn_hbm, n2_ref, dy_ref, zgu_ref, dzd_ref,
+         dz_in, zd_in) = rest[:14]
+        (acc_out, dn_out, dz_ref, zd_ref, grads_ref, wg, wu, wd, bg, bu, ad, acc_ref, dn_ref, act, dgb, dub,
+         g_tmp, u_tmp, da_tmp, g_all, sems) = rest[14:]
+        s = ids_ref[0]
+        z = ids_ref[1]
+        sem_g, sem_u, sem_d, sem_f, sem_a, sem_n, sem_o = [sems.at[i] for i in range(7)]
+
+        def put(buf, sem, src, r0, c0, ra=64):
+            dst = buf.at[pl.ds(pl.multiple_of(r0, ra), src.shape[0]), pl.ds(pl.multiple_of(c0, 128), src.shape[1])]
+            pltpu.make_async_copy(src, dst, sem).start()
+
+        def pieces_to(fn):
+            for p_ref, (mask, steps) in zip(p_refs, table):
+                for k, t in enumerate(steps):
+                    fn(p_ref, k * 3 * pr, s ^ mask, (z - t) & 3)
+
+        mine = pl.ds(part * width, width)
+        put(wg, sem_g, gs_ref.at[:, mine], 0, z * width)
+        pieces_to(lambda p, r, s_, z_: put(wg, sem_g, p.at[r : r + pr, :], s_ * pr, z_ * width))
+        for q in range(4):
+            at = pl.ds(q * quarter + part * width, width)
+            here = pl.ds(q * width, width)
+            pltpu.make_async_copy(bg_hbm.at[:, at], bg.at[:, here], sem_f).start()
+            pltpu.make_async_copy(bu_hbm.at[:, at], bu.at[:, here], sem_f).start()
+            pltpu.make_async_copy(ad_hbm.at[at, :], ad.at[here, :], sem_f).start()
+        put(wu, sem_u, us_ref.at[:, mine], 0, z * width)
+        pieces_to(lambda p, r, s_, z_: put(wu, sem_u, p.at[r + pr : r + 2 * pr, :], s_ * pr, z_ * width))
+        for q in range(4):
+            put(wd, sem_d, ds_ref.at[pl.ds(q * quarter + part * width, width), :], q * width, z * h_d)
+        half = dr - pr
+
+        def put_down(p, r, s_, z_):
+            put(wd, sem_d, p.at[r + 2 * pr : r + 3 * pr, :h_d], s_ * dr, z_ * h_d)
+            put(wd, sem_d, p.at[r + 2 * pr : r + 2 * pr + half, h_d:], s_ * dr + pr, z_ * h_d)
+            put(wd, sem_d, p.at[r + 2 * pr + half : r + 3 * pr, h_d:], s_ * dr + pr, z_ * h_d + width - h_d)
+
+        pieces_to(put_down)
+        load_acc = pltpu.make_async_copy(acc_hbm, acc_ref, sem_a)
+        load_acc.start()
+        if not first:
+            load_dn = pltpu.make_async_copy(dn_hbm, dn_ref, sem_n)
+            load_dn.start()
+
+        zg_t = zgu_ref[:, :c].T
+        zu_t = zgu_ref[:, c:].T
+        dzd_t = dzd_ref[...].T
+        for q in range(4):
+            at = pl.ds(q * quarter + part * width, width)
+            here = pl.ds(q * width, width)
+            pltpu.make_async_copy(bg_hbm.at[:, at], bg.at[:, here], sem_f).wait()
+            pltpu.make_async_copy(bu_hbm.at[:, at], bu.at[:, here], sem_f).wait()
+            pltpu.make_async_copy(ad_hbm.at[at, :], ad.at[here, :], sem_f).wait()
+        pltpu.make_async_copy(wg, wg, sem_g).wait()
+        pltpu.make_async_copy(wu, wu, sem_u).wait()
+        pltpu.make_async_copy(wd, wd, sem_d).wait()
+
+        def block(j):
+            cc = col(j)
+            g_tmp[...] = nn(n2_ref[...], wg[:, cc]) + nn(zgu_ref[:, :c], bg[:, cc])
+            u_tmp[...] = nn(n2_ref[...], wu[:, cc]) + nn(zgu_ref[:, c:], bu[:, cc])
+            da_tmp[...] = nt(dy_ref[...], wd[cc, :]) + nt(dzd_ref[...], ad[cc, :])
+
+            def point(i):
+                g = g_tmp[row(i), :]
+                u = u_tmp[row(i), :]
+                da = da_tmp[row(i), :]
+                sg = jax.nn.sigmoid(g)
+                gs = g * sg
+                act[row(i), cc] = (gs * u).astype(bf16)
+                dub[row(i), cc] = (da * gs).astype(bf16)
+                dgb[row(i), cc] = (da * u * (sg + gs * (1.0 - sg))).astype(bf16)
+
+            loop(rows // ROWS, point)
+            g_all[0, :, cc] = nn(zg_t, dgb[:, cc])
+            g_all[1, :, cc] = nn(zu_t, dub[:, cc])
+            g_all[2, :, cc] = nn(dzd_t, act[:, cc])
+
+        loop(fp // BN, block)
+        for k in range(3):
+            for q in range(4):
+                v = g_all[k, :, q * width : (q + 1) * width]
+                grads_ref[:, q, k] = v.reshape(dps, c // dps, width).astype(bf16)
+        dzg = nt(dgb[...], bg[...])
+        dzu = nt(dub[...], bu[...])
+        zd = nn(act[...], ad[...])
+        if first:
+            dz_ref[:, :c] = dzg
+            dz_ref[:, c:] = dzu
+            zd_ref[...] = zd
+        else:
+            dz_ref[:, :c] = dz_in[:, :c] + dzg
+            dz_ref[:, c:] = dz_in[:, c:] + dzu
+            zd_ref[...] = zd_in[...] + zd
+        load_acc.wait()
+
+        def out_block(j):
+            acc_ref[:, col(j)] += nn(act[...], wd[:, col(j)])
+
+        loop(d // BN, out_block)
+        store_acc = pltpu.make_async_copy(acc_ref, acc_out, sem_a)
+        store_acc.start()
+        if not first:
+            load_dn.wait()
+
+        def dn_block(j):
+            v = nt(dgb[...], wg[col(j), :]) + nt(dub[...], wu[col(j), :])
+            dn_ref[:, col(j)] = v if first else dn_ref[:, col(j)] + v
+
+        loop(d // BN, dn_block)
+        store_dn = pltpu.make_async_copy(dn_ref, dn_out, sem_n)
+        store_dn.start()
+        store_acc.wait()
+        store_dn.wait()
+
+    outs = [
+        sds((rows, d), f32), sds((rows, d), f32), sds((rows, 2 * c), f32), sds((rows, c), f32),
+        sds((dps, 4, 3, c // dps, width), bf16),
+    ]
+    if first:
+        acc, dn = dn, dn
+        dz_acc = jnp.zeros((8, 2 * c), f32)
+        zd_acc = jnp.zeros((8, c), f32)
+    return pl.pallas_call(
+        kernel,
+        name=f"ffn{part}",
+        out_shape=outs,
+        in_specs=[smem_spec()] + [any_spec()] * (n_pieces + 8) + [vmem_spec()] * 6,
+        out_specs=[any_spec()] * 2 + [vmem_spec()] * 3,
+        scratch_shapes=[
+            pltpu.VMEM((d, fp), bf16), pltpu.VMEM((d, fp), bf16), pltpu.VMEM((fp, d), bf16),
+            pltpu.VMEM((c, fp), bf16), pltpu.VMEM((c, fp), bf16), pltpu.VMEM((fp, c), bf16),
+            pltpu.VMEM((rows, d), f32), pltpu.VMEM((rows, d), f32),
+            pltpu.VMEM((rows, fp), bf16), pltpu.VMEM((rows, fp), bf16), pltpu.VMEM((rows, fp), bf16),
+            pltpu.VMEM((rows, BN), f32), pltpu.VMEM((rows, BN), f32), pltpu.VMEM((rows, BN), f32),
+            pltpu.VMEM((3, c, fp), f32),
+            pltpu.SemaphoreType.DMA((7,)),
+        ],
+        compiler_params=params(),
+        cost_estimate=cost(2.6 * rows * d * 6 * fp),
+    )(ids, *pieces, gate_shard, up_shard, down_shard, b_gate, b_up, a_down, acc, dn, n2, dy, zgu, dzd,
+      dz_acc, zd_acc)
+
+
+def norm_back_rows(v, gain, dn):
+    r = lax.rsqrt(jnp.mean(v * v, axis=-1, keepdims=True) + eps_norm)
+    scaled = gain * dn
+    return r * scaled - v * (r * r * r * jnp.mean(v * scaled, axis=-1, keepdims=True))
+
+
+def spread(ref, at, v):
+    dps, c = ref.shape[0], v.shape[0]
+    n = v.shape[1] // 4
+    for q in range(4):
+        ref[:, q, :, at : at + n] = v[:, q * n : (q + 1) * n].reshape(dps, c // dps, n).astype(bf16)
+
+
+def middle_call(acc, dn, dz_acc, zd_acc, h, n2, dy, y, zout, sel2, gain2, b_down, a_gu, b_out):
+    rows, d = h.shape
+    c = zout.shape[1]
+    blocks = d // BN
+    dps = lax.axis_size("dp")
+
+    def kernel(acc_ref, dn_ref, dz_in, zd_in, h_ref, n2_ref, dy_ref, y_ref, zout_ref, sel_ref, g2_ref,
+               b_down_ref, a_gu_ref, b_out_ref, res_ref, dh_ref, dhb, dzo, ga_ref, dzgu, zd):
+        sel = sel_ref[...]
+        sel_f = sel.astype(f32)
+        zd[...] = zd_in[...].astype(bf16) * sel
+        dzgu[:, :c] = (dz_in[:, :c] * sel_f).astype(bf16)
+        dzgu[:, c:] = (dz_in[:, c:] * sel_f).astype(bf16)
+
+        def results(j):
+            res_ref[:, col(j)] = (acc_ref[:, col(j)] + nn(zd[...], b_down_ref[:, col(j)])).astype(bf16)
+
+        loop(blocks, results)
+        spread(ga_ref, d // 4, nn(zd[...].T, dy_ref[...]))
+
+        def dns(j):
+            dh_ref[:, col(j)] = dn_ref[:, col(j)] + nt(dzgu[...], a_gu_ref[col(j), :])
+
+        loop(blocks, dns)
+        g = nn(dzgu[...].T, n2_ref[...])
+        spread(ga_ref, 2 * (d // 4), g[:c])
+        spread(ga_ref, 3 * (d // 4), g[c:])
+        g2 = g2_ref[...]
+
+        def norm2(i):
+            v = dy_ref[row(i), :].astype(f32) + norm_back_rows(h_ref[row(i), :], g2, dh_ref[row(i), :])
+            dh_ref[row(i), :] = v
+            dhb[row(i), :] = v.astype(bf16)
+
+        loop(rows // ROWS, norm2)
+        dzo[...] = (nt(dhb[...], b_out_ref[...]) * sel_f).astype(bf16)
+        spread(ga_ref, 0, nn(zout_ref[...].T, dhb[...]))
+        spread(ga_ref, 4 * (d // 4), nn(dzo[...].T, y_ref[...]))
+
+    return pl.pallas_call(
+        kernel,
+        name="middle",
+        out_shape=[
+            sds((rows, d), bf16), sds((rows, d), f32), sds((rows, d), bf16), sds((rows, c), bf16),
+            sds((dps, 4, c // dps, 5 * (d // 4)), bf16),
+        ],
+        in_specs=[vmem_spec()] * 14,
+        out_specs=[vmem_spec()] * 5,
+        scratch_shapes=[pltpu.VMEM((rows, 2 * c), bf16), pltpu.VMEM((rows, c), bf16)],
+        compiler_params=params(),
+        cost_estimate=cost(2 * rows * d * 4 * d),
+    )(acc, dn, dz_acc, zd_acc, h, n2, dy, y, zout, sel2, gain2, b_down, a_gu, b_out)
+
+
+def back_call(dhb, dzo, mix, cv, zin, n1, sel2, m1, m2, taps, a_out, b_in, w_out):
+    rows, d = dhb.shape
+    c = zin.shape[1]
+    blocks = d // BN
+    dps = lax.axis_size("dp")
+
+    def kernel(dhb, dzo, mix_ref, cv_ref, zin_ref, n1_ref, sel_ref, m1_ref, m2_ref, taps_ref, a_out_ref,
+               b_in_ref, w_out_ref, dp_ref, dzi_ref, gi_ref):
+        sel_f = sel_ref[...].astype(f32)
+        m1 = m1_ref[...]
+        m2 = m2_ref[...]
+
+        def conv(j):
+            dyc = nt(dhb[...], w_out_ref[col(j), :]) + nt(dzo[...], a_out_ref[col(j), :])
+            dp_ref[:, col(blocks + j)] = (dyc * cv_ref[:, col(j)].astype(f32)).astype(bf16)
+            dcv = dyc * mix_ref[:, col(blocks + j)].astype(f32)
+            dbx = (
+                taps_ref[2:3, col(j)] * dcv
+                + taps_ref[1:2, col(j)] * pltpu.roll(dcv * m1, rows - 1, 0)
+                + taps_ref[0:1, col(j)] * pltpu.roll(dcv * m2, rows - 2, 0)
+            )
+            dp_ref[:, col(j)] = (dbx * mix_ref[:, col(2 * blocks + j)].astype(f32)).astype(bf16)
+            dp_ref[:, col(2 * blocks + j)] = (dbx * mix_ref[:, col(j)].astype(f32)).astype(bf16)
+
+        loop(blocks, conv)
+        dzi_ref[...] = (nt(dp_ref[...], b_in_ref[...]) * sel_f).astype(bf16)
+        spread(gi_ref, 0, nn(zin_ref[...].T, dp_ref[...]))
+        spread(gi_ref, 3 * (d // 4), nn(dzi_ref[...].T, n1_ref[...]))
+
+    return pl.pallas_call(
+        kernel,
+        name="back",
+        out_shape=[
+            sds((rows, 3 * d), bf16), sds((rows, c), bf16), sds((dps, 4, c // dps, d), bf16),
+        ],
+        in_specs=[vmem_spec()] * 13,
+        out_specs=[vmem_spec()] * 3,
+        compiler_params=params(),
+        cost_estimate=cost(2 * rows * d * 4 * d),
+    )(dhb, dzo, mix, cv, zin, n1, sel2, m1, m2, taps, a_out, b_in, w_out)
+
+
+def last_call(dp, dzi, dh, x, gain1, a_in, w_in):
+    rows, d = x.shape
+
+    def kernel(dp_ref, dzi_ref, dh_ref, x_ref, g1_ref, a_in_ref, w_in_ref, out_ref, dn_ref):
+        def dns(j):
+            dn_ref[:, col(j)] = nt(dp_ref[...], w_in_ref[col(j), :]) + nt(dzi_ref[...], a_in_ref[col(j), :])
+
+        loop(d // BN, dns)
+        g1 = g1_ref[...]
+
+        def norm1(i):
+            v = dh_ref[row(i), :] + norm_back_rows(x_ref[row(i), :].astype(f32), g1, dn_ref[row(i), :])
+            out_ref[row(i), :] = v.astype(bf16)
+
+        loop(rows // ROWS, norm1)
+
+    return pl.pallas_call(
+        kernel,
+        name="last",
+        out_shape=sds((rows, d), bf16),
+        in_specs=[vmem_spec()] * 7,
+        out_specs=vmem_spec(),
+        scratch_shapes=[pltpu.VMEM((rows, d), f32)],
+        compiler_params=params(),
+        cost_estimate=cost(2 * rows * d * 4 * d),
+    )(dp, dzi, dh, x, gain1, a_in, w_in)
+
+
+def core_copies(arrays):
+    return [swap_dp(a, CORE_BIT) for a in arrays]
+
+
+def near(zs):
+    return [swap_dp(zs, X_BIT), swap_dp(zs, Y_BIT), swap_dp(zs, X_BIT | Y_BIT)]
+
+
+def spread_over_dp(values):
+    s = lax.axis_index("dp")
+    values = values[None]
+    bit = 1
+    while bit < lax.axis_size("dp"):
+        other = swap_dp(values, bit)
+        mine_first = jnp.concatenate([values, other], axis=0)
+        other_first = jnp.concatenate([other, values], axis=0)
+        values = jnp.where((s & bit) == 0, mine_first, other_first)
+        bit *= 2
+    return values
+
+
+def total(values):
+    return jnp.sum(values.astype(f32), axis=0).astype(bf16)
+
+
+def exchange(values, axis):
+    flat = values.reshape(values.shape[0], -1, values.shape[-1])
+    return lax.all_to_all(flat, axis, split_axis=0, concat_axis=0, tiled=True).reshape(values.shape)
+
+
+def send_to_groups(values):
+    groups, z = lax.axis_size("group"), lax.axis_index("group")
+    out = []
+    for t in range(1, groups):
+        piece = lax.dynamic_index_in_dim(values, (z + t) % groups, 0, keepdims=False)
+        out.append(lax.ppermute(piece, "group", [(i, (i + t) % groups) for i in range(groups)]))
+    return [*out, lax.dynamic_index_in_dim(values, z, 0, keepdims=False)]
+
+
+def add_up(parts):
+    whole = parts[0].astype(f32)
+    for p in parts[1:]:
+        whole = whole + p.astype(f32)
+    return whole.astype(bf16)
+
+
+def local_pieces(
+    tokens, cotangent, order, lengths, adapter_ids, norm_gain, ffn_gain, conv_weight,
+    in_weight, out_weight, gate_weight, up_weight, down_weight,
+    a_in, b_in, a_out, b_out, a_gate, b_gate, a_up, b_up, a_down, b_down,
+):
+    dp_count = lax.axis_size("dp")
+    s = lax.axis_index("dp")
+    z = lax.axis_index("group")
+    ids = jnp.stack([s, z]).astype(jnp.int32)
+    rows, d = tokens.shape
+    order_row = order[0]
+    counting = jnp.arange(dp_count, dtype=jnp.int32)
+    inverse_row = jnp.sum(
+        jnp.where(order_row[None, :] == counting[:, None], counting[None, :], 0), axis=1
+    )
+    pr = d // dp_count
+    quarter = gate_weight.shape[1]
+    width = quarter // PARTS
+    dr = 4 * width // dp_count
+    h_d = down_weight.shape[1]
+
+    def rows_of(w):
+        return lax.dynamic_slice_in_dim(w, s * pr, pr, 0)
+
+    io_piece = jnp.concatenate([rows_of(in_weight), rows_of(out_weight)], axis=1)
+    gate_rows = rows_of(gate_weight)
+    up_rows = rows_of(up_weight)
+    per = width // dr
+
+    def ffn_piece(j):
+        down = lax.dynamic_slice_in_dim(
+            down_weight, (s // per) * quarter + j * width + (s % per) * dr, dr, 0
+        )
+        cols = slice(j * width, (j + 1) * width)
+        tail = jnp.concatenate([down[pr:, :128], down[pr:, 128:]], axis=0)
+        packed = jnp.concatenate([down[:pr], tail], axis=1)
+        return jnp.concatenate([gate_rows[:, cols], up_rows[:, cols], packed], axis=0)
+
+    packed = [ffn_piece(j) for j in range(PARTS)]
+    arrived = lax.all_to_all(cotangent, "dp", split_axis=0, concat_axis=0, tiled=True)
+    zs_io = from_planes(io_piece)
+    near_io = near(zs_io)
+    zs = [from_planes(after(packed[0], zs_io))]
+    for j in range(1, PARTS):
+        zs.append(from_planes(after(packed[j], zs[j - 1])))
+    io = [zs_io, *near_io]
+    io = io + core_copies(io)
+    dy = lax.all_to_all(
+        after(regroup(arrived, inverse_row, dp_count), zs_io), "dp", split_axis=0, concat_axis=0, tiled=True
+    )
+
+    sel, after_one, after_two = per_token_tables(
+        lengths[:, 0, :][s], adapter_ids[:, 0, :][s], rows, a_in.shape[1], ADAPTER_RANK
+    )
+    sel2 = sel * adapter_scale
+    gain1 = norm_gain[None, :]
+    gain2 = ffn_gain[None, :]
+    a_gu = jnp.concatenate([a_gate, a_up], axis=1)
+    nears = near(after(zs[0], dy, *near_io))
+    n1, zin, mix, cv, y, zout, h, n2, zgu, w_in, w_out = front_call(
+        after(ids, dy, zs[1]), io, in_weight, out_weight, tokens, gain1, gain2, conv_weight,
+        sel2, after_one, after_two, a_in, b_in, a_out, b_out, a_gu,
+    )
+    dzd = (nt(dy, b_down) * sel2.astype(f32)).astype(bf16)
+    state = (None, h, None, None)
+    previous = n2
+    grads = []
+    for j in range(PARTS):
+        arrays = [zs[j], *[after(v, previous) for v in nears]]
+        arrays = arrays + core_copies(arrays)
+        if j + 1 < PARTS:
+            nears = near(after(zs[j + 1], previous, *arrays[1:4]))
+        if j == PARTS - 1:
+            early = exchange(after(jnp.concatenate(grads, axis=2), *arrays), "dp")
+        *state, g = ffn_call(
+            j, after(ids, *zs[j + 1 : j + 3]), arrays, gate_weight, up_weight,
+            down_weight, n2, dy, zgu, dzd, b_gate, b_up, a_down, *state,
+        )
+        previous = state[2]
+        grads.append(g)
+    late = exchange(grads[-1], "dp")
+    early_dp = total(after(early, g))
+    early = send_to_groups(early_dp)
+    result, dh, dhb, dzo, g_a = middle_call(
+        *state, h, n2, dy, y, zout, sel2, after(gain2, early_dp), b_down, a_gu, b_out
+    )
+    g_a = exchange(g_a, "dp")
+    early = add_up([after(early[0], dzo), *early[1:]])
+    late_dp = total(after(late, dzo))
+    late = send_to_groups(late_dp)
+    dp, dzi, g_i = back_call(
+        dhb, dzo, mix, cv, zin, n1, sel2, after_one, after_two, after(conv_weight, late_dp, early), a_out, b_in,
+        w_out,
+    )
+    g_i = exchange(g_i, "dp")
+    late = add_up([after(late[0], dzi), *late[1:]])
+    ffn = jnp.concatenate([early, late], axis=0).astype(f32)
+    ga_dp = total(after(g_a, dzi))
+    g_a = send_to_groups(ga_dp)
+    ffn = lax.all_gather(ffn, "dp")
+    input_grad = last_call(dp, dzi, dh, tokens, after(gain1, ga_dp), a_in, w_in)
+    g_i = add_up(send_to_groups(total(after(g_i, input_grad))))
+    g_a = add_up([after(g_a[0], input_grad), *g_a[1:]])
+    small = spread_over_dp(jnp.concatenate([g_a, g_i], axis=1)).astype(f32)
+    c = a_in.shape[1]
+    ffn = ffn.transpose(1, 0, 2, 3).reshape(PARTS * 3, c, width)
+
+    def joined(k):
+        return jnp.concatenate([ffn[3 * j + k] for j in range(PARTS)], axis=1)
+
+    q = d // lax.axis_size("group")
+    small = small.reshape(c, -1)
+    side, front_grads = small[:, : 5 * q], small[:, 5 * q :]
+    cuts = [front_grads[:, : 3 * q], front_grads[:, 3 * q :]] + [side[:, k * q : (k + 1) * q] for k in range(5)]
+    g_in_b, g_in_a, g_out_b, g_down_b, g_gate_a, g_up_a, g_out_a = cuts
+    return (
+        result, input_grad, g_in_a.T, g_in_b, g_out_a.T, g_out_b, g_gate_a.T, joined(0), g_up_a.T, joined(1),
+        joined(2).T, g_down_b,
+    )
+
+
 def solution(mesh):
     in_specs = (
         P(("dp", "group"), None),
@@ -358,4 +1050,5 @@
         P("group", None),
         P(None, "group"),
     )
-    return jax.shard_map(local, mesh=mesh, in_specs=in_specs, out_specs=out_specs, check_vma=False)
+    small = dict(mesh.shape) == {"dp": 8, "group": 4}
+    return jax.shard_map(local_pieces if small else local, mesh=mesh, in_specs=in_specs, out_specs=out_specs, check_vma=False)

time: 885 us -> 481 us (0.54)
  waiting for transfers between devices: 456 us -> 81.9 us
  matrix products: 237 us -> 2.37 us
  Pallas kernels: 0 us -> 225 us
  starting transfers between devices: 9.12 us -> 99.5 us
  local copies, waits for them, and re-layouts: 109 us -> 29 us
  other arithmetic: 32.9 us -> 14.2 us
    dot_general x40 -> x1, matrix products: 237 us -> 2.37 us  [nt(): lax.dot_general(a, b, (((1,), (1,)), ((), ())), preferred_element_type=f32)]
    all_gather x6 -> x1, waiting for transfers between devices: 226 us -> 0.01 us  [local_pieces(): ffn = lax.all_gather(ffn, 'dp')]
    pallas_call x0 -> x11, Pallas kernels: none -> 225 us  [the longest x3 136 us: ffn_call(): pl.pallas_call(kernel, name=f'ffn{part}', out_shape=outs, in_specs=[smem_...]
    unnamed x9 -> x1, waiting for transfers between devices: 112 us -> 0.02 us
    ppermute x0 -> x55, waiting for transfers between devices: none -> 81.9 us  [the longest x12 44.1 us: from_planes(): lax.ppermute(piece, 'group', [(i, (i + t) % groups) for i in range(groups)])]
    reduce_scatter x1 -> x0, waiting for transfers between devices: 75.1 us -> none  [reduce_grads(): lax.psum_scatter(flat, ('group', 'dp'), scatter_dimension=0, tiled=True)]
    ppermute x0 -> x55, starting transfers between devices: none -> 73.6 us  [the longest x12 36.4 us: from_planes(): lax.ppermute(piece, 'group', [(i, (i + t) % groups) for i in range(groups)])]
    dot_general x5 -> x0, local copies, waits for them, and re-layouts: 51 us -> none  [wide_product(): jnp.einsum('rk,gkn->rgn', rows, stacked, preferred_element_type=jnp.float32)]
  transfers between devices with their start and end apart: 10 -> 62, of which waited for: 9 -> 19; matrix products, arithmetic and copies ran while one was open for 23% -> 6% of each run, Pallas kernels for 0% -> 48%
where the time goes in v2:
time: 481 us; the launch traced here: 472 us
  Pallas kernels  225 us (47%)
  starting transfers between devices  99.5 us (21%)
  waiting for transfers between devices  81.9 us (17%)
  local copies, waits for them, and re-layouts  29 us (6%)
  between operations  20.3 us (4%)
  other arithmetic  14.2 us (3%)
    pallas_call x3, Pallas kernels, ffn_call(): pl.pallas_call(kernel, name=f'ffn{part}', out_shape=outs, in_specs=[smem_...  136 us
    ppermute x12, waiting for transfers between devices, from_planes(): lax.ppermute(piece, 'group', [(i, (i + t) % groups) for i in range(groups)])  44.1 us
    ppermute x12, starting transfers between devices, from_planes(): lax.ppermute(piece, 'group', [(i, (i + t) % groups) for i in range(groups)])  36.4 us
    pallas_call x1, Pallas kernels, front_call(): pl.pallas_call(kernel, name='front', out_shape=outs, in_specs=[smem_spec(...  29.2 us
    ppermute x31, waiting for transfers between devices, swap_dp(): lax.ppermute(values, 'dp', [(i, i ^ bit) for i in range(lax.axis_size('dp...  27.9 us
    ppermute x31, starting transfers between devices, swap_dp(): lax.ppermute(values, 'dp', [(i, i ^ bit) for i in range(lax.axis_size('dp...  20.5 us
    pallas_call x1, Pallas kernels, last_call(): pl.pallas_call(kernel, name='last', out_shape=sds((rows, d), bf16), in_sp...  17.5 us
    pallas_call x1, Pallas kernels, back_call(): pl.pallas_call(kernel, name='back', out_shape=[sds((rows, 3 * d), bf16),...  16.9 us
  transfers between devices with their start and end apart: 62, of which 19 were waited for; matrix products, arithmetic and copies ran while one was open for 6% of the time, Pallas kernels for 48%

profile of v2, /device:TPU:0, one launch (start us, length us, event | category | flops | bytes accessed | tf_op | source)
XLA Modules:
  0.0 472.2 jit_solution(9456865849662208025)
XLA Ops:
  7.2 5.2 %all-to-all-start = ((bf16[8,128,1024]{2,1,0:T(8,128)(2,1)}), bf16[8,128,1024]{2,1,0:T(8,128)(2,1)S(1)}, u32[]{:S(2)}, u32[]{:S(2)}) async-start(bf16[8,128,1024]{2,1,0:T(8,128)(2,1)} %bitcast.112), calls=%async_computation | async-start | bytes 4194304 | tf_op jit(solution)/shard_map/all_to_all | solution.py:931
  15.8 2.6 collective-permute-start.1
  25.7 10.4 %collective-permute-done.1.refs_1_ = bf16[128,1024]{1,0:T(8,128)(2,1)S(1)} collective-permute-done((bf16[128,1024]{1,0:T(8,128)(2,1)S(1)}, bf16[128,1024]{1,0:T(8,128)(2,1)S(1)}, u32[]{:S(2)}, u32[]{:S(2)}) %collective-permute-start.1) | collective-permute-done | bytes 262176 | tf_op jit(solution)/shard_map/ppermute | solution.py:370
  45.4 4.0 all-to-all-start.1
  57.2 5.4 %collective-permute-start.3 = (bf16[384,384]{1,0:T(8,128)(2,1)S(1)}, bf16[384,384]{1,0:T(8,128)(2,1)S(1)}, u32[]{:S(2)}, u32[]{:S(2)}) collective-permute-start(bf16[384,384]{1,0:T(8,128)(2,1)S(1)} %maximum_maximum_fusion.2), channel_id=1, source_target_pairs={{0,1},{1,2},{2,3},{3,0},{4,5},{5,6},{6,7},{7,4},{8,9},{9,10},{10,1... | collective-permute-start | bytes 884744 | tf_op jit(solution)/shard_map/ppermute | solution.py:370
  65.0 7.4 %collective-permute-done.3.refs_0_ = bf16[384,384]{1,0:T(8,128)(2,1)S(1)} collective-permute-done((bf16[384,384]{1,0:T(8,128)(2,1)S(1)}, bf16[384,384]{1,0:T(8,128)(2,1)S(1)}, u32[]{:S(2)}, u32[]{:S(2)}) %collective-permute-start.3) | collective-permute-done | bytes 294944 | tf_op jit(solution)/shard_map/ppermute | solution.py:370
  73.9 10.0 %collective-permute-done.4.refs_1_ = bf16[384,384]{1,0:T(8,128)(2,1)S(1)} collective-permute-done((bf16[384,384]{1,0:T(8,128)(2,1)S(1)}, bf16[384,384]{1,0:T(8,128)(2,1)S(1)}, u32[]{:S(2)}, u32[]{:S(2)}) %collective-permute-start.4) | collective-permute-done | bytes 294944 | tf_op jit(solution)/shard_map/ppermute | solution.py:370
  84.0 8.6 %collective-permute-done.12.refs_2_ = bf16[384,1024]{1,0:T(8,128)(2,1)} collective-permute-done((bf16[384,1024]{1,0:T(8,128)(2,1)S(1)}, bf16[384,1024]{1,0:T(8,128)(2,1)}, u32[]{:S(2)}, u32[]{:S(2)}) %collective-permute-start.12) | collective-permute-done | bytes 786464 | tf_op jit(solution)/shard_map/ppermute | solution.py:339
  95.4 5.4 %collective-permute-start.6 = (bf16[384,384]{1,0:T(8,128)(2,1)}, bf16[384,384]{1,0:T(8,128)(2,1)S(1)}, u32[]{:S(2)}, u32[]{:S(2)}) collective-permute-start(bf16[384,384]{1,0:T(8,128)(2,1)} %maximum_maximum_fusion.1), channel_id=1, source_target_pairs={{0,1},{1,2},{2,3},{3,0},{4,5},{5,6},{6,7},{7,4},{8,9},{9,10},{10,1... | collective-permute-start | bytes 884744 | tf_op jit(solution)/shard_map/ppermute | solution.py:370
  103.5 6.4 %collective-permute-done.14.refs_4_ = bf16[384,1024]{1,0:T(8,128)(2,1)} collective-permute-done((bf16[384,1024]{1,0:T(8,128)(2,1)S(1)}, bf16[384,1024]{1,0:T(8,128)(2,1)}, u32[]{:S(2)}, u32[]{:S(2)}) %collective-permute-start.14) | collective-permute-done | bytes 786464 | tf_op jit(solution)/shard_map/ppermute | solution.py:339
  109.9 7.1 %collective-permute-start.8 = (bf16[384,384]{1,0:T(8,128)(2,1)}, bf16[384,384]{1,0:T(8,128)(2,1)}, u32[]{:S(2)}, u32[]{:S(2)}) collective-permute-start(bf16[384,384]{1,0:T(8,128)(2,1)} %maximum_maximum_fusion.1), channel_id=1, source_target_pairs={{0,3},{1,0},{2,1},{3,2},{4,7},{5,4},{6,5},{7,6},{8,11},{9,8},{10,9... | collective-permute-start | bytes 884744 | tf_op jit(solution)/shard_map/ppermute | solution.py:370
  117.5 5.7 %collective-permute-done.7.refs_1_ = bf16[384,384]{1,0:T(8,128)(2,1)S(1)} collective-permute-done((bf16[384,384]{1,0:T(8,128)(2,1)}, bf16[384,384]{1,0:T(8,128)(2,1)S(1)}, u32[]{:S(2)}, u32[]{:S(2)}) %collective-permute-start.7) | collective-permute-done | bytes 294944 | tf_op jit(solution)/shard_map/ppermute | solution.py:370
  137.3 5.3 %collective-permute-start.11 = (bf16[384,384]{1,0:T(8,128)(2,1)}, bf16[384,384]{1,0:T(8,128)(2,1)}, u32[]{:S(2)}, u32[]{:S(2)}) collective-permute-start(bf16[384,384]{1,0:T(8,128)(2,1)} %maximum_maximum_fusion), channel_id=1, source_target_pairs={{0,3},{1,0},{2,1},{3,2},{4,7},{5,4},{6,5},{7,6},{8,11},{9,8},{10,9... | collective-permute-start | bytes 884744 | tf_op jit(solution)/shard_map/ppermute | solution.py:370
  142.6 29.2 %front.1 = (bf16[1024,1024]{1,0:T(8,128)(2,1)}, bf16[1024,128]{1,0:T(8,128)(2,1)}, bf16[1024,3072]{1,0:T(8,128)(2,1)}, bf16[1024,1024]{1,0:T(8,128)(2,1)}, bf16[...) custom-call(s32[2]{0:T(128)} %pad_add_fusion.refs_0_, ...), custom_call_target="tpu_custom_call" | custom-call | flops 697932160 | bytes 697932 | tf_op jit(solution)/shard_map/front/pallas_call | solution.py:531
  174.3 8.9 %collective-permute-done.9.refs_0_ = bf16[384,384]{1,0:T(8,128)(2,1)S(1)} collective-permute-done((bf16[384,384]{1,0:T(8,128)(2,1)S(1)}, bf16[384,384]{1,0:T(8,128)(2,1)S(1)}, u32[]{:S(2)}, u32[]{:S(2)}) %collective-permute-start.9) | collective-permute-done | bytes 294944 | tf_op jit(solution)/shard_map/ppermute | solution.py:370
  189.0 2.4 fusion.refs_20_
  192.5 45.1 %ffn0.1 = (f32[1024,1024]{1,0:T(8,128)}, f32[1024,1024]{1,0:T(8,128)}, f32[1024,256]{1,0:T(8,128)}, f32[1024,128]{1,0:T(8,128)}, bf16[8,4,3,16,384]{4,3,2,1,0:T(8,128)(2,1)}) custom-call(s32[2]{0:T(128)} %pad_add_fusion.refs_0_, bf16[1152,384]{1,0:T(8,128)(2,1)} %stacked.5.refs_1_, bf16[1152,384]{1,0:T(8,128)(2,1)} %collective-permute-done.15.refs_2_, ...), custom_call_target="tpu_custom_call" | custom-call | flops 1570347392 | bytes 1570347 | tf_op jit(solution)/shard_map/ffn0/pallas_call | solution.py:688
  244.0 45.8 %ffn1.1 = (f32[1024,1024]{1,0:T(8,128)}, f32[1024,1024]{1,0:T(8,128)}, f32[1024,256]{1,0:T(8,128)}, f32[1024,128]{1,0:T(8,128)}, bf16[8,4,3,16,384]{4,3,2,1,0:T(8,128)(2,1)}) custom-call(s32[2]{0:T(128)} %pad_add_fusion.refs_0_, bf16[1152,384]{1,0:T(8,128)(2,1)} %stacked.6.refs_1_, bf16[1152,384]{1,0:T(8,128)(2,1)} %collective-permute-done.26.refs_2_, ...), custom_call_target="tpu_custom_call" | custom-call | flops 1570347392 | bytes 1570347 | tf_op jit(solution)/shard_map/ffn1/pallas_call | solution.py:688
  290.7 2.9 pad_maximum_fusion
  296.5 3.6 all-to-all-start.2
  300.1 45.4 %ffn2.1 = (f32[1024,1024]{1,0:T(8,128)}, f32[1024,1024]{1,0:T(8,128)}, f32[1024,256]{1,0:T(8,128)}, f32[1024,128]{1,0:T(8,128)}, bf16[8,4,3,16,384]{4,3,2,1,0:T(8,128)(2,1)}) custom-call(s32[2]{0:T(128)} %pad_add_fusion.refs_0_, bf16[1152,384]{1,0:T(8,128)(2,1)} %stacked.7.refs_1_, bf16[1152,384]{1,0:T(8,128)(2,1)} %collective-permute-done.29.refs_2_, ...), custom_call_target="tpu_custom_call" | custom-call | flops 1570347392 | bytes 1570347 | tf_op jit(solution)/shard_map/ffn2/pallas_call | solution.py:688
  345.6 4.4 all-to-all-start.3
  351.0 16.6 %middle.1 = (bf16[1024,1024]{1,0:T(8,128)(2,1)}, f32[1024,1024]{1,0:T(8,128)}, bf16[1024,1024]{1,0:T(8,128)(2,1)}, bf16[1024,128]{1,0:T(8,128)(2,1)}, bf16[8,4,16,1280]{3,2,1,0:T(8,128)(2,1)}) custom-call(f32[1024,1024]{1,0:T(8,128)} %get-tuple-element.106.acc_ref, f32[1024,1024]{1,0:T(8,128)} %get-tuple-element.107.dn_ref, ...), custom_call_target="tpu_custom_call" | custom-call | flops 536870912 | bytes 536870 | tf_op jit(solution)/shard_map/middle/pallas_call | solution.py:761
  367.6 4.4 all-to-all-start.4
  372.5 3.4 collective-permute-start.42
  376.8 2.3 collective-permute-done.40
  381.3 16.9 %back.1 = (bf16[1024,3072]{1,0:T(8,128)(2,1)}, bf16[1024,128]{1,0:T(8,128)(2,1)}, bf16[8,4,16,1024]{3,2,1,0:T(8,128)(2,1)}) custom-call(bf16[1024,1024]{1,0:T(8,128)(2,1)} %get-tuple-element.119.dhb, bf16[1024,128]{1,0:T(8,128)(2,1)} %get-tuple-element.120.dzo, bf16[1024,3072]{1,0:T(8,128)(2,1)} %get-tuple-element.121.mix_ref, ...), custom_call_target="tpu_custom_call" | custom-call | flops 536870912 | bytes 536870 | tf_op jit(solution)/shard_map/back/pallas_call | solution.py:805
  398.3 4.3 all-to-all-start.5
  410.9 17.5 %last.1 = bf16[1024,1024]{1,0:T(8,128)(2,1)} custom-call(bf16[1024,3072]{1,0:T(8,128)(2,1)} %get-tuple-element.129.dp_ref, bf16[1024,128]{1,0:T(8,128)(2,1)} %get-tuple-element.130.dzi_ref, f32[1024,1024]{1,0:T(8,128)} %get-tuple-element.131.dh_ref, bf16[1024,1024]{1,0:T(8,128)(2,1)} %x_ref.1, f32[1,1024]{1,0:T(1,128)} %bitcast.129, ...), custom_call_target="tpu_custom_call" | custom-call | flops 536870912 | bytes 536870 | tf_op jit(solution)/shard_map/last/pallas_call | solution.py:834
  435.0 2.5 collective-permute-start.45
  442.8 4.2 collective-permute-done.50
  448.8 6.7 %collective-permute-done.51 = bf16[4,16,2304]{2,1,0:T(8,128)(2,1)S(1)} collective-permute-done((bf16[4,16,2304]{2,1,0:T(8,128)(2,1)S(1)}, bf16[4,16,2304]{2,1,0:T(8,128)(2,1)S(1)}, u32[]{:S(2)}, u32[]{:S(2)}) %collective-permute-start.51) | collective-permute-done | bytes 294944 | tf_op jit(solution)/shard_map/ppermute | solution.py:339
  (229 shorter events, 101.8 us)
Async XLA Ops:
  7.2 32.4 %all-to-all-start = ((bf16[8,128,1024]{2,1,0:T(8,128)(2,1)}), bf16[8,128,1024]{2,1,0:T(8,128)(2,1)S(1)}, u32[]{:S(2)}, u32[]{:S(2)}) async-start(bf16[8,128,1024]{2,1,0:T(8,128)(2,1)} %bitcast.112), calls=%async_computation | async-start | bytes 4194304 | tf_op jit(solution)/shard_map/all_to_all | solution.py:931
  15.8 20.3 %collective-permute-start.1 = (bf16[128,1024]{1,0:T(8,128)(2,1)S(1)}, bf16[128,1024]{1,0:T(8,128)(2,1)S(1)}, u32[]{:S(2)}, u32[]{:S(2)}) collective-permute-start(bf16[128,1024]{1,0:T(8,128)(2,1)S(1)} %pad_maximum_fusion.3), channel_id=1, source_target_pairs={{0,2},{1,3},{2,0},{3,1},{4,6},{5,7},{6,4},{7,5},{8,10},{9,11},{10,... | collective-permute-start | bytes 786440 | tf_op jit(solution)/shard_map/ppermute | solution.py:370
  18.4 17.8 %collective-permute-start.2 = (bf16[128,1024]{1,0:T(8,128)(2,1)S(1)}, bf16[128,1024]{1,0:T(8,128)(2,1)S(1)}, u32[]{:S(2)}, u32[]{:S(2)}) collective-permute-start(bf16[128,1024]{1,0:T(8,128)(2,1)S(1)} %pad_maximum_fusion.3), channel_id=1, source_target_pairs={{0,3},{1,0},{2,1},{3,2},{4,7},{5,4},{6,5},{7,6},{8,11},{9,8},{10,9... | collective-permute-start | bytes 786440 | tf_op jit(solution)/shard_map/ppermute | solution.py:370
  45.4 71.7 %all-to-all-start.1 = ((bf16[8,128,1024]{2,1,0:T(8,128)(2,1)}), bf16[8,128,1024]{2,1,0:T(8,128)(2,1)S(1)}, u32[]{:S(2)}, u32[]{:S(2)}) async-start(bf16[8,128,1024]{2,1,0:T(8,128)(2,1)} %bitcast.13), calls=%async_computation.1 | async-start | bytes 4194304 | tf_op jit(solution)/shard_map/all_to_all | solution.py:939
  51.3 41.3 %collective-permute-start.12 = (bf16[384,1024]{1,0:T(8,128)(2,1)S(1)}, bf16[384,1024]{1,0:T(8,128)(2,1)}, u32[]{:S(2)}, u32[]{:S(2)}) collective-permute-start(bf16[384,1024]{1,0:T(8,128)(2,1)S(1)} %copy-done.4), channel_id=1, source_target_pairs={{0,8},{4,12},{8,0},{12,4},{16,24},{20,28},{24,16},{28,20},{1,9},{5... | collective-permute-start | bytes 2359304 | tf_op jit(solution)/shard_map/ppermute | solution.py:339
  54.8 46.1 %collective-permute-start.13 = (bf16[384,1024]{1,0:T(8,128)(2,1)S(1)}, bf16[384,1024]{1,0:T(8,128)(2,1)}, u32[]{:S(2)}, u32[]{:S(2)}) collective-permute-start(bf16[384,1024]{1,0:T(8,128)(2,1)S(1)} %copy-done.4), channel_id=1, source_target_pairs={{0,16},{4,20},{8,24},{12,28},{16,0},{20,4},{24,8},{28,12},{1,17},{... | collective-permute-start | bytes 2359304 | tf_op jit(solution)/shard_map/ppermute | solution.py:339
  57.1 52.8 %collective-permute-start.14 = (bf16[384,1024]{1,0:T(8,128)(2,1)S(1)}, bf16[384,1024]{1,0:T(8,128)(2,1)}, u32[]{:S(2)}, u32[]{:S(2)}) collective-permute-start(bf16[384,1024]{1,0:T(8,128)(2,1)S(1)} %copy-done.4), channel_id=1, source_target_pairs={{0,24},{4,28},{8,16},{12,20},{16,8},{20,12},{24,0},{28,4},{1,25},{... | collective-permute-start | bytes 2359304 | tf_op jit(solution)/shard_map/ppermute | solution.py:339
  62.7 21.3 %collective-permute-start.4 = (bf16[384,384]{1,0:T(8,128)(2,1)S(1)}, bf16[384,384]{1,0:T(8,128)(2,1)S(1)}, u32[]{:S(2)}, u32[]{:S(2)}) collective-permute-start(bf16[384,384]{1,0:T(8,128)(2,1)S(1)} %maximum_maximum_fusion.2), channel_id=1, source_target_pairs={{0,2},{1,3},{2,0},{3,1},{4,6},{5,7},{6,4},{7,5},{8,10},{9,11},{10,... | collective-permute-start | bytes 884744 | tf_op jit(solution)/shard_map/ppermute | solution.py:370
  72.4 21.0 %collective-permute-start.5 = (bf16[384,384]{1,0:T(8,128)(2,1)S(1)}, bf16[384,384]{1,0:T(8,128)(2,1)}, u32[]{:S(2)}, u32[]{:S(2)}) collective-permute-start(bf16[384,384]{1,0:T(8,128)(2,1)S(1)} %maximum_maximum_fusion.2), channel_id=1, source_target_pairs={{0,3},{1,0},{2,1},{3,2},{4,7},{5,4},{6,5},{7,6},{8,11},{9,8},{10,9... | collective-permute-start | bytes 884744 | tf_op jit(solution)/shard_map/ppermute | solution.py:370
  84.0 44.6 %collective-permute-start.16 = (bf16[384,1024]{1,0:T(8,128)(2,1)S(1)}, bf16[384,1024]{1,0:T(8,128)(2,1)}, u32[]{:S(2)}, u32[]{:S(2)}) collective-permute-start(bf16[384,1024]{1,0:T(8,128)(2,1)S(1)} %copy-done.4), channel_id=1, source_target_pairs={{0,4},{4,0},{8,12},{12,8},{16,20},{20,16},{24,28},{28,24},{1,5},{5... | collective-permute-start | bytes 2359304 | tf_op jit(solution)/shard_map/ppermute | solution.py:339
  92.6 36.5 %collective-permute-start.17 = (bf16[384,1024]{1,0:T(8,128)(2,1)}, bf16[384,1024]{1,0:T(8,128)(2,1)}, u32[]{:S(2)}, u32[]{:S(2)}) collective-permute-start(bf16[384,1024]{1,0:T(8,128)(2,1)} %collective-permute-done.12.refs_2_), channel_id=1, source_target_pairs={{0,4},{4,0},{8,12},{12,8},{16,20},{20,16},{24,28},{28,24},{1,5},{5... | collective-permute-start | bytes 2359304 | tf_op jit(solution)/shard_map/ppermute | solution.py:339
  95.4 21.7 %collective-permute-start.6 = (bf16[384,384]{1,0:T(8,128)(2,1)}, bf16[384,384]{1,0:T(8,128)(2,1)S(1)}, u32[]{:S(2)}, u32[]{:S(2)}) collective-permute-start(bf16[384,384]{1,0:T(8,128)(2,1)} %maximum_maximum_fusion.1), channel_id=1, source_target_pairs={{0,1},{1,2},{2,3},{3,0},{4,5},{5,6},{6,7},{7,4},{8,9},{9,10},{10,1... | collective-permute-start | bytes 884744 | tf_op jit(solution)/shard_map/ppermute | solution.py:370
  100.9 22.4 %collective-permute-start.7 = (bf16[384,384]{1,0:T(8,128)(2,1)}, bf16[384,384]{1,0:T(8,128)(2,1)S(1)}, u32[]{:S(2)}, u32[]{:S(2)}) collective-permute-start(bf16[384,384]{1,0:T(8,128)(2,1)} %maximum_maximum_fusion.1), channel_id=1, source_target_pairs={{0,2},{1,3},{2,0},{3,1},{4,6},{5,7},{6,4},{7,5},{8,10},{9,11},{10,... | collective-permute-start | bytes 884744 | tf_op jit(solution)/shard_map/ppermute | solution.py:370
  109.9 18.7 %collective-permute-start.8 = (bf16[384,384]{1,0:T(8,128)(2,1)}, bf16[384,384]{1,0:T(8,128)(2,1)}, u32[]{:S(2)}, u32[]{:S(2)}) collective-permute-start(bf16[384,384]{1,0:T(8,128)(2,1)} %maximum_maximum_fusion.1), channel_id=1, source_target_pairs={{0,3},{1,0},{2,1},{3,2},{4,7},{5,4},{6,5},{7,6},{8,11},{9,8},{10,9... | collective-permute-start | bytes 884744 | tf_op jit(solution)/shard_map/ppermute | solution.py:370
  117.1 54.7 %collective-permute-start.21 = (bf16[1152,384]{1,0:T(8,128)(2,1)}, bf16[1152,384]{1,0:T(8,128)(2,1)}, u32[]{:S(2)}, u32[]{:S(2)}) collective-permute-start(bf16[1152,384]{1,0:T(8,128)(2,1)} %stacked.5.refs_1_), channel_id=1, source_target_pairs={{0,24},{4,28},{8,16},{12,20},{16,8},{20,12},{24,0},{28,4},{1,25},{... | collective-permute-start | bytes 2654216 | tf_op jit(solution)/shard_map/ppermute | solution.py:339
  123.2 48.7 %collective-permute-start.20 = (bf16[1152,384]{1,0:T(8,128)(2,1)}, bf16[1152,384]{1,0:T(8,128)(2,1)}, u32[]{:S(2)}, u32[]{:S(2)}) collective-permute-start(bf16[1152,384]{1,0:T(8,128)(2,1)} %stacked.5.refs_1_), channel_id=1, source_target_pairs={{0,16},{4,20},{8,24},{12,28},{16,0},{20,4},{24,8},{28,12},{1,17},{... | collective-permute-start | bytes 2654216 | tf_op jit(solution)/shard_map/ppermute | solution.py:339
  129.1 43.3 %collective-permute-start.15 = (bf16[1152,384]{1,0:T(8,128)(2,1)}, bf16[1152,384]{1,0:T(8,128)(2,1)}, u32[]{:S(2)}, u32[]{:S(2)}) collective-permute-start(bf16[1152,384]{1,0:T(8,128)(2,1)} %stacked.5.refs_1_), channel_id=1, source_target_pairs={{0,8},{4,12},{8,0},{12,4},{16,24},{20,28},{24,16},{28,20},{1,9},{5... | collective-permute-start | bytes 2654216 | tf_op jit(solution)/shard_map/ppermute | solution.py:339
  137.2 36.6 %collective-permute-start.10 = (bf16[384,384]{1,0:T(8,128)(2,1)}, bf16[384,384]{1,0:T(8,128)(2,1)}, u32[]{:S(2)}, u32[]{:S(2)}) collective-permute-start(bf16[384,384]{1,0:T(8,128)(2,1)} %maximum_maximum_fusion), channel_id=1, source_target_pairs={{0,2},{1,3},{2,0},{3,1},{4,6},{5,7},{6,4},{7,5},{8,10},{9,11},{10,... | collective-permute-start | bytes 884744 | tf_op jit(solution)/shard_map/ppermute | solution.py:370
  137.3 36.5 %collective-permute-start.11 = (bf16[384,384]{1,0:T(8,128)(2,1)}, bf16[384,384]{1,0:T(8,128)(2,1)}, u32[]{:S(2)}, u32[]{:S(2)}) collective-permute-start(bf16[384,384]{1,0:T(8,128)(2,1)} %maximum_maximum_fusion), channel_id=1, source_target_pairs={{0,3},{1,0},{2,1},{3,2},{4,7},{5,4},{6,5},{7,6},{8,11},{9,8},{10,9... | collective-permute-start | bytes 884744 | tf_op jit(solution)/shard_map/ppermute | solution.py:370
  183.3 54.4 %collective-permute-start.28 = (bf16[1152,384]{1,0:T(8,128)(2,1)}, bf16[1152,384]{1,0:T(8,128)(2,1)}, u32[]{:S(2)}, u32[]{:S(2)}) collective-permute-start(bf16[1152,384]{1,0:T(8,128)(2,1)} %stacked.6.refs_1_), channel_id=1, source_target_pairs={{0,24},{4,28},{8,16},{12,20},{16,8},{20,12},{24,0},{28,4},{1,25},{... | collective-permute-start | bytes 2654216 | tf_op jit(solution)/shard_map/ppermute | solution.py:339
  186.9 51.4 %collective-permute-start.27 = (bf16[1152,384]{1,0:T(8,128)(2,1)}, bf16[1152,384]{1,0:T(8,128)(2,1)}, u32[]{:S(2)}, u32[]{:S(2)}) collective-permute-start(bf16[1152,384]{1,0:T(8,128)(2,1)} %stacked.6.refs_1_), channel_id=1, source_target_pairs={{0,16},{4,20},{8,24},{12,28},{16,0},{20,4},{24,8},{28,12},{1,17},{... | collective-permute-start | bytes 2654216 | tf_op jit(solution)/shard_map/ppermute | solution.py:339
  188.4 50.0 %collective-permute-start.26 = (bf16[1152,384]{1,0:T(8,128)(2,1)}, bf16[1152,384]{1,0:T(8,128)(2,1)}, u32[]{:S(2)}, u32[]{:S(2)}) collective-permute-start(bf16[1152,384]{1,0:T(8,128)(2,1)} %stacked.6.refs_1_), channel_id=1, source_target_pairs={{0,8},{4,12},{8,0},{12,4},{16,24},{20,28},{24,16},{28,20},{1,9},{5... | collective-permute-start | bytes 2654216 | tf_op jit(solution)/shard_map/ppermute | solution.py:339
  191.3 48.9 %collective-permute-start.30 = (bf16[1152,384]{1,0:T(8,128)(2,1)}, bf16[1152,384]{1,0:T(8,128)(2,1)S(1)}, u32[]{:S(2)}, u32[]{:S(2)}) collective-permute-start(bf16[1152,384]{1,0:T(8,128)(2,1)} %stacked.6.refs_1_), channel_id=1, source_target_pairs={{0,4},{4,0},{8,12},{12,8},{16,20},{20,16},{24,28},{28,24},{1,5},{5... | collective-permute-start | bytes 2654216 | tf_op jit(solution)/shard_map/ppermute | solution.py:339
  238.8 51.0 %collective-permute-start.35 = (bf16[1152,384]{1,0:T(8,128)(2,1)S(1)}, bf16[1152,384]{1,0:T(8,128)(2,1)S(1)}, u32[]{:S(2)}, u32[]{:S(2)}) collective-permute-start(bf16[1152,384]{1,0:T(8,128)(2,1)S(1)} %copy-done.2), channel_id=1, source_target_pairs={{0,24},{4,28},{8,16},{12,20},{16,8},{20,12},{24,0},{28,4},{1,25},{... | collective-permute-start | bytes 2654216 | tf_op jit(solution)/shard_map/ppermute | solution.py:339
  240.2 50.0 %collective-permute-start.34 = (bf16[1152,384]{1,0:T(8,128)(2,1)S(1)}, bf16[1152,384]{1,0:T(8,128)(2,1)}, u32[]{:S(2)}, u32[]{:S(2)}) collective-permute-start(bf16[1152,384]{1,0:T(8,128)(2,1)S(1)} %copy-done.2), channel_id=1, source_target_pairs={{0,16},{4,20},{8,24},{12,28},{16,0},{20,4},{24,8},{28,12},{1,17},{... | collective-permute-start | bytes 2654216 | tf_op jit(solution)/shard_map/ppermute | solution.py:339
  241.7 48.6 %collective-permute-start.29 = (bf16[1152,384]{1,0:T(8,128)(2,1)S(1)}, bf16[1152,384]{1,0:T(8,128)(2,1)}, u32[]{:S(2)}, u32[]{:S(2)}) collective-permute-start(bf16[1152,384]{1,0:T(8,128)(2,1)S(1)} %copy-done.2), channel_id=1, source_target_pairs={{0,8},{4,12},{8,0},{12,4},{16,24},{20,28},{24,16},{28,20},{1,9},{5... | collective-permute-start | bytes 2654216 | tf_op jit(solution)/shard_map/ppermute | solution.py:339
  242.3 51.4 %collective-permute-start.36 = (bf16[1152,384]{1,0:T(8,128)(2,1)S(1)}, bf16[1152,384]{1,0:T(8,128)(2,1)}, u32[]{:S(2)}, u32[]{:S(2)}) collective-permute-start(bf16[1152,384]{1,0:T(8,128)(2,1)S(1)} %copy-done.2), channel_id=1, source_target_pairs={{0,4},{4,0},{8,12},{12,8},{16,20},{20,16},{24,28},{28,24},{1,5},{5... | collective-permute-start | bytes 2654216 | tf_op jit(solution)/shard_map/ppermute | solution.py:339
  296.5 49.1 %all-to-all-start.2 = ((bf16[8,384,384]{2,1,0:T(8,128)(2,1)}), bf16[8,384,384]{2,1,0:T(8,128)(2,1)S(1)}, u32[]{:S(2)}, u32[]{:S(2)}) async-start(bf16[8,384,384]{2,1,0:T(8,128)(2,1)} %bitcast.18), calls=%async_computation.2 | async-start | bytes 4718592 | tf_op jit(solution)/shard_map/all_to_all | solution.py:873
  345.6 22.1 %all-to-all-start.3 = ((bf16[8,192,384]{2,1,0:T(8,128)(2,1)}), bf16[8,192,384]{2,1,0:T(8,128)(2,1)S(1)}, u32[]{:S(2)}, u32[]{:S(2)}) async-start(bf16[8,192,384]{2,1,0:T(8,128)(2,1)} %bitcast.114), calls=%async_computation.3 | async-start | bytes 2359296 | tf_op jit(solution)/shard_map/all_to_all | solution.py:873
  367.6 30.6 %all-to-all-start.4 = ((bf16[8,64,1280]{2,1,0:T(8,128)(2,1)}), bf16[8,64,1280]{2,1,0:T(8,128)(2,1)S(1)}, u32[]{:S(2)}, u32[]{:S(2)}) async-start(bf16[8,64,1280]{2,1,0:T(8,128)(2,1)} %bitcast.113), calls=%async_computation.4 | async-start | bytes 2621440 | tf_op jit(solution)/shard_map/all_to_all | solution.py:873
  398.3 30.2 %all-to-all-start.5 = ((bf16[8,64,1024]{2,1,0:T(8,128)(2,1)}), bf16[8,64,1024]{2,1,0:T(8,128)(2,1)S(1)}, u32[]{:S(2)}, u32[]{:S(2)}) async-start(bf16[8,64,1024]{2,1,0:T(8,128)(2,1)} %bitcast.115), calls=%async_computation.5 | async-start | bytes 2097152 | tf_op jit(solution)/shard_map/all_to_all | solution.py:873
  402.6 57.7 %all-gather.2.cloned.1.call-start = ((), (), s32[]{:S(2)}) async-start(), calls=%async_computation.6 | async-start | bytes 1990656 | tf_op jit(solution)/shard_map/all_gather | solution.py:991
  (59 other events, 685.8 us)
Sparse Core Ops, SparseCore 0:
  410.9 26.9 all-gather.1

commit v3 on v2

v3 whole, which is shorter than its diff:
```python
import jax
import jax.numpy as jnp
from jax import lax
from jax.experimental import pallas as pl
from jax.experimental.pallas import tpu as pltpu
from jax.sharding import PartitionSpec as P

ADAPTER_RANK = 16


eps_norm = 1e-05
adapter_scale = 2.0


def matrix_product(left, right):
    return jnp.dot(left, right, preferred_element_type=jnp.float32)


def transposed_left_matmul(left, right):
    return lax.dot_general(
        left, right, (((0,), (0,)), ((), ())), preferred_element_type=jnp.float32
    )


def transposed_right_matmul(left, right):
    return lax.dot_general(
        left, right, (((1,), (1,)), ((), ())), preferred_element_type=jnp.float32
    )


def per_token_tables(
    sequence_length_row, adapter_index_row, count_of_rows, adapter_column_span, adapter_rank_size
):
    count = sequence_length_row.shape[0]
    earlier = jnp.arange(count)[:, None] <= jnp.arange(count)[None, :]
    finish = jnp.sum(jnp.where(earlier, sequence_length_row[:, None], 0), axis=0)
    starts = finish - sequence_length_row
    counter = jnp.arange(count_of_rows, dtype=jnp.int32)
    member = ((counter[:, None] >= starts[None, :]) & (counter[:, None] < finish[None, :])).astype(
        jnp.int32
    )
    beginning = jnp.sum(member * starts[None, :], axis=1)
    position = counter - beginning
    chosen = jnp.sum(member * adapter_index_row[None, :], axis=1)
    column_span = jnp.arange(adapter_column_span, dtype=jnp.int32) // adapter_rank_size
    select_adapter = (column_span[None, :] == chosen[:, None]).astype(jnp.bfloat16)
    after_one = (position >= 1).astype(jnp.float32)[:, None]
    after_two = (position >= 2).astype(jnp.float32)[:, None]
    return (select_adapter, after_one, after_two)


def delayed(values, amount):
    return jnp.concatenate(
        [jnp.zeros((amount, values.shape[1]), values.dtype), values[:-amount]], axis=0
    )


def advanced(values, amount):
    return jnp.concatenate(
        [values[amount:], jnp.zeros((amount, values.shape[1]), values.dtype)], axis=0
    )


def regroup(values, picks, pieces):
    size = values.shape[0] // pieces
    return jnp.concatenate(
        [lax.dynamic_slice_in_dim(values, picks[i] * size, size, 0) for i in range(pieces)], axis=0
    )


def gather_weight(shard):
    size = shard.shape[0] // lax.axis_size("dp")
    piece = lax.dynamic_slice_in_dim(shard, lax.axis_index("dp") * size, size, 0)
    stacked = lax.all_gather(piece, ("group", "dp"))
    return stacked.reshape(lax.axis_size("group"), shard.shape[0], shard.shape[1])


def wide_product(rows, stacked):
    out = jnp.einsum("rk,gkn->rgn", rows, stacked, preferred_element_type=jnp.float32)
    return out.reshape(rows.shape[0], -1)


def wide_product_back(grads, stacked):
    shaped = grads.reshape(grads.shape[0], stacked.shape[0], stacked.shape[2])
    return jnp.einsum("rgn,gkn->rk", shaped, stacked, preferred_element_type=jnp.float32)


def reduce_grads(terms):
    groups = lax.axis_size("group")
    parts = [t.astype(jnp.bfloat16).reshape(groups, -1, t.shape[1]) for t in terms]
    joined = jnp.concatenate(parts, axis=1)
    flat = joined.reshape(-1, joined.shape[2])
    mine = lax.psum_scatter(flat, ("group", "dp"), scatter_dimension=0, tiled=True)
    share = lax.all_gather(mine, "dp", tiled=True)
    out, at = [], 0
    for p in parts:
        out.append(share[at : at + p.shape[1]].astype(jnp.float32))
        at += p.shape[1]
    return out


def inverse_root(values):
    return lax.rsqrt(jnp.mean(values * values, axis=-1, keepdims=True) + eps_norm)


def norm_back(values, inverse, gain, incoming_gradient):
    scaled = gain * incoming_gradient
    return inverse * scaled - values * (inverse * inverse * inverse) * jnp.mean(
        values * scaled, axis=-1, keepdims=True
    )


def adapter_project(
    input_rows, frozen_weight, adapter_down_factor, adapter_up_factor, select_adapter
):
    reduced_sum = (
        matrix_product(input_rows, adapter_down_factor).astype(jnp.bfloat16) * select_adapter
    )
    return (
        wide_product(input_rows, frozen_weight)
        + adapter_scale * matrix_product(reduced_sum, adapter_up_factor),
        reduced_sum,
    )


def adapter_project_backward(
    incoming_gradient,
    input_rows,
    frozen_weight,
    adapter_down_factor,
    adapter_up_factor,
    reduced_sum,
    select_adapter,
):
    gradient_rank_space = incoming_gradient.astype(jnp.bfloat16)
    gradient_up_factor = adapter_scale * transposed_left_matmul(gradient_rank_space, reduced_sum)
    gradient_reduced_sum = (
        adapter_scale
        * transposed_right_matmul(gradient_rank_space, adapter_up_factor)
        * select_adapter
    ).astype(jnp.bfloat16)
    grad_down = transposed_left_matmul(input_rows, gradient_reduced_sum)
    input_gradients = wide_product_back(
        gradient_rank_space, frozen_weight
    ) + transposed_right_matmul(gradient_reduced_sum, adapter_down_factor)
    return (input_gradients, grad_down, gradient_up_factor)


def local(
    tokens,
    cotangent,
    order,
    lengths,
    adapter_ids,
    norm_gain,
    ffn_gain,
    conv_weight,
    in_weight,
    out_weight,
    gate_weight,
    up_weight,
    down_weight,
    input_first_factor,
    input_second_factor,
    output_first_factor,
    output_second_factor,
    gate_first_factor,
    gate_second_factor,
    up_first_factor,
    up_second_factor,
    down_first_factor,
    down_second_factor,
):
    dp_count = lax.axis_size("dp")
    dp_index = lax.axis_index("dp")
    count_of_rows = tokens.shape[0]
    model_width = tokens.shape[1]
    order_row = order[0]
    counting = jnp.arange(dp_count, dtype=jnp.int32)
    inverse_row = jnp.sum(
        jnp.where(order_row[None, :] == counting[:, None], counting[None, :], 0), axis=1
    )
    arrived = lax.all_to_all(cotangent, "dp", split_axis=0, concat_axis=0, tiled=True)
    cotangent = lax.all_to_all(
        regroup(arrived, inverse_row, dp_count), "dp", split_axis=0, concat_axis=0, tiled=True
    )
    pack_source = dp_index
    hidden_in = tokens
    sequence_length_row = lengths[:, 0, :][pack_source]
    adapter_index_row = adapter_ids[:, 0, :][pack_source]
    select_adapter, after_one, after_two = per_token_tables(
        sequence_length_row,
        adapter_index_row,
        count_of_rows,
        input_first_factor.shape[1],
        ADAPTER_RANK,
    )
    shards = (in_weight, out_weight, gate_weight, up_weight, down_weight)
    full_in, full_out, full_gate, full_up, full_down = [gather_weight(w) for w in shards]
    hidden32 = hidden_in.astype(jnp.float32)
    inverse_one = inverse_root(hidden32)
    normed = (hidden32 * inverse_one * norm_gain).astype(jnp.bfloat16)
    mixed_in, reduced_in = adapter_project(
        normed, full_in, input_first_factor, input_second_factor, select_adapter
    )
    input_gate = mixed_in[:, :model_width]
    output_gate = mixed_in[:, model_width : 2 * model_width]
    conv_input = mixed_in[:, 2 * model_width :]
    gated = input_gate * conv_input
    convolved = (
        conv_weight[2] * gated
        + conv_weight[1] * delayed(gated, 1) * after_one
        + conv_weight[0] * delayed(gated, 2) * after_two
    )
    mixer = (output_gate * convolved).astype(jnp.bfloat16)
    branch, reduced_out = adapter_project(
        mixer, full_out, output_first_factor, output_second_factor, select_adapter
    )
    middle = hidden32 + branch
    inverse_two = inverse_root(middle)
    normed_two = (middle * inverse_two * ffn_gain).astype(jnp.bfloat16)
    gate_pre, reduced_gate = adapter_project(
        normed_two, full_gate, gate_first_factor, gate_second_factor, select_adapter
    )
    up_pre, reduced_up = adapter_project(
        normed_two, full_up, up_first_factor, up_second_factor, select_adapter
    )
    sigmoid_gate = jax.nn.sigmoid(gate_pre)
    activated = (gate_pre * sigmoid_gate * up_pre).astype(jnp.bfloat16)
    ffn_out, reduced_down = adapter_project(
        activated, full_down, down_first_factor, down_second_factor, select_adapter
    )
    result = (middle + ffn_out).astype(jnp.bfloat16)
    back_in, back_out, back_gate, back_up, back_down = full_in, full_out, full_gate, full_up, full_down
    upstream32 = cotangent.astype(jnp.float32)
    grad_act, down_a_grad, down_b_grad = adapter_project_backward(
        upstream32,
        activated,
        back_down,
        down_first_factor,
        down_second_factor,
        reduced_down,
        select_adapter,
    )
    grad_gate_pre = grad_act * up_pre * (sigmoid_gate * (1.0 + gate_pre * (1.0 - sigmoid_gate)))
    grad_up_pre = grad_act * gate_pre * sigmoid_gate
    grad_from_gate, gate_a_grad, gate_b_grad = adapter_project_backward(
        grad_gate_pre,
        normed_two,
        back_gate,
        gate_first_factor,
        gate_second_factor,
        reduced_gate,
        select_adapter,
    )
    grad_from_up, up_a_grad, up_b_grad = adapter_project_backward(
        grad_up_pre,
        normed_two,
        back_up,
        up_first_factor,
        up_second_factor,
        reduced_up,
        select_adapter,
    )
    grad_middle = upstream32 + norm_back(
        middle, inverse_two, ffn_gain, grad_from_gate + grad_from_up
    )
    grad_mixer, out_a_grad, out_b_grad = adapter_project_backward(
        grad_middle,
        mixer,
        back_out,
        output_first_factor,
        output_second_factor,
        reduced_out,
        select_adapter,
    )
    grad_output_gate = grad_mixer * convolved
    grad_conv = grad_mixer * output_gate
    grad_gated = (
        conv_weight[2] * grad_conv
        + conv_weight[1] * advanced(grad_conv * after_one, 1)
        + conv_weight[0] * advanced(grad_conv * after_two, 2)
    )
    grad_mixed = jnp.concatenate(
        [grad_gated * conv_input, grad_output_gate, grad_gated * input_gate], axis=1
    )
    grad_normed, in_a_grad, in_b_grad = adapter_project_backward(
        grad_mixed,
        normed,
        back_in,
        input_first_factor,
        input_second_factor,
        reduced_in,
        select_adapter,
    )
    grad_input = (grad_middle + norm_back(hidden32, inverse_one, norm_gain, grad_normed)).astype(
        jnp.bfloat16
    )
    early = reduce_grads(
        [down_a_grad, down_b_grad, gate_a_grad, gate_b_grad, up_a_grad, up_b_grad, out_a_grad, out_b_grad]
    )
    late = reduce_grads([in_a_grad, in_b_grad])
    totals = (
        late[0], late[1].T, early[6], early[7].T, early[2], early[3].T, early[4], early[5].T,
        early[0], early[1].T,
    )
    return (
        result,
        grad_input,
        totals[0],
        totals[1],
        totals[2],
        totals[3],
        totals[4],
        totals[5],
        totals[6],
        totals[7],
        totals[8],
        totals[9],
    )


f32 = jnp.float32
bf16 = jnp.bfloat16
VMEM_BYTES = 60 * 2**20
PARTS = 3
X_BIT, Y_BIT, CORE_BIT = 2, 4, 1


def nn(a, b):
    return lax.dot_general(a, b, (((1,), (0,)), ((), ())), preferred_element_type=f32)


def nt(a, b):
    return lax.dot_general(a, b, (((1,), (1,)), ((), ())), preferred_element_type=f32)


def swap_dp(values, bit):
    return lax.ppermute(values, "dp", [(i, i ^ bit) for i in range(lax.axis_size("dp"))])


def stacked(parts, start, width):
    size = parts[0].shape[0]

    def kernel(*refs):
        out_ref, sems = refs[-2], refs[-1]
        copies = [
            pltpu.make_async_copy(
                refs[k].at[:, start : start + width], out_ref.at[k * size : (k + 1) * size], sems.at[k]
            )
            for k in range(len(parts))
        ]
        for copy in copies:
            copy.start()
        for copy in copies:
            copy.wait()

    return pl.pallas_call(
        kernel,
        name="stacked",
        out_shape=jax.ShapeDtypeStruct((len(parts) * size, width), parts[0].dtype),
        in_specs=[any_spec()] * len(parts),
        out_specs=vmem_spec(),
        scratch_shapes=[pltpu.SemaphoreType.DMA((len(parts),))],
        compiler_params=pltpu.CompilerParams(vmem_limit_bytes=4 * 2**20),
    )(*parts)


def others(ids, values):
    groups, size, width = values.shape

    def kernel(ids_ref, in_ref, out_ref, sem):
        for t in range(1, groups):
            q = lax.rem(ids_ref[1] + groups - t, groups)
            pltpu.make_async_copy(in_ref.at[q], out_ref.at[(t - 1) * size : t * size], sem).start()
        pltpu.make_async_copy(out_ref, out_ref, sem).wait()

    return pl.pallas_call(
        kernel,
        name="others",
        out_shape=sds(((groups - 1) * size, width), bf16),
        in_specs=[smem_spec(), any_spec()],
        out_specs=vmem_spec(),
        scratch_shapes=[pltpu.SemaphoreType.DMA],
        compiler_params=pltpu.CompilerParams(vmem_limit_bytes=4 * 2**20),
    )(ids, values)


def picked(values, picks, pieces):
    size = values.shape[0] // pieces

    def kernel(picks_ref, in_ref, out_ref, sem):
        for k in range(pieces):
            at = pl.multiple_of(picks_ref[k] * size, size)
            pltpu.make_async_copy(in_ref.at[pl.ds(at, size)], out_ref.at[k * size : (k + 1) * size], sem).start()
        pltpu.make_async_copy(out_ref, out_ref, sem).wait()

    return pl.pallas_call(
        kernel,
        name="picked",
        out_shape=jax.ShapeDtypeStruct(values.shape, values.dtype),
        in_specs=[smem_spec(), any_spec()],
        out_specs=vmem_spec(),
        scratch_shapes=[pltpu.SemaphoreType.DMA],
        compiler_params=pltpu.CompilerParams(vmem_limit_bytes=6 * 2**20),
    )(picks, values)


def totals_by_shift(ids, values):
    terms, groups = values.shape[0], values.shape[1]
    shape = values.shape[2:]

    def kernel(ids_ref, in_ref, *out_refs):
        z = ids_ref[1]
        for t in range(groups):
            q = lax.rem(z + t, groups)
            whole = in_ref[0, q].astype(f32)
            for k in range(1, terms):
                whole = whole + in_ref[k, q].astype(f32)
            out_refs[(t - 1) % groups][...] = whole.astype(bf16)

    return pl.pallas_call(
        kernel,
        name="totals",
        out_shape=[jax.ShapeDtypeStruct(shape, bf16)] * groups,
        in_specs=[smem_spec(), vmem_spec()],
        out_specs=[vmem_spec()] * groups,
        compiler_params=pltpu.CompilerParams(vmem_limit_bytes=8 * 2**20),
    )(ids, values)


def from_planes(joined, widths):
    groups = lax.axis_size("group")
    got = [
        lax.ppermute(joined, "group", [(i, (i + t) % groups) for i in range(groups)])
        for t in range(1, groups)
    ]
    out, at = [], 0
    for width in widths:
        out.append(stacked(got, at, width))
        at += width
    return out


def after(values, *others):
    return lax.optimization_barrier((values, *others))[0]


def piece_table(relay=None):
    both = X_BIT | Y_BIT
    table = [(m, (1, 2, 3)) for m in (0, X_BIT, Y_BIT)]
    if relay is None:
        table.append((both, (1, 2, 3)))
    else:
        table += [(both, tuple(range(1, relay + 1))), (both, tuple(range(relay + 1, 4)))]
    return table + [(m | CORE_BIT, steps) for m, steps in table]


def any_spec():
    return pl.BlockSpec(memory_space=pl.ANY)


def vmem_spec():
    return pl.BlockSpec(memory_space=pltpu.VMEM)


def smem_spec():
    return pl.BlockSpec(memory_space=pltpu.SMEM)


def params(size=VMEM_BYTES):
    return pltpu.CompilerParams(vmem_limit_bytes=size)


def cost(flops):
    return pl.CostEstimate(flops=int(flops) // 4096, transcendentals=0, bytes_accessed=0)


def sds(shape, dtype):
    return jax.ShapeDtypeStruct(shape, dtype)


BN = 256


def col(i):
    return pl.ds(pl.multiple_of(i * BN, BN), BN)


ROWS = 128


def row(i):
    return pl.ds(pl.multiple_of(i * ROWS, ROWS), ROWS)


def loop(n, body):
    def step(i, carry):
        body(i)
        return carry

    lax.fori_loop(0, n, step, 0)


def fetched(pairs, sems):
    copies = [pltpu.make_async_copy(a, b, sems.at[k]) for k, (a, b) in enumerate(pairs)]
    for copy in copies:
        copy.start()
    return [copy.wait for copy in copies]


def put_at(buf, sem, src, r0, c0):
    dst = buf.at[pl.ds(pl.multiple_of(r0, 64), src.shape[0]), pl.ds(pl.multiple_of(c0, 128), src.shape[1])]
    pltpu.make_async_copy(src, dst, sem).start()


def own_pieces(ids, in_shard, out_shard, gate_shard, up_shard, down_shard, dps):
    d = in_shard.shape[0]
    pr = d // dps
    quarter = gate_shard.shape[1]
    width = quarter // PARTS
    dr = 4 * width // dps
    per = width // dr
    h_i, h_o, h_d = in_shard.shape[1], out_shard.shape[1], down_shard.shape[1]
    copies = [1] * (PARTS - 1) + [lax.axis_size("group")]
    shapes = [(pr, h_i + h_o + 3 * width), (pr, 3 * width), (copies[-1] * pr, 3 * width)]

    def kernel(ids_ref, in_ref, out_ref, gate_ref, up_ref, down_ref, *rest):
        outs, sems = rest[:-1], rest[-1]
        s = ids_ref[0]
        mine = pl.ds(pl.multiple_of(s * pr, pr), pr)
        for j in range(PARTS):
            dst = outs[j]
            at = 0

            def put(src, r0=0, n=pr, width_=None):
                for k in range(copies[j]):
                    to = dst.at[k * pr + r0 : k * pr + r0 + n, at : at + width_]
                    pltpu.make_async_copy(src, to, sems.at[j]).start()

            if j == 0:
                put(in_ref.at[mine], width_=h_i)
                at = h_i
                put(out_ref.at[mine], width_=h_o)
                at = h_i + h_o
            cols = pl.ds(j * width, width)
            put(gate_ref.at[mine, cols], width_=width)
            at += width
            put(up_ref.at[mine, cols], width_=width)
            at += width
            top = pl.multiple_of((s // per) * quarter + j * width + (s % per) * dr, 64)
            put(down_ref.at[pl.ds(top, pr)], width_=h_d)
            at += h_d
            half = dr - pr
            put(down_ref.at[pl.ds(top + pr, half), : width - h_d], n=half, width_=width - h_d)
            put(down_ref.at[pl.ds(top + pr, half), width - h_d :], r0=half, n=half, width_=width - h_d)
        for j, dst in enumerate(outs):
            pltpu.make_async_copy(dst, dst, sems.at[j]).wait()

    return pl.pallas_call(
        kernel,
        name="own",
        out_shape=[sds(v, bf16) for v in shapes],
        in_specs=[smem_spec()] + [any_spec()] * 5,
        out_specs=[vmem_spec()] * PARTS,
        scratch_shapes=[pltpu.SemaphoreType.DMA((PARTS,))],
        compiler_params=pltpu.CompilerParams(vmem_limit_bytes=6 * 2**20),
    )(ids, in_shard, out_shard, gate_shard, up_shard, down_shard)


def gather_copies(ids_ref, p_refs, table, pr, buf, sem, shard_ref, lo):
    s, z = ids_ref[0], ids_ref[1]
    n = shard_ref.shape[1]
    put_at(buf, sem, shard_ref, 0, z * n)
    for p_ref, (mask, steps) in zip(p_refs, table):
        for k, t in enumerate(steps):
            put_at(buf, sem, p_ref.at[k * pr : (k + 1) * pr, lo : lo + n], (s ^ mask) * pr, ((z - t) & 3) * n)


def front_call(ids, pieces, relay, in_shard, x, gain1, taps, sel2, m1, m2, a_in, b_in):
    rows, d = x.shape
    table = piece_table(relay)
    n_pieces = len(pieces)
    pr = d // lax.axis_size("dp")
    c = a_in.shape[1]
    blocks = d // BN

    def kernel(*refs):
        ids_ref = refs[0]
        p_refs = refs[1 : 1 + n_pieces]
        (in_ref, x_ref, g1_ref, taps_ref, sel_ref, m1_ref, m2_ref, a_in_ref, b_in_ref) = refs[1 + n_pieces : 10 + n_pieces]
        (n1_out, zin_ref, mix_out, cv_out, y_out, w_out, n1_ref, mix_ref, cv_ref, y_ref, w_in,
         sem_in, sems) = refs[10 + n_pieces :]
        gather_copies(ids_ref, p_refs, table, pr, w_in, sem_in, in_ref, 0)
        g1 = g1_ref[...]

        def norm1(i):
            v = x_ref[row(i), :].astype(f32)
            r = lax.rsqrt(jnp.mean(v * v, axis=-1, keepdims=True) + eps_norm)
            n1_ref[row(i), :] = (v * r * g1).astype(bf16)

        loop(rows // ROWS, norm1)
        zin_ref[...] = nn(n1_ref[...], a_in_ref[...]).astype(bf16) * sel_ref[...]
        pltpu.make_async_copy(w_in, w_in, sem_in).wait()
        stores = fetched([(n1_ref, n1_out), (w_in, w_out)], sems)
        m1 = m1_ref[...]
        m2 = m2_ref[...]

        def mix(j):
            def part(k):
                cc = col(k * blocks + j)
                v = nn(n1_ref[...], w_in[:, cc]) + nn(zin_ref[...], b_in_ref[:, cc])
                mix_ref[:, cc] = v.astype(bf16)
                pltpu.make_async_copy(mix_ref.at[:, cc], mix_out.at[:, cc], sems.at[2]).start()
                return v

            bg = part(0)
            bx = bg * part(2)
            cv = (
                taps_ref[2:3, col(j)] * bx
                + taps_ref[1:2, col(j)] * pltpu.roll(bx, 1, 0) * m1
                + taps_ref[0:1, col(j)] * pltpu.roll(bx, 2, 0) * m2
            )
            cv_ref[:, col(j)] = cv.astype(bf16)
            pltpu.make_async_copy(cv_ref.at[:, col(j)], cv_out.at[:, col(j)], sems.at[3]).start()
            y_ref[:, col(j)] = (part(1) * cv).astype(bf16)
            pltpu.make_async_copy(y_ref.at[:, col(j)], y_out.at[:, col(j)], sems.at[4]).start()

        loop(blocks, mix)
        for wait in stores:
            wait()
        pltpu.make_async_copy(mix_ref, mix_out, sems.at[2]).wait()
        pltpu.make_async_copy(cv_ref, cv_out, sems.at[3]).wait()
        pltpu.make_async_copy(y_ref, y_out, sems.at[4]).wait()

    wide = [(rows, d), (rows, 3 * d), (rows, d), (rows, d), (d, 3 * d)]
    return pl.pallas_call(
        kernel,
        name="front",
        out_shape=[sds(wide[0], bf16), sds((rows, c), bf16)] + [sds(v, bf16) for v in wide[1:]],
        in_specs=[smem_spec()] + [any_spec()] * (n_pieces + 1) + [vmem_spec()] * 8,
        out_specs=[any_spec(), vmem_spec()] + [any_spec()] * 4,
        scratch_shapes=[pltpu.VMEM(v, bf16) for v in wide]
        + [pltpu.SemaphoreType.DMA, pltpu.SemaphoreType.DMA((5,))],
        compiler_params=params(),
        cost_estimate=cost(2.6 * rows * d * 3 * d),
    )(ids, *pieces, in_shard, x, gain1, taps, sel2, m1, m2, a_in, b_in)


def join_call(ids, pieces, relay, out_shard, y, x, gain2, sel2, a_out, b_out, a_gate, a_up):
    rows, d = x.shape
    table = piece_table(relay)
    n_pieces = len(pieces)
    pr = d // lax.axis_size("dp")
    c = a_out.shape[1]
    lo = pieces[0].shape[1] - out_shard.shape[1]

    def kernel(*refs):
        ids_ref = refs[0]
        p_refs = refs[1 : 1 + n_pieces]
        (out_ref, x_hbm, y_ref, g2_ref, sel_ref, a_out_ref, b_out_ref, a_gate_ref, a_up_ref) = refs[
            1 + n_pieces : 10 + n_pieces
        ]
        (zout_ref, hb_ref, n2_ref, zgu_ref, w_out_hbm, x_ref, h_ref, w_out, sem_out, sems) = refs[10 + n_pieces :]
        gather_copies(ids_ref, p_refs, table, pr, w_out, sem_out, out_ref, lo)
        [wait_x] = fetched([(x_hbm, x_ref)], sems)
        sel = sel_ref[...]
        zout_ref[...] = nn(y_ref[...], a_out_ref[...]).astype(bf16) * sel
        wait_x()
        pltpu.make_async_copy(w_out, w_out, sem_out).wait()
        [wait_store] = fetched([(w_out, w_out_hbm)], sems)

        def mid(j):
            o = nn(y_ref[...], w_out[:, col(j)]) + nn(zout_ref[...], b_out_ref[:, col(j)])
            h_ref[:, col(j)] = x_ref[:, col(j)].astype(f32) + o

        loop(d // BN, mid)
        g2 = g2_ref[...]

        def norm2(i):
            v = h_ref[row(i), :]
            hb_ref[row(i), :] = v.astype(bf16)
            r = lax.rsqrt(jnp.mean(v * v, axis=-1, keepdims=True) + eps_norm)
            n2_ref[row(i), :] = (v * r * g2).astype(bf16)

        loop(rows // ROWS, norm2)
        zgu_ref[:, :c] = nn(n2_ref[...], a_gate_ref[...]).astype(bf16) * sel
        zgu_ref[:, c:] = nn(n2_ref[...], a_up_ref[...]).astype(bf16) * sel
        wait_store()

    return pl.pallas_call(
        kernel,
        name="join",
        out_shape=[
            sds((rows, c), bf16), sds((rows, d), bf16), sds((rows, d), bf16), sds((rows, 2 * c), bf16),
            sds((d, d), bf16),
        ],
        in_specs=[smem_spec()] + [any_spec()] * (n_pieces + 2) + [vmem_spec()] * 7,
        out_specs=[vmem_spec()] * 4 + [any_spec()],
        scratch_shapes=[
            pltpu.VMEM((rows, d), bf16), pltpu.VMEM((rows, d), f32), pltpu.VMEM((d, d), bf16),
            pltpu.SemaphoreType.DMA, pltpu.SemaphoreType.DMA((1,)),
        ],
        compiler_params=params(),
        cost_estimate=cost(2.6 * rows * d * d),
    )(ids, *pieces, out_shard, x, y, gain2, sel2, a_out, b_out, a_gate, a_up)


def ffn_call(part, ids, pieces, relay, gate_shard, up_shard, down_shard, n2, dy, zgu, dzd,
             b_gate, b_up, a_down, earlier, *state):
    rows, d = n2.shape
    table = piece_table(relay)
    n_pieces = len(pieces)
    quarter = gate_shard.shape[1]
    width = quarter // PARTS
    fp = 4 * width
    pr = d // lax.axis_size("dp")
    dr = fp // lax.axis_size("dp")
    c = zgu.shape[1] // 2
    h_d = down_shard.shape[1]
    n_state = len(state)
    first = n_state == 1
    joins = earlier is not None
    n_join = int(joins)
    dps = lax.axis_size("dp")
    half_rows = rows // 2

    def kernel(*refs):
        ids_ref = refs[0]
        p_refs = refs[1 : 1 + n_pieces]
        rest = refs[1 + n_pieces :]
        (gs_ref, us_ref, ds_ref, bg_hbm, bu_hbm, ad_hbm, n2_hbm, dy_hbm, zgu_hbm, dzd_hbm) = rest[:10]
        earlier_ref = rest[10] if joins else None
        rest = rest[10 + n_join :]
        state_in = rest[:n_state]
        state_out = rest[n_state : n_state + 4]
        (grads_out, acc_ref, dn_ref, dz_ref, zd_ref, grads_ref, wgu, wd, nzg, nzu, dyz, act, dgu,
         da_all, g_all, sems) = rest[n_state + 4 :]
        state = (acc_ref, dn_ref, dz_ref, zd_ref)
        s = ids_ref[0]
        z = ids_ref[1]
        sem_d, sem_g, sem_y, sem_n, sem_b, sem_o = [sems.at[i] for i in range(6)]
        sem_s = sems.at[6:14]

        def put(buf, sem, src, r0, c0, ra=64):
            dst = buf.at[pl.ds(pl.multiple_of(r0, ra), src.shape[0]), pl.ds(pl.multiple_of(c0, 128), src.shape[1])]
            pltpu.make_async_copy(src, dst, sem).start()

        def pieces_to(fn):
            for p_ref, (mask, steps) in zip(p_refs, table):
                for k, t in enumerate(steps):
                    fn(p_ref, k * pr, s ^ mask, (z - t) & 3)

        put(dyz, sem_y, dy_hbm, 0, 0)
        put(dyz, sem_y, dzd_hbm, 0, d)
        for q in range(4):
            at = pl.ds(q * quarter + part * width, width)
            put(wd, sem_d, ds_ref.at[at, :], q * width, z * h_d)
            put(wd, sem_d, ad_hbm.at[at, :], q * width, d)
        half = dr - pr

        def put_down(p, r, s_, z_):
            at = 2 * width
            put(wd, sem_d, p.at[r : r + pr, at : at + h_d], s_ * dr, z_ * h_d)
            put(wd, sem_d, p.at[r : r + half, at + h_d :], s_ * dr + pr, z_ * h_d)
            put(wd, sem_d, p.at[r + half : r + pr, at + h_d :], s_ * dr + pr, z_ * h_d + width - h_d)

        pieces_to(put_down)
        put(nzg, sem_n, n2_hbm, 0, 0)
        put(nzg, sem_n, zgu_hbm.at[:, :c], 0, d)
        put(nzu, sem_n, n2_hbm, 0, 0)
        put(nzu, sem_n, zgu_hbm.at[:, c:], 0, d)
        mine = pl.ds(part * width, width)
        put(wgu, sem_g, gs_ref.at[:, mine], 0, z * width)
        put(wgu, sem_g, us_ref.at[:, mine], 0, fp + z * width)
        for q in range(4):
            at = pl.ds(q * quarter + part * width, width)
            put(wgu, sem_g, bg_hbm.at[:, at], d, q * width)
            put(wgu, sem_g, bu_hbm.at[:, at], d, fp + q * width)

        def put_up(p, r, s_, z_):
            put(wgu, sem_g, p.at[r : r + pr, :width], s_ * pr, z_ * width)
            put(wgu, sem_g, p.at[r : r + pr, width : 2 * width], s_ * pr, fp + z_ * width)

        pieces_to(put_up)
        if joins:
            load_earlier = pltpu.make_async_copy(earlier_ref, grads_ref.at[:, :, :3], sem_b)
            load_earlier.start()
        loads = [pltpu.make_async_copy(a, b, sem_s.at[k]) for k, (a, b) in enumerate(zip(state_in, state))]
        stores = [pltpu.make_async_copy(a, b, sem_s.at[4 + k]) for k, (a, b) in enumerate(zip(state, state_out))]
        for load in loads:
            load.start()

        pltpu.make_async_copy(dyz, dyz, sem_y).wait()
        dzd_t = dyz[:, d:].T
        pltpu.make_async_copy(wd, wd, sem_d).wait()

        def down(j):
            da_all[:, col(j)] = nt(dyz[...], wd[col(j), :])

        loop(fp // BN, down)
        pltpu.make_async_copy(nzg, nzg, sem_n).wait()
        pltpu.make_async_copy(nzu, nzu, sem_n).wait()
        pltpu.make_async_copy(wgu, wgu, sem_g).wait()
        zg_t = nzg[:, d:].T
        zu_t = nzu[:, d:].T
        blocks = fp // BN

        def up_col(j):
            return pl.ds(pl.multiple_of(fp + j * BN, BN), BN)

        def point(j):
            for i in range(2):
                rr = slice(i * half_rows, (i + 1) * half_rows)
                g = nn(nzg[rr, :], wgu[:, col(j)])
                u = nn(nzu[rr, :], wgu[:, up_col(j)])
                da = da_all[rr, col(j)]
                sg = jax.nn.sigmoid(g)
                gs = g * sg
                act[rr, col(j)] = (gs * u).astype(bf16)
                dgu[rr, up_col(j)] = (da * gs).astype(bf16)
                dgu[rr, col(j)] = (da * u * (sg + gs * (1.0 - sg))).astype(bf16)

        def weight_grads(j):
            g_all[0, :, col(j)] = nn(zg_t, dgu[:, col(j)])
            g_all[1, :, col(j)] = nn(zu_t, dgu[:, up_col(j)])
            g_all[2, :, col(j)] = nn(dzd_t, act[:, col(j)])

        point(0)

        def both(j):
            point(j + 1)
            weight_grads(j)

        loop(blocks - 1, both)
        weight_grads(blocks - 1)
        for k in range(3):
            for q in range(4):
                v = g_all[k, :, q * width : (q + 1) * width]
                grads_ref[:, q, 3 * n_join + k] = v.reshape(dps, c // dps, width).astype(bf16)
        if joins:
            load_earlier.wait()
        store_grads = pltpu.make_async_copy(grads_ref, grads_out, sem_o)
        store_grads.start()
        for load in loads:
            load.wait()
        zd = nn(act[...], wd[:, d:])
        dzg = nt(dgu[:, :fp], wgu[d:, :fp])
        dzu = nt(dgu[:, fp:], wgu[d:, fp:])
        if first:
            dz_ref[:, :c] = dzg
            dz_ref[:, c:] = dzu
            zd_ref[...] = zd
        else:
            dz_ref[:, :c] += dzg
            dz_ref[:, c:] += dzu
            zd_ref[...] += zd
        stores[2].start()
        stores[3].start()

        def out_block(j):
            acc_ref[:, col(j)] = (acc_ref[:, col(j)].astype(f32) + nn(act[...], wd[:, col(j)])).astype(bf16)

        loop(d // BN, out_block)
        stores[0].start()

        def dn_block(j):
            v = nt(dgu[...], wgu[col(j), :])
            dn_ref[:, col(j)] = (v if first else dn_ref[:, col(j)].astype(f32) + v).astype(bf16)

        loop(d // BN, dn_block)
        stores[1].start()
        store_grads.wait()
        for store in stores:
            store.wait()

    state_shapes = [((rows, d), bf16), ((rows, d), bf16), ((rows, 2 * c), f32), ((rows, c), f32)]
    grads_shape = (dps, 4, 3 * (1 + n_join), c // dps, width)
    n_any = n_pieces + 10 + n_join + n_state
    return pl.pallas_call(
        kernel,
        name=f"ffn{part}",
        out_shape=[sds(*v) for v in state_shapes] + [sds(grads_shape, bf16)],
        in_specs=[smem_spec()] + [any_spec()] * n_any,
        out_specs=[any_spec()] * 5,
        scratch_shapes=[pltpu.VMEM(*v) for v in state_shapes] + [
            pltpu.VMEM(grads_shape, bf16),
            pltpu.VMEM((d + c, 2 * fp), bf16), pltpu.VMEM((fp, d + c), bf16),
            pltpu.VMEM((rows, d + c), bf16), pltpu.VMEM((rows, d + c), bf16), pltpu.VMEM((rows, d + c), bf16),
            pltpu.VMEM((rows, fp), bf16), pltpu.VMEM((rows, 2 * fp), bf16), pltpu.VMEM((rows, fp), f32),
            pltpu.VMEM((3, c, fp), f32),
            pltpu.SemaphoreType.DMA((14,)),
        ],
        compiler_params=params(),
        cost_estimate=cost(2.6 * rows * d * 6 * fp),
    )(ids, *pieces, gate_shard, up_shard, down_shard, b_gate, b_up, a_down, n2, dy, zgu, dzd,
      *([earlier] if joins else []), *state)


def norm_back_rows(v, gain, dn):
    r = lax.rsqrt(jnp.mean(v * v, axis=-1, keepdims=True) + eps_norm)
    scaled = gain * dn
    return r * scaled - v * (r * r * r * jnp.mean(v * scaled, axis=-1, keepdims=True))


def spread(ref, at, v):
    dps, c = ref.shape[0], v.shape[0]
    n = v.shape[1] // 4
    for q in range(4):
        ref[:, q, :, at : at + n] = v[:, q * n : (q + 1) * n].reshape(dps, c // dps, n).astype(bf16)


def middle_call(acc, dn, dz_acc, zd_acc, h, n2, dy, y, zout, sel2, gain2, b_down, a_gate, a_up, b_out):
    rows, d = h.shape
    c = zout.shape[1]
    blocks = d // BN
    dps = lax.axis_size("dp")

    def kernel(dn_hbm, n2_hbm, dy_hbm, h_hbm, y_hbm, acc_hbm, dz_in, zd_in, zout_ref, sel_ref, g2_ref,
               b_down_ref, a_gate_ref, a_up_ref, b_out_ref, res_out, dhb_out, dzo, ga_ref,
               dn_ref, n2_ref, dy_ref, h_ref, y_ref, acc_ref, dh_ref, dhb, dzgu, zd, sems):
        wait_dn, wait_n2, wait_dy, wait_h, wait_y, wait_acc = fetched(
            [(dn_hbm, dn_ref), (n2_hbm, n2_ref), (dy_hbm, dy_ref), (h_hbm, h_ref), (y_hbm, y_ref), (acc_hbm, acc_ref)],
            sems,
        )
        sel = sel_ref[...]
        sel_f = sel.astype(f32)
        zd[...] = zd_in[...].astype(bf16) * sel
        dzgu[:, :c] = (dz_in[:, :c] * sel_f).astype(bf16)
        dzgu[:, c:] = (dz_in[:, c:] * sel_f).astype(bf16)
        wait_dn()

        def dns(j):
            v = nt(dzgu[:, :c], a_gate_ref[col(j), :]) + nt(dzgu[:, c:], a_up_ref[col(j), :])
            dh_ref[:, col(j)] = dn_ref[:, col(j)].astype(f32) + v

        loop(blocks, dns)
        wait_n2()
        g = nn(dzgu[...].T, n2_ref[...])
        spread(ga_ref, 2 * (d // 4), g[:c])
        spread(ga_ref, 3 * (d // 4), g[c:])
        wait_dy()
        wait_h()
        g2 = g2_ref[...]

        def norm2(i):
            v = dy_ref[row(i), :].astype(f32) + norm_back_rows(h_ref[row(i), :].astype(f32), g2, dh_ref[row(i), :])
            dhb[row(i), :] = v.astype(bf16)

        loop(rows // ROWS, norm2)
        store_dhb = pltpu.make_async_copy(dhb, dhb_out, sems.at[6])
        store_dhb.start()
        wait_acc()

        def results(j):
            v = acc_ref[:, col(j)].astype(f32) + nn(zd[...], b_down_ref[:, col(j)])
            acc_ref[:, col(j)] = v.astype(bf16)

        loop(blocks, results)
        store_res = pltpu.make_async_copy(acc_ref, res_out, sems.at[7])
        store_res.start()
        spread(ga_ref, d // 4, nn(zd[...].T, dy_ref[...]))
        dzo[...] = (nt(dhb[...], b_out_ref[...]) * sel_f).astype(bf16)
        spread(ga_ref, 0, nn(zout_ref[...].T, dhb[...]))
        wait_y()
        spread(ga_ref, 4 * (d // 4), nn(dzo[...].T, y_ref[...]))
        store_dhb.wait()
        store_res.wait()

    wide = pltpu.VMEM((rows, d), bf16)
    return pl.pallas_call(
        kernel,
        name="middle",
        out_shape=[
            sds((rows, d), bf16), sds((rows, d), bf16), sds((rows, c), bf16),
            sds((dps, 4, c // dps, 5 * (d // 4)), bf16),
        ],
        in_specs=[any_spec()] * 6 + [vmem_spec()] * 9,
        out_specs=[any_spec()] * 2 + [vmem_spec()] * 2,
        scratch_shapes=[
            *[wide] * 6, pltpu.VMEM((rows, d), f32), wide, pltpu.VMEM((rows, 2 * c), bf16),
            pltpu.VMEM((rows, c), bf16), pltpu.SemaphoreType.DMA((8,)),
        ],
        compiler_params=params(),
        cost_estimate=cost(2 * rows * d * 4 * d),
    )(dn, n2, dy, h, y, acc, dz_acc, zd_acc, zout, sel2, gain2, b_down, a_gate, a_up, b_out)


def back_call(dhb, dzo, mix, cv, zin, n1, sel2, m1, m2, taps, a_out, b_in, w_out):
    rows, d = dhb.shape
    c = zin.shape[1]
    blocks = d // BN
    dps = lax.axis_size("dp")

    def kernel(w_out_hbm, dhb_hbm, cv_hbm, mix_hbm, n1_hbm, dzo, zin_ref, sel_ref, m1_ref, m2_ref, taps_ref,
               a_out_ref, b_in_ref, dp_out, dzi_ref, gi_ref, w_out_ref, dhb, cv_ref, mix_ref, n1_ref, dp_ref, sems):
        wait_w, wait_dhb, wait_cv, wait_mix, wait_n1 = fetched(
            [(w_out_hbm, w_out_ref), (dhb_hbm, dhb), (cv_hbm, cv_ref), (mix_hbm, mix_ref), (n1_hbm, n1_ref)], sems
        )
        sel_f = sel_ref[...].astype(f32)
        m1 = m1_ref[...]
        m2 = m2_ref[...]
        wait_w()
        wait_dhb()
        wait_cv()
        wait_mix()

        def conv(j):
            dyc = nt(dhb[...], w_out_ref[col(j), :]) + nt(dzo[...], a_out_ref[col(j), :])
            dp_ref[:, col(blocks + j)] = (dyc * cv_ref[:, col(j)].astype(f32)).astype(bf16)
            dcv = dyc * mix_ref[:, col(blocks + j)].astype(f32)
            dbx = (
                taps_ref[2:3, col(j)] * dcv
                + taps_ref[1:2, col(j)] * pltpu.roll(dcv * m1, rows - 1, 0)
                + taps_ref[0:1, col(j)] * pltpu.roll(dcv * m2, rows - 2, 0)
            )
            dp_ref[:, col(j)] = (dbx * mix_ref[:, col(2 * blocks + j)].astype(f32)).astype(bf16)
            dp_ref[:, col(2 * blocks + j)] = (dbx * mix_ref[:, col(j)].astype(f32)).astype(bf16)

        loop(blocks, conv)
        store = pltpu.make_async_copy(dp_ref, dp_out, sems.at[5])
        store.start()
        dzi_ref[...] = (nt(dp_ref[...], b_in_ref[...]) * sel_f).astype(bf16)
        spread(gi_ref, 0, nn(zin_ref[...].T, dp_ref[...]))
        wait_n1()
        spread(gi_ref, 3 * (d // 4), nn(dzi_ref[...].T, n1_ref[...]))
        store.wait()

    wide, long = pltpu.VMEM((rows, d), bf16), pltpu.VMEM((rows, 3 * d), bf16)
    return pl.pallas_call(
        kernel,
        name="back",
        out_shape=[
            sds((rows, 3 * d), bf16), sds((rows, c), bf16), sds((dps, 4, c // dps, d), bf16),
        ],
        in_specs=[any_spec()] * 5 + [vmem_spec()] * 8,
        out_specs=[any_spec()] + [vmem_spec()] * 2,
        scratch_shapes=[pltpu.VMEM((d, d), bf16), wide, wide, long, wide, long, pltpu.SemaphoreType.DMA((6,))],
        compiler_params=params(),
        cost_estimate=cost(2 * rows * d * 4 * d),
    )(w_out, dhb, cv, mix, n1, dzo, zin, sel2, m1, m2, taps, a_out, b_in)


def last_call(dp, dzi, dh, x, gain1, a_in, w_in):
    rows, d = x.shape
    parts = 4

    def kernel(dp_hbm, w_in_hbm, dh_hbm, x_hbm, dzi_ref, g1_ref, a_in_ref, out_hbm, dp_ref, w_in_ref, dh_ref, x_ref,
               dn_ref, sems):
        n = d // parts
        wait_dp, *wait_w, wait_dh, wait_x = fetched(
            [(dp_hbm, dp_ref)]
            + [(w_in_hbm.at[k * n : (k + 1) * n], w_in_ref.at[k * n : (k + 1) * n]) for k in range(parts)]
            + [(dh_hbm, dh_ref), (x_hbm, x_ref)],
            sems,
        )
        wait_dp()
        for wait in wait_w:
            wait()

        def dns(j):
            dn_ref[:, col(j)] = nt(dp_ref[...], w_in_ref[col(j), :]) + nt(dzi_ref[...], a_in_ref[col(j), :])

        loop(d // BN, dns)
        g1 = g1_ref[...]
        wait_dh()
        wait_x()

        def norm1(i):
            v = dh_ref[row(i), :].astype(f32) + norm_back_rows(x_ref[row(i), :].astype(f32), g1, dn_ref[row(i), :])
            dh_ref[row(i), :] = v.astype(bf16)
            pltpu.make_async_copy(dh_ref.at[row(i)], out_hbm.at[row(i)], sems.at[parts + 3]).start()

        loop(rows // ROWS, norm1)
        pltpu.make_async_copy(dh_ref, out_hbm, sems.at[parts + 3]).wait()

    return pl.pallas_call(
        kernel,
        name="last",
        out_shape=sds((rows, d), bf16),
        in_specs=[any_spec()] * 4 + [vmem_spec()] * 3,
        out_specs=any_spec(),
        scratch_shapes=[
            pltpu.VMEM((rows, 3 * d), bf16), pltpu.VMEM((d, 3 * d), bf16), pltpu.VMEM((rows, d), bf16),
            pltpu.VMEM((rows, d), bf16), pltpu.VMEM((rows, d), f32), pltpu.SemaphoreType.DMA((parts + 4,)),
        ],
        compiler_params=params(),
        cost_estimate=cost(2 * rows * d * 4 * d),
    )(dp, w_in, dh, x, dzi, gain1, a_in)


def core_copies(arrays):
    return [swap_dp(a, CORE_BIT) for a in arrays]


def near(zs):
    return [swap_dp(zs, X_BIT), swap_dp(zs, Y_BIT), swap_dp(zs, X_BIT | Y_BIT)]


def far(xs, ys, relay):
    cut = xs.shape[0] // 3 * relay
    return [swap_dp(xs[:cut], Y_BIT), swap_dp(ys[cut:], X_BIT)]


def near_shares(values):
    return [values, *near(values)]


def all_shares(shares):
    return [*shares, *core_copies(shares)]


def finish_call(ids, shares, layout):
    masks = [m for m, _ in piece_table()]
    n = len(shares)
    r = shares[0].shape[-2]
    c = r * n
    widths = [sum(w for _, _, w in parts) for parts, _ in layout]

    def kernel(*refs):
        ids_ref, ins, outs, bufs = refs[0], refs[1 : 1 + n], refs[1 + n : 1 + n + len(layout)], refs[1 + n + len(layout) :]
        s = ids_ref[0]
        for k, (parts, flip) in enumerate(layout):
            target = bufs[k] if flip else outs[k]
            for share, mask in zip(ins, masks):
                at = pl.ds(pl.multiple_of((s ^ mask) * r, r), r)
                to = 0
                for lead, start, w in parts:
                    v = share[:, start : start + w] if lead is None else share[lead, :, start : start + w]
                    target[at, to : to + w] = v.astype(f32)
                    to += w
            if flip:
                outs[k][...] = bufs[k][...].T

    return pl.pallas_call(
        kernel,
        name="finish",
        out_shape=[sds((w, c) if flip else (c, w), f32) for w, (_, flip) in zip(widths, layout)],
        in_specs=[smem_spec()] + [vmem_spec()] * n,
        out_specs=[vmem_spec()] * len(layout),
        scratch_shapes=[pltpu.VMEM((c, w), f32) for w in widths],
        compiler_params=pltpu.CompilerParams(vmem_limit_bytes=16 * 2**20),
    )(ids, *shares)


def exchange(values, axis):
    flat = values.reshape(values.shape[0], -1, values.shape[-1])
    return lax.all_to_all(flat, axis, split_axis=0, concat_axis=0, tiled=True).reshape(values.shape)


def send_to_groups(sums):
    groups = lax.axis_size("group")
    out = [
        lax.ppermute(sums[t - 1], "group", [(i, (i + t) % groups) for i in range(groups)])
        for t in range(1, groups)
    ]
    return [*out, sums[-1]]


def add_up(parts):
    whole = parts[0].astype(f32)
    for p in parts[1:]:
        whole = whole + p.astype(f32)
    return whole.astype(bf16)


def local_pieces(
    tokens, cotangent, order, lengths, adapter_ids, norm_gain, ffn_gain, conv_weight,
    in_weight, out_weight, gate_weight, up_weight, down_weight,
    a_in, b_in, a_out, b_out, a_gate, b_gate, a_up, b_up, a_down, b_down,
):
    dp_count = lax.axis_size("dp")
    s = lax.axis_index("dp")
    z = lax.axis_index("group")
    ids = jnp.stack([s, z]).astype(jnp.int32)
    rows, d = tokens.shape
    order_row = order[0]
    counting = jnp.arange(dp_count, dtype=jnp.int32)
    inverse_row = jnp.sum(
        jnp.where(order_row[None, :] == counting[:, None], counting[None, :], 0), axis=1
    )
    width = gate_weight.shape[1] // PARTS
    packed = own_pieces(ids, in_weight, out_weight, gate_weight, up_weight, down_weight, dp_count)
    arrived = lax.all_to_all(cotangent, "dp", split_axis=0, concat_axis=0, tiled=True)
    io_width = in_weight.shape[1] + out_weight.shape[1]
    zs_io, *zs = from_planes(packed[0], [io_width, 3 * width])
    near_io = [swap_dp(zs_io, X_BIT), swap_dp(zs_io, Y_BIT)]
    near_io += far(*near_io, 1)
    zs += from_planes(after(packed[1], zs_io), [3 * width])
    io = [zs_io, *near_io]
    io = io + core_copies(io)
    dy = lax.all_to_all(
        picked(arrived, after(inverse_row, packed[0]), dp_count), "dp", split_axis=0, concat_axis=0,
        tiled=True,
    )

    sel, after_one, after_two = per_token_tables(
        lengths[:, 0, :][s], adapter_ids[:, 0, :][s], rows, a_in.shape[1], ADAPTER_RANK
    )
    sel2 = sel * adapter_scale
    gain1 = norm_gain[None, :]
    gain2 = ffn_gain[None, :]
    first = after(zs[0], dy, *near_io)
    nears = [swap_dp(first, X_BIT), swap_dp(first, Y_BIT)]
    n1, zin, mix, cv, y, w_in = front_call(
        after(ids, dy, zs[0]), io, 1, in_weight, tokens, gain1, conv_weight, sel2, after_one, after_two, a_in, b_in,
    )
    nears += far(*[after(v, zin) for v in nears], 2)
    groups = lax.axis_size("group")
    zs.append(others(ids, exchange(after(packed[2], zin).reshape(groups, -1, 3 * width), "group")))
    zout, h, n2, zgu, w_out = join_call(
        ids, io, 1, out_weight, y, tokens, gain2, sel2, a_out, b_out, a_gate, a_up,
    )
    dzd = (nt(dy, b_down) * sel2.astype(f32)).astype(bf16)
    state = (h,)
    previous = n2
    grads = []
    for j in range(PARTS):
        arrays = [zs[j], *[after(v, previous) for v in nears]]
        arrays = arrays + core_copies(arrays)
        if j + 1 < PARTS:
            nears = near(after(zs[j + 1], previous, *nears))
        if j == PARTS - 1:
            early = exchange(after(grads[-1], *arrays), "dp")
        *state, g = ffn_call(
            j, after(ids, *zs[j + 1 : j + 2]), arrays, 2 if j == 0 else None, gate_weight, up_weight,
            down_weight, n2, dy, zgu, dzd, b_gate, b_up, a_down, grads[0] if j == 1 else None, *state,
        )
        previous = state[2]
        grads.append(g)
    late = exchange(grads[-1], "dp")
    early_sums = totals_by_shift(ids, after(early, g))
    early = send_to_groups(early_sums)
    result, dhb, dzo, g_a = middle_call(
        *state, h, n2, dy, y, zout, sel2, after(gain2, early_sums[0]), b_down, a_gate, a_up, b_out
    )
    g_a = exchange(g_a, "dp")
    early = add_up([after(early[0], dzo), *early[1:]])
    late_sums = totals_by_shift(ids, after(late, dzo))
    late = send_to_groups(late_sums)
    dp, dzi, g_i = back_call(
        dhb, dzo, mix, cv, zin, n1, sel2, after_one, after_two, after(conv_weight, late_sums[0], early), a_out,
        b_in, w_out,
    )
    g_i = exchange(g_i, "dp")
    late = add_up([after(late[0], dzi), *late[1:]])
    ffn = near_shares(jnp.concatenate([early, late], axis=0))
    ga_sums = totals_by_shift(ids, after(g_a, dzi))
    g_a = send_to_groups(ga_sums)
    input_grad = last_call(dp, dzi, dhb, tokens, after(gain1, ga_sums[0]), a_in, w_in)
    gi_sums = totals_by_shift(ids, after(g_i, input_grad))
    g_i = send_to_groups(gi_sums)
    g_a = add_up([after(g_a[0], input_grad), *g_a[1:]])
    ffn = all_shares([after(v, input_grad) for v in ffn])
    q = d // lax.axis_size("group")
    layout = [([(3 * j + k, 0, width) for j in range(PARTS)], k == 2) for k in range(3)]
    g_gate_b, g_up_b, g_down_a = finish_call(after(ids, gi_sums[0]), ffn, layout)
    g_i = add_up(g_i)
    small = all_shares(near_shares(jnp.concatenate([g_a, g_i], axis=1)))
    layout = [([(None, k * q, q)], k >= 2) for k in range(5)]
    layout += [([(None, 5 * q, 3 * q)], False), ([(None, 8 * q, q)], True)]
    g_out_b, g_down_b, g_gate_a, g_up_a, g_out_a, g_in_b, g_in_a = finish_call(ids, small, layout)
    return (
        result, input_grad, g_in_a, g_in_b, g_out_a, g_out_b, g_gate_a, g_gate_b, g_up_a, g_up_b, g_down_a,
        g_down_b,
    )


def solution(mesh):
    in_specs = (
        P(("dp", "group"), None),
        P(("dp", "group"), None),
        P("group", None),
        P(None, "group", None),
        P(None, "group", None),
        P(),
        P(),
        P(),
        P(None, "group"),
        P(None, "group"),
        P(None, "group"),
        P(None, "group"),
        P(None, "group"),
        P(),
        P(),
        P(),
        P(),
        P(),
        P(),
        P(),
        P(),
        P(),
        P(),
    )
    out_specs = (
        P(("dp", "group"), None),
        P(("dp", "group"), None),
        P("group", None),
        P(None, "group"),
        P("group", None),
        P(None, "group"),
        P("group", None),
        P(None, "group"),
        P("group", None),
        P(None, "group"),
        P("group", None),
        P(None, "group"),
    )
    small = dict(mesh.shape) == {"dp": 8, "group": 4}
    return jax.shard_map(local_pieces if small else local, mesh=mesh, in_specs=in_specs, out_specs=out_specs, check_vma=False)
```

time: 481 us -> 411 us (0.85)
  Pallas kernels: 225 us -> 200 us
  between operations: 20.3 us -> 1.61 us
  local copies, waits for them, and re-layouts: 29 us -> 16.4 us
  other arithmetic: 14.2 us -> 3.11 us
  starting transfers between devices: 99.5 us -> 93.4 us
    ppermute x24 -> x18, waiting for transfers between devices: 54 us -> 24.2 us  [the longest x6 13.7 us: from_planes(): lax.ppermute(joined, 'group', [(i, (i + t) % groups) for i in range(group...]
    ppermute x24 -> x18, starting transfers between devices: 53.1 us -> 32.1 us  [the longest x12 18.7 us: send_to_groups(): lax.ppermute(sums[t - 1], 'group', [(i, (i + t) % groups) for i in range(...]
    ppermute x31 -> x46, waiting for transfers between devices: 27.9 us -> 47.2 us  [swap_dp(): lax.ppermute(values, 'dp', [(i, i ^ bit) for i in range(lax.axis_size('dp...]
    all_to_all x1, waiting for transfers between devices: 0.01 us -> 13.9 us  [local_pieces(): lax.all_to_all(cotangent, 'dp', split_axis=0, concat_axis=0, tiled=True)]
    pallas_call x4 -> x14, Pallas kernels: 166 us -> 153 us  [the longest x3 111 us: ffn_call(): pl.pallas_call(kernel, name=f'ffn{part}', out_shape=[sds(*v) for v in sta...]
    pallas_call x4 -> x3, Pallas kernels: 8.28 us -> 0.39 us  [stacked(): pl.pallas_call(kernel, name='stacked', out_shape=jax.ShapeDtypeStruct((le...]
    ppermute x31 -> x46, starting transfers between devices: 20.5 us -> 28.1 us  [swap_dp(): lax.ppermute(values, 'dp', [(i, i ^ bit) for i in range(lax.axis_size('dp...]
    concatenate x8 -> x2, other arithmetic: 7.34 us -> 0.03 us  [the longest x1 0.02 us: local_pieces(): ffn = near_shares(jnp.concatenate([early, late], axis=0))]
  transfers between devices with their start and end apart: 62 -> 71, of which waited for: 19 -> 27; matrix products, arithmetic and copies ran while one was open for 6% -> 3% of each run, Pallas kernels for 48% -> 49%
where the time goes in v3:
time: 411 us; the launch traced here: 404 us
  Pallas kernels  200 us (49%)
  starting transfers between devices  93.4 us (23%)
  waiting for transfers between devices  86.3 us (21%)
  local copies, waits for them, and re-layouts  16.4 us (4%)
    pallas_call x3, Pallas kernels, ffn_call(): pl.pallas_call(kernel, name=f'ffn{part}', out_shape=[sds(*v) for v in sta...  111 us
    ppermute x46, waiting for transfers between devices, swap_dp(): lax.ppermute(values, 'dp', [(i, i ^ bit) for i in range(lax.axis_size('dp...  47.2 us
    ppermute x46, starting transfers between devices, swap_dp(): lax.ppermute(values, 'dp', [(i, i ^ bit) for i in range(lax.axis_size('dp...  28.1 us
    all_to_all x5, starting transfers between devices, exchange(): lax.all_to_all(flat, axis, split_axis=0, concat_axis=0, tiled=True)  23.4 us
    ppermute x12, starting transfers between devices, send_to_groups(): lax.ppermute(sums[t - 1], 'group', [(i, (i + t) % groups) for i in range(...  18.7 us
    pallas_call x1, Pallas kernels, front_call(): pl.pallas_call(kernel, name='front', out_shape=[sds(wide[0], bf16), sds((...  17.5 us
    pallas_call x1, Pallas kernels, back_call(): pl.pallas_call(kernel, name='back', out_shape=[sds((rows, 3 * d), bf16),...  17.4 us
    pallas_call x1, Pallas kernels, last_call(): pl.pallas_call(kernel, name='last', out_shape=sds((rows, d), bf16), in_sp...  16 us
  transfers between devices with their start and end apart: 71, of which 27 were waited for; matrix products, arithmetic and copies ran while one was open for 3% of the time, Pallas kernels for 49%

profile of v3, /device:TPU:0, one launch (start us, length us, event | category | flops | bytes accessed | tf_op | source)
XLA Modules:
  0.0 403.5 jit_solution(3718563619364164872)
XLA Ops:
  0.7 5.4 %all-to-all-start = ((bf16[8,128,1024]{2,1,0:T(8,128)(2,1)}), bf16[8,128,1024]{2,1,0:T(8,128)(2,1)}, u32[]{:S(2)}, u32[]{:S(2)}) async-start(bf16[8,128,1024]{2,1,0:T(8,128)(2,1)} %bitcast.27), calls=%async_computation | async-start | bytes 4194304 | tf_op jit(solution)/shard_map/all_to_all | solution.py:1184
  12.6 2.3 collective-permute-start
  14.9 2.6 collective-permute-start.1
  19.0 13.9 %all-to-all-done = bf16[8,128,1024]{2,1,0:T(8,128)(2,1)} async-done(((bf16[8,128,1024]{2,1,0:T(8,128)(2,1)}), bf16[8,128,1024]{2,1,0:T(8,128)(2,1)}, u32[]{:S(2)}, u32[]{:S(2)}) %all-to-all-start) | async-done | bytes 2097184 | tf_op jit(solution)/shard_map/all_to_all | solution.py:1184
  32.9 3.4 picked.1
  36.2 4.4 %all-to-all-start.1 = ((bf16[8,128,1024]{2,1,0:T(8,128)(2,1)}), bf16[8,128,1024]{2,1,0:T(8,128)(2,1)}, u32[]{:S(2)}, u32[]{:S(2)}) async-start(bf16[8,128,1024]{2,1,0:T(8,128)(2,1)} %bitcast.5), calls=%async_computation.1 | async-start | bytes 4194304 | tf_op jit(solution)/shard_map/all_to_all | solution.py:1192
  40.6 13.7 %collective-permute-done.1.refs_1_ = bf16[128,2176]{1,0:T(8,128)(2,1)S(1)} collective-permute-done((bf16[128,2176]{1,0:T(8,128)(2,1)}, bf16[128,2176]{1,0:T(8,128)(2,1)S(1)}, u32[]{:S(2)}, u32[]{:S(2)}) %collective-permute-start.1) | collective-permute-done | bytes 557088 | tf_op jit(solution)/shard_map/ppermute | solution.py:435
  57.7 25.4 %collective-permute-done.4.refs_3_ = bf16[384,1024]{1,0:T(8,128)(2,1)S(1)} collective-permute-done((bf16[384,1024]{1,0:T(8,128)(2,1)S(1)}, bf16[384,1024]{1,0:T(8,128)(2,1)S(1)}, u32[]{:S(2)}, u32[]{:S(2)}) %collective-permute-start.4) | collective-permute-done | bytes 786464 | tf_op jit(solution)/shard_map/ppermute | solution.py:339
  85.5 7.2 %collective-permute-done.5.refs_4_ = bf16[128,1024]{1,0:T(8,128)(2,1)S(1)} collective-permute-done((bf16[128,1024]{1,0:T(8,128)(2,1)S(1)}, bf16[128,1024]{1,0:T(8,128)(2,1)S(1)}, u32[]{:S(2)}, u32[]{:S(2)}) %collective-permute-start.5) | collective-permute-done | bytes 262176 | tf_op jit(solution)/shard_map/ppermute | solution.py:339
  93.5 3.4 collective-permute-done.6.refs_5_
  103.7 3.8 collective-permute-start.12
  107.6 17.5 %front.1 = (bf16[1024,1024]{1,0:T(8,128)(2,1)}, bf16[1024,128]{1,0:T(8,128)(2,1)}, bf16[1024,3072]{1,0:T(8,128)(2,1)}, bf16[1024,1024]{1,0:T(8,128)(2,1)}, bf16[...) custom-call(s32[2]{0:T(128)} %copy-done.12, bf16[384,1024]{1,0:T(8,128)(2,1)} %copy-done.3, ...), custom_call_target="tpu_custom_call" | custom-call | flops 2044723 | tf_op jit(solution)/shard_map/front/pallas_call | solution.py:637
  134.1 12.4 %join.1 = (bf16[1024,128]{1,0:T(8,128)(2,1)}, bf16[1024,1024]{1,0:T(8,128)(2,1)}, bf16[1024,1024]{1,0:T(8,128)(2,1)}, bf16[1024,256]{1,0:T(8,128)(2,1)}, bf16[1024,1024]{1,0:T(8,128)(2,1)}) custom-call(s32[2]{0:T(128)} %copy-done.12, bf16[384,1024]{1,0:T(8,128)(2,1)} %copy-done.3, bf16[384,1024]{1,0:T(8,128)(2,1)} %copy-done.34, ...), custom_call_target="tpu_custom_call" | custom-call | flops 681574 | tf_op jit(solution)/shard_map/join/pallas_call | solution.py:691
  147.8 7.3 %all-to-all-start.2 = ((bf16[4,128,1152]{2,1,0:T(8,128)(2,1)}), bf16[4,128,1152]{2,1,0:T(8,128)(2,1)S(1)}, u32[]{:S(2)}, u32[]{:S(2)}) async-start(bf16[4,128,1152]{2,1,0:T(8,128)(2,1)} %bitcast.25), calls=%async_computation.2 | async-start | bytes 2359296 | tf_op jit(solution)/shard_map/all_to_all | solution.py:1148
  158.6 2.1 collective-permute-done.23.refs_10_
  162.5 3.0 fusion.refs_20_.refs_18_
  166.4 37.0 %ffn0.1 = (bf16[1024,1024]{1,0:T(8,128)(2,1)}, bf16[1024,1024]{1,0:T(8,128)(2,1)}, f32[1024,256]{1,0:T(8,128)}, f32[1024,128]{1,0:T(8,128)}, bf16[8,4,3,16,384]{4,3,2,1,0:T(8,128)(2,1)}) custom-call(s32[2]{0:T(128)} %copy-done.12, bf16[384,1152]{1,0:T(8,128)(2,1)} %copy-done.6, bf16[384,1152]{1,0:T(8,128)(2,1)} %collective-permute-done.15.refs_2_, ...), custom_call_target="tpu_custom_call" | custom-call | flops 6134169 | tf_op jit(solution)/shard_map/ffn0/pallas_call | solution.py:880
  209.0 37.2 %ffn1.1 = (bf16[1024,1024]{1,0:T(8,128)(2,1)}, bf16[1024,1024]{1,0:T(8,128)(2,1)}, f32[1024,256]{1,0:T(8,128)}, f32[1024,128]{1,0:T(8,128)}, bf16[8,4,6,16,384]{4,3,2,1,0:T(8,128)(2,1)}) custom-call(s32[2]{0:T(128)} %copy-done.12, bf16[384,1152]{1,0:T(8,128)(2,1)} %copy-done.5, bf16[384,1152]{1,0:T(8,128)(2,1)} %collective-permute-done.24.refs_2_, ...), custom_call_target="tpu_custom_call" | custom-call | flops 6134169 | tf_op jit(solution)/shard_map/ffn1/pallas_call | solution.py:880
  252.3 4.1 %all-to-all-start.3 = ((bf16[8,384,384]{2,1,0:T(8,128)(2,1)}), bf16[8,384,384]{2,1,0:T(8,128)(2,1)S(1)}, u32[]{:S(2)}, u32[]{:S(2)}) async-start(bf16[8,384,384]{2,1,0:T(8,128)(2,1)} %bitcast.26), calls=%async_computation.3 | async-start | bytes 4718592 | tf_op jit(solution)/shard_map/all_to_all | solution.py:1148
  256.4 37.1 %ffn2.1 = (bf16[1024,1024]{1,0:T(8,128)(2,1)}, bf16[1024,1024]{1,0:T(8,128)(2,1)}, f32[1024,256]{1,0:T(8,128)}, f32[1024,128]{1,0:T(8,128)}, bf16[8,4,3,16,384]{4,3,2,1,0:T(8,128)(2,1)}) custom-call(s32[2]{0:T(128)} %copy-done.12, bf16[384,1152]{1,0:T(8,128)(2,1)} %copy-done.7, bf16[384,1152]{1,0:T(8,128)(2,1)} %copy-done.40, bf16[384,1152]{1,0:T(8,128)(2,1)} %copy-done.39, ...), custom_call_target="tpu_custom_call" | custom-call | flops 6134169 | tf_op jit(solution)/shard_map/ffn2/pallas_call | solution.py:880
  293.5 4.4 %all-to-all-start.4 = ((bf16[8,192,384]{2,1,0:T(8,128)(2,1)}), bf16[8,192,384]{2,1,0:T(8,128)(2,1)S(1)}, u32[]{:S(2)}, u32[]{:S(2)}) async-start(bf16[8,192,384]{2,1,0:T(8,128)(2,1)} %bitcast.29), calls=%async_computation.4 | async-start | bytes 2359296 | tf_op jit(solution)/shard_map/all_to_all | solution.py:1148
  301.3 12.4 %middle.1 = (bf16[1024,1024]{1,0:T(8,128)(2,1)}, bf16[1024,1024]{1,0:T(8,128)(2,1)}, bf16[1024,128]{1,0:T(8,128)(2,1)}, bf16[8,4,16,1280]{3,2,1,0:T(8,128)(2,1)}) custom-call(bf16[1024,1024]{1,0:T(8,128)(2,1)} %get-tuple-element.149.dn_hbm, bf16[1024,1024]{1,0:T(8,128)(2,1)} %get-tuple-element.122.refs_17_.refs_15_.n2_hbm, ...), custom_call_target="tpu_custom_call" | custom-call | flops 2097152 | tf_op jit(solution)/shard_map/middle/pallas_call | solution.py:971
  314.6 3.6 all-to-all-start.5
  320.3 2.4 collective-permute-start.39
  325.1 3.1 collective-permute-done.39
  328.4 17.4 %back.1 = (bf16[1024,3072]{1,0:T(8,128)(2,1)}, bf16[1024,128]{1,0:T(8,128)(2,1)}, bf16[8,4,16,1024]{3,2,1,0:T(8,128)(2,1)}) custom-call(bf16[1024,1024]{1,0:T(8,128)(2,1)} %get-tuple-element.161.w_out_hbm, bf16[1024,1024]{1,0:T(8,128)(2,1)} %get-tuple-element.162.dhb_hbm.dh_hbm, bf16[1024,1024]{1,0:T(8,128)(2,1)} %get-tuple-element.163.cv_hbm, ...), custom_call_target="tpu_custom_call" | custom-call | flops 2097152 | tf_op jit(solution)/shard_map/back/pallas_call | solution.py:1030
  345.9 4.0 all-to-all-start.6
  357.7 2.8 collective-permute-start.59
  362.0 16.0 %last.1 = bf16[1024,1024]{1,0:T(8,128)(2,1)} custom-call(bf16[1024,3072]{1,0:T(8,128)(2,1)} %get-tuple-element.174.dp_hbm, bf16[1024,3072]{1,0:T(8,128)(2,1)} %get-tuple-element.175.w_in_hbm, bf16[1024,1024]{1,0:T(8,128)(2,1)} %get-tuple-element.162.dhb_hbm.dh_hbm, bf16[1024,1024]{1,0:T(8,128)(2,1)} %x_hbm.1, bf16[1024,128]{1,0:T(8,128)(2,1)} %get-tuple-element.176.dzi_ref, ...), custom_call_target="tpu_custom_call" | custom-call | flops 2097152 | tf_op jit(solution)/shard_map/last/pallas_call | solution.py:1077
  379.7 2.1 collective-permute-start.45
  388.7 2.2 collective-permute-done.42
  397.6 2.2 collective-permute-done.49.refs_4_
  (252 shorter events, 86.1 us)
Async XLA Ops:
  0.7 32.2 %all-to-all-start = ((bf16[8,128,1024]{2,1,0:T(8,128)(2,1)}), bf16[8,128,1024]{2,1,0:T(8,128)(2,1)}, u32[]{:S(2)}, u32[]{:S(2)}) async-start(bf16[8,128,1024]{2,1,0:T(8,128)(2,1)} %bitcast.27), calls=%async_computation | async-start | bytes 4194304 | tf_op jit(solution)/shard_map/all_to_all | solution.py:1184
  12.6 28.0 %collective-permute-start = (bf16[128,2176]{1,0:T(8,128)(2,1)}, bf16[128,2176]{1,0:T(8,128)(2,1)S(1)}, u32[]{:S(2)}, u32[]{:S(2)}) collective-permute-start(bf16[128,2176]{1,0:T(8,128)(2,1)} %get-tuple-element.112), channel_id=1, source_target_pairs={{0,1},{1,2},{2,3},{3,0},{4,5},{5,6},{6,7},{7,4},{8,9},{9,10},{10,1... | collective-permute-start | bytes 1671176 | tf_op jit(solution)/shard_map/ppermute | solution.py:435
  14.9 39.4 %collective-permute-start.1 = (bf16[128,2176]{1,0:T(8,128)(2,1)}, bf16[128,2176]{1,0:T(8,128)(2,1)S(1)}, u32[]{:S(2)}, u32[]{:S(2)}) collective-permute-start(bf16[128,2176]{1,0:T(8,128)(2,1)} %get-tuple-element.112), channel_id=1, source_target_pairs={{0,2},{1,3},{2,0},{3,1},{4,6},{5,7},{6,4},{7,5},{8,10},{9,11},{10,... | collective-permute-start | bytes 1671176 | tf_op jit(solution)/shard_map/ppermute | solution.py:435
  17.5 36.8 %collective-permute-start.2 = (bf16[128,2176]{1,0:T(8,128)(2,1)}, bf16[128,2176]{1,0:T(8,128)(2,1)S(1)}, u32[]{:S(2)}, u32[]{:S(2)}) collective-permute-start(bf16[128,2176]{1,0:T(8,128)(2,1)} %get-tuple-element.112), channel_id=1, source_target_pairs={{0,3},{1,0},{2,1},{3,2},{4,7},{5,4},{6,5},{7,6},{8,11},{9,8},{10,9... | collective-permute-start | bytes 1671176 | tf_op jit(solution)/shard_map/ppermute | solution.py:435
  36.2 60.7 %all-to-all-start.1 = ((bf16[8,128,1024]{2,1,0:T(8,128)(2,1)}), bf16[8,128,1024]{2,1,0:T(8,128)(2,1)}, u32[]{:S(2)}, u32[]{:S(2)}) async-start(bf16[8,128,1024]{2,1,0:T(8,128)(2,1)} %bitcast.5), calls=%async_computation.1 | async-start | bytes 4194304 | tf_op jit(solution)/shard_map/all_to_all | solution.py:1192
  54.4 28.6 %collective-permute-start.4 = (bf16[384,1024]{1,0:T(8,128)(2,1)S(1)}, bf16[384,1024]{1,0:T(8,128)(2,1)S(1)}, u32[]{:S(2)}, u32[]{:S(2)}) collective-permute-start(bf16[384,1024]{1,0:T(8,128)(2,1)S(1)} %stacked.4.refs_1_), channel_id=1, source_target_pairs={{0,16},{4,20},{8,24},{12,28},{16,0},{20,4},{24,8},{28,12},{1,17},{... | collective-permute-start | bytes 2359304 | tf_op jit(solution)/shard_map/ppermute | solution.py:339
  56.2 28.4 %collective-permute-start.3 = (bf16[384,1024]{1,0:T(8,128)(2,1)S(1)}, bf16[384,1024]{1,0:T(8,128)(2,1)S(1)}, u32[]{:S(2)}, u32[]{:S(2)}) collective-permute-start(bf16[384,1024]{1,0:T(8,128)(2,1)S(1)} %stacked.4.refs_1_), channel_id=1, source_target_pairs={{0,8},{4,12},{8,0},{12,4},{16,24},{20,28},{24,16},{28,20},{1,9},{5... | collective-permute-start | bytes 2359304 | tf_op jit(solution)/shard_map/ppermute | solution.py:339
  57.7 41.9 %collective-permute-start.7 = (bf16[384,1024]{1,0:T(8,128)(2,1)S(1)}, bf16[384,1024]{1,0:T(8,128)(2,1)}, u32[]{:S(2)}, u32[]{:S(2)}) collective-permute-start(bf16[384,1024]{1,0:T(8,128)(2,1)S(1)} %stacked.4.refs_1_), channel_id=1, source_target_pairs={{0,4},{4,0},{8,12},{12,8},{16,20},{20,16},{24,28},{28,24},{1,5},{5... | collective-permute-start | bytes 2359304 | tf_op jit(solution)/shard_map/ppermute | solution.py:339
  96.9 28.2 %collective-permute-start.15 = (bf16[384,1152]{1,0:T(8,128)(2,1)S(1)}, bf16[384,1152]{1,0:T(8,128)(2,1)}, u32[]{:S(2)}, u32[]{:S(2)}) collective-permute-start(bf16[384,1152]{1,0:T(8,128)(2,1)S(1)} %stacked.3.refs_1_), channel_id=1, source_target_pairs={{0,8},{4,12},{8,0},{12,4},{16,24},{20,28},{24,16},{28,20},{1,9},{5... | collective-permute-start | bytes 2654216 | tf_op jit(solution)/shard_map/ppermute | solution.py:339
  99.6 29.6 %collective-permute-start.16 = (bf16[384,1152]{1,0:T(8,128)(2,1)S(1)}, bf16[384,1152]{1,0:T(8,128)(2,1)}, u32[]{:S(2)}, u32[]{:S(2)}) collective-permute-start(bf16[384,1152]{1,0:T(8,128)(2,1)S(1)} %stacked.3.refs_1_), channel_id=1, source_target_pairs={{0,16},{4,20},{8,24},{12,28},{16,0},{20,4},{24,8},{28,12},{1,17},{... | collective-permute-start | bytes 2654216 | tf_op jit(solution)/shard_map/ppermute | solution.py:339
  103.7 28.8 %collective-permute-start.12 = (bf16[128,1152]{1,0:T(8,128)(2,1)}, bf16[128,1152]{1,0:T(8,128)(2,1)S(1)}, u32[]{:S(2)}, u32[]{:S(2)}) collective-permute-start(bf16[128,1152]{1,0:T(8,128)(2,1)} %copy-done.19), channel_id=1, source_target_pairs={{0,1},{1,2},{2,3},{3,0},{4,5},{5,6},{6,7},{7,4},{8,9},{9,10},{10,1... | collective-permute-start | bytes 884744 | tf_op jit(solution)/shard_map/ppermute | solution.py:435
  127.1 29.2 %collective-permute-start.17 = (bf16[256,1152]{1,0:T(8,128)(2,1)}, bf16[256,1152]{1,0:T(8,128)(2,1)}, u32[]{:S(2)}, u32[]{:S(2)}) collective-permute-start(bf16[256,1152]{1,0:T(8,128)(2,1)} %slice.14), channel_id=1, source_target_pairs={{0,16},{4,20},{8,24},{12,28},{16,0},{20,4},{24,8},{28,12},{1,17},{... | collective-permute-start | bytes 1769480 | tf_op jit(solution)/shard_map/ppermute | solution.py:339
  127.6 30.5 %collective-permute-start.19 = (bf16[384,1152]{1,0:T(8,128)(2,1)S(1)}, bf16[384,1152]{1,0:T(8,128)(2,1)}, u32[]{:S(2)}, u32[]{:S(2)}) collective-permute-start(bf16[384,1152]{1,0:T(8,128)(2,1)S(1)} %stacked.3.refs_1_), channel_id=1, source_target_pairs={{0,4},{4,0},{8,12},{12,8},{16,20},{20,16},{24,28},{28,24},{1,5},{5... | collective-permute-start | bytes 2654216 | tf_op jit(solution)/shard_map/ppermute | solution.py:339
  127.6 18.8 %collective-permute-start.13 = (bf16[128,1152]{1,0:T(8,128)(2,1)S(1)}, bf16[128,1152]{1,0:T(8,128)(2,1)S(1)}, u32[]{:S(2)}, u32[]{:S(2)}) collective-permute-start(bf16[128,1152]{1,0:T(8,128)(2,1)S(1)} %copy-done.20), channel_id=1, source_target_pairs={{0,2},{1,3},{2,0},{3,1},{4,6},{5,7},{6,4},{7,5},{8,10},{9,11},{10,... | collective-permute-start | bytes 884744 | tf_op jit(solution)/shard_map/ppermute | solution.py:435
  132.6 23.7 %collective-permute-start.18 = (bf16[128,1152]{1,0:T(8,128)(2,1)}, bf16[128,1152]{1,0:T(8,128)(2,1)}, u32[]{:S(2)}, u32[]{:S(2)}) collective-permute-start(bf16[128,1152]{1,0:T(8,128)(2,1)} %slice.15), channel_id=1, source_target_pairs={{0,8},{4,12},{8,0},{12,4},{16,24},{20,28},{24,16},{28,20},{1,9},{5... | collective-permute-start | bytes 884744 | tf_op jit(solution)/shard_map/ppermute | solution.py:339
  147.3 18.3 %collective-permute-start.20 = (bf16[384,1152]{1,0:T(8,128)(2,1)}, bf16[384,1152]{1,0:T(8,128)(2,1)}, u32[]{:S(2)}, u32[]{:S(2)}) collective-permute-start(bf16[384,1152]{1,0:T(8,128)(2,1)} %collective-permute-done.15.refs_2_), channel_id=1, source_target_pairs={{0,4},{4,0},{8,12},{12,8},{16,20},{20,16},{24,28},{28,24},{1,5},{5... | collective-permute-start | bytes 2654216 | tf_op jit(solution)/shard_map/ppermute | solution.py:339
  147.8 56.8 %all-to-all-start.2 = ((bf16[4,128,1152]{2,1,0:T(8,128)(2,1)}), bf16[4,128,1152]{2,1,0:T(8,128)(2,1)S(1)}, u32[]{:S(2)}, u32[]{:S(2)}) async-start(bf16[4,128,1152]{2,1,0:T(8,128)(2,1)} %bitcast.25), calls=%async_computation.2 | async-start | bytes 2359296 | tf_op jit(solution)/shard_map/all_to_all | solution.py:1148
  156.3 47.1 %collective-permute-start.26 = (bf16[384,1152]{1,0:T(8,128)(2,1)S(1)}, bf16[384,1152]{1,0:T(8,128)(2,1)}, u32[]{:S(2)}, u32[]{:S(2)}) collective-permute-start(bf16[384,1152]{1,0:T(8,128)(2,1)S(1)} %stacked.5.refs_1_), channel_id=1, source_target_pairs={{0,24},{4,28},{8,16},{12,20},{16,8},{20,12},{24,0},{28,4},{1,25},{... | collective-permute-start | bytes 2654216 | tf_op jit(solution)/shard_map/ppermute | solution.py:339
  160.7 43.3 %collective-permute-start.25 = (bf16[384,1152]{1,0:T(8,128)(2,1)S(1)}, bf16[384,1152]{1,0:T(8,128)(2,1)}, u32[]{:S(2)}, u32[]{:S(2)}) collective-permute-start(bf16[384,1152]{1,0:T(8,128)(2,1)S(1)} %stacked.5.refs_1_), channel_id=1, source_target_pairs={{0,16},{4,20},{8,24},{12,28},{16,0},{20,4},{24,8},{28,12},{1,17},{... | collective-permute-start | bytes 2654216 | tf_op jit(solution)/shard_map/ppermute | solution.py:339
  162.2 41.9 %collective-permute-start.24 = (bf16[384,1152]{1,0:T(8,128)(2,1)S(1)}, bf16[384,1152]{1,0:T(8,128)(2,1)}, u32[]{:S(2)}, u32[]{:S(2)}) collective-permute-start(bf16[384,1152]{1,0:T(8,128)(2,1)S(1)} %stacked.5.refs_1_), channel_id=1, source_target_pairs={{0,8},{4,12},{8,0},{12,4},{16,24},{20,28},{24,16},{28,20},{1,9},{5... | collective-permute-start | bytes 2654216 | tf_op jit(solution)/shard_map/ppermute | solution.py:339
  165.6 41.5 %collective-permute-start.28 = (bf16[384,1152]{1,0:T(8,128)(2,1)S(1)}, bf16[384,1152]{1,0:T(8,128)(2,1)}, u32[]{:S(2)}, u32[]{:S(2)}) collective-permute-start(bf16[384,1152]{1,0:T(8,128)(2,1)S(1)} %stacked.5.refs_1_), channel_id=1, source_target_pairs={{0,4},{4,0},{8,12},{12,8},{16,20},{20,16},{24,28},{28,24},{1,5},{5... | collective-permute-start | bytes 2654216 | tf_op jit(solution)/shard_map/ppermute | solution.py:339
  205.3 40.9 %collective-permute-start.33 = (bf16[384,1152]{1,0:T(8,128)(2,1)S(1)}, bf16[384,1152]{1,0:T(8,128)(2,1)S(1)}, u32[]{:S(2)}, u32[]{:S(2)}) collective-permute-start(bf16[384,1152]{1,0:T(8,128)(2,1)S(1)} %others.1.refs_1_), channel_id=1, source_target_pairs={{0,24},{4,28},{8,16},{12,20},{16,8},{20,12},{24,0},{28,4},{1,25},{... | collective-permute-start | bytes 2654216 | tf_op jit(solution)/shard_map/ppermute | solution.py:339
  207.1 39.8 %collective-permute-start.32 = (bf16[384,1152]{1,0:T(8,128)(2,1)S(1)}, bf16[384,1152]{1,0:T(8,128)(2,1)S(1)}, u32[]{:S(2)}, u32[]{:S(2)}) collective-permute-start(bf16[384,1152]{1,0:T(8,128)(2,1)S(1)} %others.1.refs_1_), channel_id=1, source_target_pairs={{0,16},{4,20},{8,24},{12,28},{16,0},{20,4},{24,8},{28,12},{1,17},{... | collective-permute-start | bytes 2654216 | tf_op jit(solution)/shard_map/ppermute | solution.py:339
  208.6 38.3 %collective-permute-start.27 = (bf16[384,1152]{1,0:T(8,128)(2,1)S(1)}, bf16[384,1152]{1,0:T(8,128)(2,1)S(1)}, u32[]{:S(2)}, u32[]{:S(2)}) collective-permute-start(bf16[384,1152]{1,0:T(8,128)(2,1)S(1)} %others.1.refs_1_), channel_id=1, source_target_pairs={{0,8},{4,12},{8,0},{12,4},{16,24},{20,28},{24,16},{28,20},{1,9},{5... | collective-permute-start | bytes 2654216 | tf_op jit(solution)/shard_map/ppermute | solution.py:339
  208.9 38.5 %collective-permute-start.34 = (bf16[384,1152]{1,0:T(8,128)(2,1)S(1)}, bf16[384,1152]{1,0:T(8,128)(2,1)}, u32[]{:S(2)}, u32[]{:S(2)}) collective-permute-start(bf16[384,1152]{1,0:T(8,128)(2,1)S(1)} %others.1.refs_1_), channel_id=1, source_target_pairs={{0,4},{4,0},{8,12},{12,8},{16,20},{20,16},{24,28},{28,24},{1,5},{5... | collective-permute-start | bytes 2654216 | tf_op jit(solution)/shard_map/ppermute | solution.py:339
  252.3 41.2 %all-to-all-start.3 = ((bf16[8,384,384]{2,1,0:T(8,128)(2,1)}), bf16[8,384,384]{2,1,0:T(8,128)(2,1)S(1)}, u32[]{:S(2)}, u32[]{:S(2)}) async-start(bf16[8,384,384]{2,1,0:T(8,128)(2,1)} %bitcast.26), calls=%async_computation.3 | async-start | bytes 4718592 | tf_op jit(solution)/shard_map/all_to_all | solution.py:1148
  293.5 21.1 %all-to-all-start.4 = ((bf16[8,192,384]{2,1,0:T(8,128)(2,1)}), bf16[8,192,384]{2,1,0:T(8,128)(2,1)S(1)}, u32[]{:S(2)}, u32[]{:S(2)}) async-start(bf16[8,192,384]{2,1,0:T(8,128)(2,1)} %bitcast.29), calls=%async_computation.4 | async-start | bytes 2359296 | tf_op jit(solution)/shard_map/all_to_all | solution.py:1148
  314.6 31.2 %all-to-all-start.5 = ((bf16[8,64,1280]{2,1,0:T(8,128)(2,1)}), bf16[8,64,1280]{2,1,0:T(8,128)(2,1)S(1)}, u32[]{:S(2)}, u32[]{:S(2)}) async-start(bf16[8,64,1280]{2,1,0:T(8,128)(2,1)} %bitcast.28), calls=%async_computation.5 | async-start | bytes 2621440 | tf_op jit(solution)/shard_map/all_to_all | solution.py:1148
  345.9 32.2 %all-to-all-start.6 = ((bf16[8,64,1024]{2,1,0:T(8,128)(2,1)}), bf16[8,64,1024]{2,1,0:T(8,128)(2,1)S(1)}, u32[]{:S(2)}, u32[]{:S(2)}) async-start(bf16[8,64,1024]{2,1,0:T(8,128)(2,1)} %bitcast.30), calls=%async_computation.6 | async-start | bytes 2097152 | tf_op jit(solution)/shard_map/all_to_all | solution.py:1148
  357.7 24.1 %collective-permute-start.59 = (bf16[9,16,384]{2,1,0:T(8,128)(2,1)S(1)}, bf16[9,16,384]{2,1,0:T(8,128)(2,1)S(1)}, u32[]{:S(2)}, u32[]{:S(2)}) collective-permute-start(bf16[9,16,384]{2,1,0:T(8,128)(2,1)S(1)} %pad_maximum_fusion.refs_1_), channel_id=1, source_target_pairs={{0,24},{4,28},{8,16},{12,20},{16,8},{20,12},{24,0},{28,4},{1,25},{... | collective-permute-start | bytes 331784 | tf_op jit(solution)/shard_map/ppermute | solution.py:339
  360.5 22.2 %collective-permute-start.58 = (bf16[9,16,384]{2,1,0:T(8,128)(2,1)S(1)}, bf16[9,16,384]{2,1,0:T(8,128)(2,1)S(1)}, u32[]{:S(2)}, u32[]{:S(2)}) collective-permute-start(bf16[9,16,384]{2,1,0:T(8,128)(2,1)S(1)} %pad_maximum_fusion.refs_1_), channel_id=1, source_target_pairs={{0,16},{4,20},{8,24},{12,28},{16,0},{20,4},{24,8},{28,12},{1,17},{... | collective-permute-start | bytes 331784 | tf_op jit(solution)/shard_map/ppermute | solution.py:339
  361.1 22.8 %collective-permute-start.57 = (bf16[9,16,384]{2,1,0:T(8,128)(2,1)S(1)}, bf16[9,16,384]{2,1,0:T(8,128)(2,1)S(1)}, u32[]{:S(2)}, u32[]{:S(2)}) collective-permute-start(bf16[9,16,384]{2,1,0:T(8,128)(2,1)S(1)} %pad_maximum_fusion.refs_1_), channel_id=1, source_target_pairs={{0,8},{4,12},{8,0},{12,4},{16,24},{20,28},{24,16},{28,20},{1,9},{5... | collective-permute-start | bytes 331784 | tf_op jit(solution)/shard_map/ppermute | solution.py:339
  (88 other events, 796.0 us)

commit v4 on v3

--- a/solution.py
+++ b/solution.py
@@ -406,27 +406,32 @@
     )(picks, values)
 
 
-def totals_by_shift(ids, values):
-    terms, groups = values.shape[0], values.shape[1]
-    shape = values.shape[2:]
-
-    def kernel(ids_ref, in_ref, *out_refs):
+def totals_by_shift(ids, one, two):
+    terms, groups = one.shape[0], one.shape[1]
+    shape = list(one.shape[2:])
+    along = 0 if len(shape) == 3 else len(shape) - 1
+    cut = shape[along]
+    shape[along] += two.shape[2 + along]
+
+    def kernel(ids_ref, one_ref, two_ref, *out_refs):
         z = ids_ref[1]
         for t in range(groups):
             q = lax.rem(z + t, groups)
-            whole = in_ref[0, q].astype(f32)
-            for k in range(1, terms):
-                whole = whole + in_ref[k, q].astype(f32)
-            out_refs[(t - 1) % groups][...] = whole.astype(bf16)
+            for in_ref, at in ((one_ref, slice(0, cut)), (two_ref, slice(cut, shape[along]))):
+                whole = in_ref[0, q].astype(f32)
+                for k in range(1, terms):
+                    whole = whole + in_ref[k, q].astype(f32)
+                where = (at,) if along == 0 else (slice(None), at)
+                out_refs[(t - 1) % groups][where] = whole.astype(bf16)
 
     return pl.pallas_call(
         kernel,
         name="totals",
-        out_shape=[jax.ShapeDtypeStruct(shape, bf16)] * groups,
-        in_specs=[smem_spec(), vmem_spec()],
+        out_shape=[jax.ShapeDtypeStruct(tuple(shape), bf16)] * groups,
+        in_specs=[smem_spec(), vmem_spec(), vmem_spec()],
         out_specs=[vmem_spec()] * groups,
-        compiler_params=pltpu.CompilerParams(vmem_limit_bytes=8 * 2**20),
-    )(ids, values)
+        compiler_params=pltpu.CompilerParams(vmem_limit_bytes=16 * 2**20),
+    )(ids, one, two)
 
 
 def from_planes(joined, widths):
@@ -458,6 +463,10 @@
 
 def any_spec():
     return pl.BlockSpec(memory_space=pl.ANY)
+
+
+def hbm_spec():
+    return pl.BlockSpec(memory_space=pltpu.HBM)
 
 
 def vmem_spec():
@@ -561,7 +570,7 @@
         kernel,
         name="own",
         out_shape=[sds(v, bf16) for v in shapes],
-        in_specs=[smem_spec()] + [any_spec()] * 5,
+        in_specs=[smem_spec()] + [hbm_spec()] * 5,
         out_specs=[vmem_spec()] * PARTS,
         scratch_shapes=[pltpu.SemaphoreType.DMA((PARTS,))],
         compiler_params=pltpu.CompilerParams(vmem_limit_bytes=6 * 2**20),
@@ -1180,6 +1189,10 @@
         jnp.where(order_row[None, :] == counting[:, None], counting[None, :], 0), axis=1
     )
     width = gate_weight.shape[1] // PARTS
+    sel, after_one, after_two = per_token_tables(
+        lengths[:, 0, :][s], adapter_ids[:, 0, :][s], rows, a_in.shape[1], ADAPTER_RANK
+    )
+    sel2 = sel * adapter_scale
     packed = own_pieces(ids, in_weight, out_weight, gate_weight, up_weight, down_weight, dp_count)
     arrived = lax.all_to_all(cotangent, "dp", split_axis=0, concat_axis=0, tiled=True)
     io_width = in_weight.shape[1] + out_weight.shape[1]
@@ -1190,14 +1203,10 @@
     io = [zs_io, *near_io]
     io = io + core_copies(io)
     dy = lax.all_to_all(
-        picked(arrived, after(inverse_row, packed[0]), dp_count), "dp", split_axis=0, concat_axis=0,
+        picked(arrived, after(inverse_row, packed[0], sel2, after_one, after_two), dp_count), "dp", split_axis=0, concat_axis=0,
         tiled=True,
     )
 
-    sel, after_one, after_two = per_token_tables(
-        lengths[:, 0, :][s], adapter_ids[:, 0, :][s], rows, a_in.shape[1], ADAPTER_RANK
-    )
-    sel2 = sel * adapter_scale
     gain1 = norm_gain[None, :]
     gain2 = ffn_gain[None, :]
     first = after(zs[0], dy, *near_io)
@@ -1229,34 +1238,24 @@
         previous = state[2]
         grads.append(g)
     late = exchange(grads[-1], "dp")
-    early_sums = totals_by_shift(ids, after(early, g))
-    early = send_to_groups(early_sums)
     result, dhb, dzo, g_a = middle_call(
-        *state, h, n2, dy, y, zout, sel2, after(gain2, early_sums[0]), b_down, a_gate, a_up, b_out
-    )
+        *state, h, n2, dy, y, zout, sel2, after(gain2, early), b_down, a_gate, a_up, b_out
+    )
+    ffn_sums = totals_by_shift(ids, early, after(late, dzo))
     g_a = exchange(g_a, "dp")
-    early = add_up([after(early[0], dzo), *early[1:]])
-    late_sums = totals_by_shift(ids, after(late, dzo))
-    late = send_to_groups(late_sums)
+    ffn = send_to_groups(ffn_sums)
     dp, dzi, g_i = back_call(
-        dhb, dzo, mix, cv, zin, n1, sel2, after_one, after_two, after(conv_weight, late_sums[0], early), a_out,
-        b_in, w_out,
+        dhb, dzo, mix, cv, zin, n1, sel2, after_one, after_two, after(conv_weight, ffn_sums[0]), a_out, b_in, w_out,
     )
     g_i = exchange(g_i, "dp")
-    late = add_up([after(late[0], dzi), *late[1:]])
-    ffn = near_shares(jnp.concatenate([early, late], axis=0))
-    ga_sums = totals_by_shift(ids, after(g_a, dzi))
-    g_a = send_to_groups(ga_sums)
-    input_grad = last_call(dp, dzi, dhb, tokens, after(gain1, ga_sums[0]), a_in, w_in)
-    gi_sums = totals_by_shift(ids, after(g_i, input_grad))
-    g_i = send_to_groups(gi_sums)
-    g_a = add_up([after(g_a[0], input_grad), *g_a[1:]])
-    ffn = all_shares([after(v, input_grad) for v in ffn])
+    input_grad = last_call(dp, dzi, dhb, tokens, after(gain1, g_a), a_in, w_in)
+    sums = totals_by_shift(ids, g_a, after(g_i, input_grad))
+    small = send_to_groups(sums)
+    ffn = all_shares(near_shares(add_up([after(ffn[0], input_grad, sums[0]), *ffn[1:]])))
     q = d // lax.axis_size("group")
     layout = [([(3 * j + k, 0, width) for j in range(PARTS)], k == 2) for k in range(3)]
-    g_gate_b, g_up_b, g_down_a = finish_call(after(ids, gi_sums[0]), ffn, layout)
-    g_i = add_up(g_i)
-    small = all_shares(near_shares(jnp.concatenate([g_a, g_i], axis=1)))
+    g_gate_b, g_up_b, g_down_a = finish_call(after(ids, sums[0]), ffn, layout)
+    small = all_shares(near_shares(add_up(small)))
     layout = [([(None, k * q, q)], k >= 2) for k in range(5)]
     layout += [([(None, 5 * q, 3 * q)], False), ([(None, 8 * q, q)], True)]
     g_out_b, g_down_b, g_gate_a, g_up_a, g_out_a, g_in_b, g_in_a = finish_call(ids, small, layout)

time: 411 us -> 399 us (0.971)
  waiting for transfers between devices: 86.3 us -> 80 us
  starting transfers between devices: 93.4 us -> 87.7 us
    ppermute x12 -> x6, waiting for transfers between devices: 10.6 us -> 0.02 us  [send_to_groups(): lax.ppermute(sums[t - 1], 'group', [(i, (i + t) % groups) for i in range(...]
    ppermute x12 -> x6, starting transfers between devices: 18.7 us -> 9.79 us  [send_to_groups(): lax.ppermute(sums[t - 1], 'group', [(i, (i + t) % groups) for i in range(...]
    unnamed x98 -> x90, local copies, waits for them, and re-layouts: 11.9 us -> 14.6 us
  transfers between devices with their start and end apart: 71 -> 65, of which waited for: 27 -> 17; matrix products, arithmetic and copies ran while one was open for 3% -> 2% of each run, Pallas kernels for 49% -> 50%
where the time goes in v4:
time: 399 us; the launch traced here: 392 us
  Pallas kernels  198 us (50%)
  starting transfers between devices  87.7 us (22%)
  waiting for transfers between devices  80 us (20%)
  local copies, waits for them, and re-layouts  18.7 us (5%)
    pallas_call x3, Pallas kernels, ffn_call(): pl.pallas_call(kernel, name=f'ffn{part}', out_shape=[sds(*v) for v in sta...  111 us
    ppermute x46, waiting for transfers between devices, swap_dp(): lax.ppermute(values, 'dp', [(i, i ^ bit) for i in range(lax.axis_size('dp...  50.9 us
    ppermute x46, starting transfers between devices, swap_dp(): lax.ppermute(values, 'dp', [(i, i ^ bit) for i in range(lax.axis_size('dp...  30.9 us
    all_to_all x5, starting transfers between devices, exchange(): lax.all_to_all(flat, axis, split_axis=0, concat_axis=0, tiled=True)  24 us
    pallas_call x1, Pallas kernels, front_call(): pl.pallas_call(kernel, name='front', out_shape=[sds(wide[0], bf16), sds((...  17.5 us
    pallas_call x1, Pallas kernels, back_call(): pl.pallas_call(kernel, name='back', out_shape=[sds((rows, 3 * d), bf16),...  17.3 us
    pallas_call x1, Pallas kernels, last_call(): pl.pallas_call(kernel, name='last', out_shape=sds((rows, d), bf16), in_sp...  16 us
    unnamed x90, local copies, waits for them, and re-layouts  14.6 us
  transfers between devices with their start and end apart: 65, of which 17 were waited for; matrix products, arithmetic and copies ran while one was open for 2% of the time, Pallas kernels for 50%

profile of v4, /device:TPU:0, one launch (start us, length us, event | category | flops | bytes accessed | tf_op | source)
XLA Modules:
  0.0 392.0 jit_solution(14035853985164598918)
XLA Ops:
  0.7 5.4 %all-to-all-start = ((bf16[8,128,1024]{2,1,0:T(8,128)(2,1)}), bf16[8,128,1024]{2,1,0:T(8,128)(2,1)}, u32[]{:S(2)}, u32[]{:S(2)}) async-start(bf16[8,128,1024]{2,1,0:T(8,128)(2,1)} %bitcast.26), calls=%async_computation | async-start | bytes 4194304 | tf_op jit(solution)/shard_map/all_to_all | solution.py:1197
  13.6 2.2 collective-permute-start
  15.8 2.6 collective-permute-start.1
  22.5 10.3 %all-to-all-done = bf16[8,128,1024]{2,1,0:T(8,128)(2,1)} async-done(((bf16[8,128,1024]{2,1,0:T(8,128)(2,1)}), bf16[8,128,1024]{2,1,0:T(8,128)(2,1)}, u32[]{:S(2)}, u32[]{:S(2)}) %all-to-all-start) | async-done | bytes 2097184 | tf_op jit(solution)/shard_map/all_to_all | solution.py:1197
  32.9 3.4 picked.1
  36.2 4.4 %all-to-all-start.1 = ((bf16[8,128,1024]{2,1,0:T(8,128)(2,1)}), bf16[8,128,1024]{2,1,0:T(8,128)(2,1)}, u32[]{:S(2)}, u32[]{:S(2)}) async-start(bf16[8,128,1024]{2,1,0:T(8,128)(2,1)} %bitcast.6), calls=%async_computation.1 | async-start | bytes 4194304 | tf_op jit(solution)/shard_map/all_to_all | solution.py:1205
  40.6 14.4 %collective-permute-done.1.refs_1_ = bf16[128,2176]{1,0:T(8,128)(2,1)S(1)} collective-permute-done((bf16[128,2176]{1,0:T(8,128)(2,1)S(1)}, bf16[128,2176]{1,0:T(8,128)(2,1)S(1)}, u32[]{:S(2)}, u32[]{:S(2)}) %collective-permute-start.1) | collective-permute-done | bytes 557088 | tf_op jit(solution)/shard_map/ppermute | solution.py:440
  58.3 24.7 %collective-permute-done.4.refs_3_ = bf16[384,1024]{1,0:T(8,128)(2,1)S(1)} collective-permute-done((bf16[384,1024]{1,0:T(8,128)(2,1)S(1)}, bf16[384,1024]{1,0:T(8,128)(2,1)S(1)}, u32[]{:S(2)}, u32[]{:S(2)}) %collective-permute-start.4) | collective-permute-done | bytes 786464 | tf_op jit(solution)/shard_map/ppermute | solution.py:339
  85.2 8.2 %collective-permute-done.5.refs_4_ = bf16[128,1024]{1,0:T(8,128)(2,1)S(1)} collective-permute-done((bf16[128,1024]{1,0:T(8,128)(2,1)S(1)}, bf16[128,1024]{1,0:T(8,128)(2,1)S(1)}, u32[]{:S(2)}, u32[]{:S(2)}) %collective-permute-start.5) | collective-permute-done | bytes 262176 | tf_op jit(solution)/shard_map/ppermute | solution.py:339
  94.2 2.7 collective-permute-done.6.refs_5_
  99.5 3.1 collective-permute-done.10.refs_9_
  102.8 3.5 collective-permute-start.12
  108.0 17.5 %front.1 = (bf16[1024,1024]{1,0:T(8,128)(2,1)}, bf16[1024,128]{1,0:T(8,128)(2,1)}, bf16[1024,3072]{1,0:T(8,128)(2,1)}, bf16[1024,1024]{1,0:T(8,128)(2,1)}, bf16[...) custom-call(s32[2]{0:T(128)} %copy-done.16, bf16[384,1024]{1,0:T(8,128)(2,1)} %copy-done.3, ...), custom_call_target="tpu_custom_call" | custom-call | flops 2044723 | tf_op jit(solution)/shard_map/front/pallas_call | solution.py:646
  129.0 3.4 collective-permute-start.14
  134.7 12.3 %join.1 = (bf16[1024,128]{1,0:T(8,128)(2,1)}, bf16[1024,1024]{1,0:T(8,128)(2,1)}, bf16[1024,1024]{1,0:T(8,128)(2,1)}, bf16[1024,256]{1,0:T(8,128)(2,1)}, bf16[1024,1024]{1,0:T(8,128)(2,1)}) custom-call(s32[2]{0:T(128)} %copy-done.16, bf16[384,1024]{1,0:T(8,128)(2,1)} %copy-done.3, bf16[384,1024]{1,0:T(8,128)(2,1)} %copy-done.28, ...), custom_call_target="tpu_custom_call" | custom-call | flops 681574 | tf_op jit(solution)/shard_map/join/pallas_call | solution.py:700
  147.8 7.2 %all-to-all-start.2 = ((bf16[4,128,1152]{2,1,0:T(8,128)(2,1)}), bf16[4,128,1152]{2,1,0:T(8,128)(2,1)S(1)}, u32[]{:S(2)}, u32[]{:S(2)}) async-start(bf16[4,128,1152]{2,1,0:T(8,128)(2,1)} %bitcast.24), calls=%async_computation.2 | async-start | bytes 2359296 | tf_op jit(solution)/shard_map/all_to_all | solution.py:1157
  158.5 2.1 collective-permute-done.23.refs_10_
  162.5 3.0 fusion.refs_20_.refs_18_
  166.3 37.1 %ffn0.1 = (bf16[1024,1024]{1,0:T(8,128)(2,1)}, bf16[1024,1024]{1,0:T(8,128)(2,1)}, f32[1024,256]{1,0:T(8,128)}, f32[1024,128]{1,0:T(8,128)}, bf16[8,4,3,16,384]{4,3,2,1,0:T(8,128)(2,1)}) custom-call(s32[2]{0:T(128)} %copy-done.16, bf16[384,1152]{1,0:T(8,128)(2,1)} %copy-done.6, bf16[384,1152]{1,0:T(8,128)(2,1)} %collective-permute-done.15.refs_2_, ...), custom_call_target="tpu_custom_call" | custom-call | flops 6134169 | tf_op jit(solution)/shard_map/ffn0/pallas_call | solution.py:889
  209.0 37.2 %ffn1.1 = (bf16[1024,1024]{1,0:T(8,128)(2,1)}, bf16[1024,1024]{1,0:T(8,128)(2,1)}, f32[1024,256]{1,0:T(8,128)}, f32[1024,128]{1,0:T(8,128)}, bf16[8,4,6,16,384]{4,3,2,1,0:T(8,128)(2,1)}) custom-call(s32[2]{0:T(128)} %copy-done.16, bf16[384,1152]{1,0:T(8,128)(2,1)} %copy-done.5, bf16[384,1152]{1,0:T(8,128)(2,1)} %collective-permute-done.24.refs_2_, ...), custom_call_target="tpu_custom_call" | custom-call | flops 6134169 | tf_op jit(solution)/shard_map/ffn1/pallas_call | solution.py:889
  252.2 3.8 all-to-all-start.3
  256.1 37.1 %ffn2.1 = (bf16[1024,1024]{1,0:T(8,128)(2,1)}, bf16[1024,1024]{1,0:T(8,128)(2,1)}, f32[1024,256]{1,0:T(8,128)}, f32[1024,128]{1,0:T(8,128)}, bf16[8,4,3,16,384]{4,3,2,1,0:T(8,128)(2,1)}) custom-call(s32[2]{0:T(128)} %copy-done.16, bf16[384,1152]{1,0:T(8,128)(2,1)} %copy-done.7, bf16[384,1152]{1,0:T(8,128)(2,1)} %copy-done.36, bf16[384,1152]{1,0:T(8,128)(2,1)} %copy-done.35, ...), custom_call_target="tpu_custom_call" | custom-call | flops 6134169 | tf_op jit(solution)/shard_map/ffn2/pallas_call | solution.py:889
  293.2 4.2 %all-to-all-start.4 = ((bf16[8,192,384]{2,1,0:T(8,128)(2,1)}), bf16[8,192,384]{2,1,0:T(8,128)(2,1)S(1)}, u32[]{:S(2)}, u32[]{:S(2)}) async-start(bf16[8,192,384]{2,1,0:T(8,128)(2,1)} %bitcast.28), calls=%async_computation.4 | async-start | bytes 2359296 | tf_op jit(solution)/shard_map/all_to_all | solution.py:1157
  297.3 12.4 %middle.1 = (bf16[1024,1024]{1,0:T(8,128)(2,1)}, bf16[1024,1024]{1,0:T(8,128)(2,1)}, bf16[1024,128]{1,0:T(8,128)(2,1)}, bf16[8,4,16,1280]{3,2,1,0:T(8,128)(2,1)}) custom-call(bf16[1024,1024]{1,0:T(8,128)(2,1)} %get-tuple-element.133.dn_hbm, bf16[1024,1024]{1,0:T(8,128)(2,1)} %get-tuple-element.106.refs_17_.refs_15_.n2_hbm, ...), custom_call_target="tpu_custom_call" | custom-call | flops 2097152 | tf_op jit(solution)/shard_map/middle/pallas_call | solution.py:980
  309.8 4.4 %all-to-all-done.4 = bf16[8,192,384]{2,1,0:T(8,128)(2,1)S(1)} async-done(((bf16[8,192,384]{2,1,0:T(8,128)(2,1)}), bf16[8,192,384]{2,1,0:T(8,128)(2,1)S(1)}, u32[]{:S(2)}, u32[]{:S(2)}) %all-to-all-start.4) | async-done | bytes 1179680 | tf_op jit(solution)/shard_map/all_to_all | solution.py:1157
  314.1 4.5 %all-to-all-start.5 = ((bf16[8,64,1280]{2,1,0:T(8,128)(2,1)}), bf16[8,64,1280]{2,1,0:T(8,128)(2,1)}, u32[]{:S(2)}, u32[]{:S(2)}) async-start(bf16[8,64,1280]{2,1,0:T(8,128)(2,1)} %bitcast.27), calls=%async_computation.5 | async-start | bytes 2621440 | tf_op jit(solution)/shard_map/all_to_all | solution.py:1157
  322.3 17.3 %back.1 = (bf16[1024,3072]{1,0:T(8,128)(2,1)}, bf16[1024,128]{1,0:T(8,128)(2,1)}, bf16[8,4,16,1024]{3,2,1,0:T(8,128)(2,1)}) custom-call(bf16[1024,1024]{1,0:T(8,128)(2,1)} %get-tuple-element.142.w_out_hbm, bf16[1024,1024]{1,0:T(8,128)(2,1)} %get-tuple-element.143.dhb_hbm.dh_hbm, bf16[1024,1024]{1,0:T(8,128)(2,1)} %get-tuple-element.144.cv_hbm, ...), custom_call_target="tpu_custom_call" | custom-call | flops 2097152 | tf_op jit(solution)/shard_map/back/pallas_call | solution.py:1039
  339.6 4.2 %all-to-all-start.6 = ((bf16[8,64,1024]{2,1,0:T(8,128)(2,1)}), bf16[8,64,1024]{2,1,0:T(8,128)(2,1)S(1)}, u32[]{:S(2)}, u32[]{:S(2)}) async-start(bf16[8,64,1024]{2,1,0:T(8,128)(2,1)} %bitcast.29), calls=%async_computation.6 | async-start | bytes 2097152 | tf_op jit(solution)/shard_map/all_to_all | solution.py:1157
  346.0 2.3 collective-permute-start.49
  349.8 16.0 %last.1 = bf16[1024,1024]{1,0:T(8,128)(2,1)} custom-call(bf16[1024,3072]{1,0:T(8,128)(2,1)} %get-tuple-element.152.dp_hbm, bf16[1024,3072]{1,0:T(8,128)(2,1)} %get-tuple-element.153.w_in_hbm, bf16[1024,1024]{1,0:T(8,128)(2,1)} %get-tuple-element.143.dhb_hbm.dh_hbm, bf16[1024,1024]{1,0:T(8,128)(2,1)} %x_hbm.1, bf16[1024,128]{1,0:T(8,128)(2,1)} %get-tuple-element.154.dzi_ref, ...), custom_call_target="tpu_custom_call" | custom-call | flops 2097152 | tf_op jit(solution)/shard_map/last/pallas_call | solution.py:1086
  368.7 2.7 collective-permute-start.40
  375.0 2.4 collective-permute-start.53
  (223 shorter events, 74.1 us)
Async XLA Ops:
  0.7 32.2 %all-to-all-start = ((bf16[8,128,1024]{2,1,0:T(8,128)(2,1)}), bf16[8,128,1024]{2,1,0:T(8,128)(2,1)}, u32[]{:S(2)}, u32[]{:S(2)}) async-start(bf16[8,128,1024]{2,1,0:T(8,128)(2,1)} %bitcast.26), calls=%async_computation | async-start | bytes 4194304 | tf_op jit(solution)/shard_map/all_to_all | solution.py:1197
  13.6 27.0 %collective-permute-start = (bf16[128,2176]{1,0:T(8,128)(2,1)S(1)}, bf16[128,2176]{1,0:T(8,128)(2,1)S(1)}, u32[]{:S(2)}, u32[]{:S(2)}) collective-permute-start(bf16[128,2176]{1,0:T(8,128)(2,1)S(1)} %get-tuple-element.96), channel_id=1, source_target_pairs={{0,1},{1,2},{2,3},{3,0},{4,5},{5,6},{6,7},{7,4},{8,9},{9,10},{10,1... | collective-permute-start | bytes 1671176 | tf_op jit(solution)/shard_map/ppermute | solution.py:440
  15.8 39.2 %collective-permute-start.1 = (bf16[128,2176]{1,0:T(8,128)(2,1)S(1)}, bf16[128,2176]{1,0:T(8,128)(2,1)S(1)}, u32[]{:S(2)}, u32[]{:S(2)}) collective-permute-start(bf16[128,2176]{1,0:T(8,128)(2,1)S(1)} %get-tuple-element.96), channel_id=1, source_target_pairs={{0,2},{1,3},{2,0},{3,1},{4,6},{5,7},{6,4},{7,5},{8,10},{9,11},{10,... | collective-permute-start | bytes 1671176 | tf_op jit(solution)/shard_map/ppermute | solution.py:440
  18.4 36.6 %collective-permute-start.2 = (bf16[128,2176]{1,0:T(8,128)(2,1)S(1)}, bf16[128,2176]{1,0:T(8,128)(2,1)S(1)}, u32[]{:S(2)}, u32[]{:S(2)}) collective-permute-start(bf16[128,2176]{1,0:T(8,128)(2,1)S(1)} %get-tuple-element.96), channel_id=1, source_target_pairs={{0,3},{1,0},{2,1},{3,2},{4,7},{5,4},{6,5},{7,6},{8,11},{9,8},{10,9... | collective-permute-start | bytes 1671176 | tf_op jit(solution)/shard_map/ppermute | solution.py:440
  36.2 60.6 %all-to-all-start.1 = ((bf16[8,128,1024]{2,1,0:T(8,128)(2,1)}), bf16[8,128,1024]{2,1,0:T(8,128)(2,1)}, u32[]{:S(2)}, u32[]{:S(2)}) async-start(bf16[8,128,1024]{2,1,0:T(8,128)(2,1)} %bitcast.6), calls=%async_computation.1 | async-start | bytes 4194304 | tf_op jit(solution)/shard_map/all_to_all | solution.py:1205
  55.1 28.0 %collective-permute-start.4 = (bf16[384,1024]{1,0:T(8,128)(2,1)S(1)}, bf16[384,1024]{1,0:T(8,128)(2,1)S(1)}, u32[]{:S(2)}, u32[]{:S(2)}) collective-permute-start(bf16[384,1024]{1,0:T(8,128)(2,1)S(1)} %stacked.4.refs_1_), channel_id=1, source_target_pairs={{0,16},{4,20},{8,24},{12,28},{16,0},{20,4},{24,8},{28,12},{1,17},{... | collective-permute-start | bytes 2359304 | tf_op jit(solution)/shard_map/ppermute | solution.py:339
  56.9 27.8 %collective-permute-start.3 = (bf16[384,1024]{1,0:T(8,128)(2,1)S(1)}, bf16[384,1024]{1,0:T(8,128)(2,1)S(1)}, u32[]{:S(2)}, u32[]{:S(2)}) collective-permute-start(bf16[384,1024]{1,0:T(8,128)(2,1)S(1)} %stacked.4.refs_1_), channel_id=1, source_target_pairs={{0,8},{4,12},{8,0},{12,4},{16,24},{20,28},{24,16},{28,20},{1,9},{5... | collective-permute-start | bytes 2359304 | tf_op jit(solution)/shard_map/ppermute | solution.py:339
  96.9 28.6 %collective-permute-start.15 = (bf16[384,1152]{1,0:T(8,128)(2,1)S(1)}, bf16[384,1152]{1,0:T(8,128)(2,1)}, u32[]{:S(2)}, u32[]{:S(2)}) collective-permute-start(bf16[384,1152]{1,0:T(8,128)(2,1)S(1)} %stacked.3.refs_1_), channel_id=1, source_target_pairs={{0,8},{4,12},{8,0},{12,4},{16,24},{20,28},{24,16},{28,20},{1,9},{5... | collective-permute-start | bytes 2654216 | tf_op jit(solution)/shard_map/ppermute | solution.py:339
  99.1 29.8 %collective-permute-start.16 = (bf16[384,1152]{1,0:T(8,128)(2,1)S(1)}, bf16[384,1152]{1,0:T(8,128)(2,1)}, u32[]{:S(2)}, u32[]{:S(2)}) collective-permute-start(bf16[384,1152]{1,0:T(8,128)(2,1)S(1)} %stacked.3.refs_1_), channel_id=1, source_target_pairs={{0,16},{4,20},{8,24},{12,28},{16,0},{20,4},{24,8},{28,12},{1,17},{... | collective-permute-start | bytes 2654216 | tf_op jit(solution)/shard_map/ppermute | solution.py:339
  102.8 31.3 %collective-permute-start.12 = (bf16[128,1152]{1,0:T(8,128)(2,1)}, bf16[128,1152]{1,0:T(8,128)(2,1)S(1)}, u32[]{:S(2)}, u32[]{:S(2)}) collective-permute-start(bf16[128,1152]{1,0:T(8,128)(2,1)} %copy-done.19), channel_id=1, source_target_pairs={{0,1},{1,2},{2,3},{3,0},{4,5},{5,6},{6,7},{7,4},{8,9},{9,10},{10,1... | collective-permute-start | bytes 884744 | tf_op jit(solution)/shard_map/ppermute | solution.py:440
  127.4 28.8 %collective-permute-start.17 = (bf16[256,1152]{1,0:T(8,128)(2,1)}, bf16[256,1152]{1,0:T(8,128)(2,1)}, u32[]{:S(2)}, u32[]{:S(2)}) collective-permute-start(bf16[256,1152]{1,0:T(8,128)(2,1)} %slice.14), channel_id=1, source_target_pairs={{0,16},{4,20},{8,24},{12,28},{16,0},{20,4},{24,8},{28,12},{1,17},{... | collective-permute-start | bytes 1769480 | tf_op jit(solution)/shard_map/ppermute | solution.py:339
  128.9 29.1 %collective-permute-start.19 = (bf16[384,1152]{1,0:T(8,128)(2,1)S(1)}, bf16[384,1152]{1,0:T(8,128)(2,1)}, u32[]{:S(2)}, u32[]{:S(2)}) collective-permute-start(bf16[384,1152]{1,0:T(8,128)(2,1)S(1)} %stacked.3.refs_1_), channel_id=1, source_target_pairs={{0,4},{4,0},{8,12},{12,8},{16,20},{20,16},{24,28},{28,24},{1,5},{5... | collective-permute-start | bytes 2654216 | tf_op jit(solution)/shard_map/ppermute | solution.py:339
  128.9 18.1 %collective-permute-start.13 = (bf16[128,1152]{1,0:T(8,128)(2,1)S(1)}, bf16[128,1152]{1,0:T(8,128)(2,1)S(1)}, u32[]{:S(2)}, u32[]{:S(2)}) collective-permute-start(bf16[128,1152]{1,0:T(8,128)(2,1)S(1)} %copy-done.20), channel_id=1, source_target_pairs={{0,2},{1,3},{2,0},{3,1},{4,6},{5,7},{6,4},{7,5},{8,10},{9,11},{10,... | collective-permute-start | bytes 884744 | tf_op jit(solution)/shard_map/ppermute | solution.py:440
  129.0 18.1 %collective-permute-start.14 = (bf16[128,1152]{1,0:T(8,128)(2,1)S(1)}, bf16[128,1152]{1,0:T(8,128)(2,1)S(1)}, u32[]{:S(2)}, u32[]{:S(2)}) collective-permute-start(bf16[128,1152]{1,0:T(8,128)(2,1)S(1)} %copy-done.20), channel_id=1, source_target_pairs={{0,3},{1,0},{2,1},{3,2},{4,7},{5,4},{6,5},{7,6},{8,11},{9,8},{10,9... | collective-permute-start | bytes 884744 | tf_op jit(solution)/shard_map/ppermute | solution.py:440
  134.0 22.2 %collective-permute-start.18 = (bf16[128,1152]{1,0:T(8,128)(2,1)}, bf16[128,1152]{1,0:T(8,128)(2,1)}, u32[]{:S(2)}, u32[]{:S(2)}) collective-permute-start(bf16[128,1152]{1,0:T(8,128)(2,1)} %slice.15), channel_id=1, source_target_pairs={{0,8},{4,12},{8,0},{12,4},{16,24},{20,28},{24,16},{28,20},{1,9},{5... | collective-permute-start | bytes 884744 | tf_op jit(solution)/shard_map/ppermute | solution.py:339
  147.1 18.4 %collective-permute-start.20 = (bf16[384,1152]{1,0:T(8,128)(2,1)}, bf16[384,1152]{1,0:T(8,128)(2,1)}, u32[]{:S(2)}, u32[]{:S(2)}) collective-permute-start(bf16[384,1152]{1,0:T(8,128)(2,1)} %collective-permute-done.15.refs_2_), channel_id=1, source_target_pairs={{0,4},{4,0},{8,12},{12,8},{16,20},{20,16},{24,28},{28,24},{1,5},{5... | collective-permute-start | bytes 2654216 | tf_op jit(solution)/shard_map/ppermute | solution.py:339
  147.8 56.7 %all-to-all-start.2 = ((bf16[4,128,1152]{2,1,0:T(8,128)(2,1)}), bf16[4,128,1152]{2,1,0:T(8,128)(2,1)S(1)}, u32[]{:S(2)}, u32[]{:S(2)}) async-start(bf16[4,128,1152]{2,1,0:T(8,128)(2,1)} %bitcast.24), calls=%async_computation.2 | async-start | bytes 2359296 | tf_op jit(solution)/shard_map/all_to_all | solution.py:1157
  156.3 47.2 %collective-permute-start.26 = (bf16[384,1152]{1,0:T(8,128)(2,1)S(1)}, bf16[384,1152]{1,0:T(8,128)(2,1)}, u32[]{:S(2)}, u32[]{:S(2)}) collective-permute-start(bf16[384,1152]{1,0:T(8,128)(2,1)S(1)} %stacked.5.refs_1_), channel_id=1, source_target_pairs={{0,24},{4,28},{8,16},{12,20},{16,8},{20,12},{24,0},{28,4},{1,25},{... | collective-permute-start | bytes 2654216 | tf_op jit(solution)/shard_map/ppermute | solution.py:339
  160.6 43.4 %collective-permute-start.25 = (bf16[384,1152]{1,0:T(8,128)(2,1)S(1)}, bf16[384,1152]{1,0:T(8,128)(2,1)}, u32[]{:S(2)}, u32[]{:S(2)}) collective-permute-start(bf16[384,1152]{1,0:T(8,128)(2,1)S(1)} %stacked.5.refs_1_), channel_id=1, source_target_pairs={{0,16},{4,20},{8,24},{12,28},{16,0},{20,4},{24,8},{28,12},{1,17},{... | collective-permute-start | bytes 2654216 | tf_op jit(solution)/shard_map/ppermute | solution.py:339
  161.1 43.0 %collective-permute-start.24 = (bf16[384,1152]{1,0:T(8,128)(2,1)S(1)}, bf16[384,1152]{1,0:T(8,128)(2,1)}, u32[]{:S(2)}, u32[]{:S(2)}) collective-permute-start(bf16[384,1152]{1,0:T(8,128)(2,1)S(1)} %stacked.5.refs_1_), channel_id=1, source_target_pairs={{0,8},{4,12},{8,0},{12,4},{16,24},{20,28},{24,16},{28,20},{1,9},{5... | collective-permute-start | bytes 2654216 | tf_op jit(solution)/shard_map/ppermute | solution.py:339
  165.5 41.5 %collective-permute-start.28 = (bf16[384,1152]{1,0:T(8,128)(2,1)S(1)}, bf16[384,1152]{1,0:T(8,128)(2,1)}, u32[]{:S(2)}, u32[]{:S(2)}) collective-permute-start(bf16[384,1152]{1,0:T(8,128)(2,1)S(1)} %stacked.5.refs_1_), channel_id=1, source_target_pairs={{0,4},{4,0},{8,12},{12,8},{16,20},{20,16},{24,28},{28,24},{1,5},{5... | collective-permute-start | bytes 2654216 | tf_op jit(solution)/shard_map/ppermute | solution.py:339
  205.3 40.8 %collective-permute-start.33 = (bf16[384,1152]{1,0:T(8,128)(2,1)S(1)}, bf16[384,1152]{1,0:T(8,128)(2,1)S(1)}, u32[]{:S(2)}, u32[]{:S(2)}) collective-permute-start(bf16[384,1152]{1,0:T(8,128)(2,1)S(1)} %others.1.refs_1_), channel_id=1, source_target_pairs={{0,24},{4,28},{8,16},{12,20},{16,8},{20,12},{24,0},{28,4},{1,25},{... | collective-permute-start | bytes 2654216 | tf_op jit(solution)/shard_map/ppermute | solution.py:339
  207.0 39.9 %collective-permute-start.32 = (bf16[384,1152]{1,0:T(8,128)(2,1)S(1)}, bf16[384,1152]{1,0:T(8,128)(2,1)S(1)}, u32[]{:S(2)}, u32[]{:S(2)}) collective-permute-start(bf16[384,1152]{1,0:T(8,128)(2,1)S(1)} %others.1.refs_1_), channel_id=1, source_target_pairs={{0,16},{4,20},{8,24},{12,28},{16,0},{20,4},{24,8},{28,12},{1,17},{... | collective-permute-start | bytes 2654216 | tf_op jit(solution)/shard_map/ppermute | solution.py:339
  207.5 39.4 %collective-permute-start.27 = (bf16[384,1152]{1,0:T(8,128)(2,1)S(1)}, bf16[384,1152]{1,0:T(8,128)(2,1)S(1)}, u32[]{:S(2)}, u32[]{:S(2)}) collective-permute-start(bf16[384,1152]{1,0:T(8,128)(2,1)S(1)} %others.1.refs_1_), channel_id=1, source_target_pairs={{0,8},{4,12},{8,0},{12,4},{16,24},{20,28},{24,16},{28,20},{1,9},{5... | collective-permute-start | bytes 2654216 | tf_op jit(solution)/shard_map/ppermute | solution.py:339
  208.9 38.5 %collective-permute-start.34 = (bf16[384,1152]{1,0:T(8,128)(2,1)S(1)}, bf16[384,1152]{1,0:T(8,128)(2,1)}, u32[]{:S(2)}, u32[]{:S(2)}) collective-permute-start(bf16[384,1152]{1,0:T(8,128)(2,1)S(1)} %others.1.refs_1_), channel_id=1, source_target_pairs={{0,4},{4,0},{8,12},{12,8},{16,20},{20,16},{24,28},{28,24},{1,5},{5... | collective-permute-start | bytes 2654216 | tf_op jit(solution)/shard_map/ppermute | solution.py:339
  252.2 40.9 %all-to-all-start.3 = ((bf16[8,384,384]{2,1,0:T(8,128)(2,1)}), bf16[8,384,384]{2,1,0:T(8,128)(2,1)S(1)}, u32[]{:S(2)}, u32[]{:S(2)}) async-start(bf16[8,384,384]{2,1,0:T(8,128)(2,1)} %bitcast.25), calls=%async_computation.3 | async-start | bytes 4718592 | tf_op jit(solution)/shard_map/all_to_all | solution.py:1157
  293.2 21.0 %all-to-all-start.4 = ((bf16[8,192,384]{2,1,0:T(8,128)(2,1)}), bf16[8,192,384]{2,1,0:T(8,128)(2,1)S(1)}, u32[]{:S(2)}, u32[]{:S(2)}) async-start(bf16[8,192,384]{2,1,0:T(8,128)(2,1)} %bitcast.28), calls=%async_computation.4 | async-start | bytes 2359296 | tf_op jit(solution)/shard_map/all_to_all | solution.py:1157
  314.1 25.5 %all-to-all-start.5 = ((bf16[8,64,1280]{2,1,0:T(8,128)(2,1)}), bf16[8,64,1280]{2,1,0:T(8,128)(2,1)}, u32[]{:S(2)}, u32[]{:S(2)}) async-start(bf16[8,64,1280]{2,1,0:T(8,128)(2,1)} %bitcast.27), calls=%async_computation.5 | async-start | bytes 2621440 | tf_op jit(solution)/shard_map/all_to_all | solution.py:1157
  339.6 26.2 %all-to-all-start.6 = ((bf16[8,64,1024]{2,1,0:T(8,128)(2,1)}), bf16[8,64,1024]{2,1,0:T(8,128)(2,1)S(1)}, u32[]{:S(2)}, u32[]{:S(2)}) async-start(bf16[8,64,1024]{2,1,0:T(8,128)(2,1)} %bitcast.29), calls=%async_computation.6 | async-start | bytes 2097152 | tf_op jit(solution)/shard_map/all_to_all | solution.py:1157
  343.9 24.3 %collective-permute-start.48 = (bf16[9,16,384]{2,1,0:T(8,128)(2,1)S(1)}, bf16[9,16,384]{2,1,0:T(8,128)(2,1)S(1)}, u32[]{:S(2)}, u32[]{:S(2)}) collective-permute-start(bf16[9,16,384]{2,1,0:T(8,128)(2,1)S(1)} %copy-done.26), channel_id=1, source_target_pairs={{0,1},{1,2},{2,3},{3,0},{4,5},{5,6},{6,7},{7,4},{8,9},{9,10},{10,1... | collective-permute-start | bytes 331784 | tf_op jit(solution)/shard_map/ppermute | solution.py:1163
  346.0 25.5 %collective-permute-start.49 = (bf16[9,16,384]{2,1,0:T(8,128)(2,1)S(1)}, bf16[9,16,384]{2,1,0:T(8,128)(2,1)S(1)}, u32[]{:S(2)}, u32[]{:S(2)}) collective-permute-start(bf16[9,16,384]{2,1,0:T(8,128)(2,1)S(1)} %copy-done.24), channel_id=1, source_target_pairs={{0,2},{1,3},{2,0},{3,1},{4,6},{5,7},{6,4},{7,5},{8,10},{9,11},{10,... | collective-permute-start | bytes 331784 | tf_op jit(solution)/shard_map/ppermute | solution.py:1163
  348.3 23.1 %collective-permute-start.50 = (bf16[9,16,384]{2,1,0:T(8,128)(2,1)S(1)}, bf16[9,16,384]{2,1,0:T(8,128)(2,1)S(1)}, u32[]{:S(2)}, u32[]{:S(2)}) collective-permute-start(bf16[9,16,384]{2,1,0:T(8,128)(2,1)S(1)} %copy-done.22), channel_id=1, source_target_pairs={{0,3},{1,0},{2,1},{3,2},{4,7},{5,4},{6,5},{7,6},{8,11},{9,8},{10,9... | collective-permute-start | bytes 331784 | tf_op jit(solution)/shard_map/ppermute | solution.py:1163
  (78 other events, 601.4 us)

commit v5 on v4

--- a/solution.py
+++ b/solution.py
@@ -523,7 +523,7 @@
     pltpu.make_async_copy(src, dst, sem).start()
 
 
-def own_pieces(ids, in_shard, out_shard, gate_shard, up_shard, down_shard, dps):
+def own_pieces(ids, in_shard, out_shard, gate_shard, up_shard, down_shard, dps, parts):
     d = in_shard.shape[0]
     pr = d // dps
     quarter = gate_shard.shape[1]
@@ -531,15 +531,14 @@
     dr = 4 * width // dps
     per = width // dr
     h_i, h_o, h_d = in_shard.shape[1], out_shard.shape[1], down_shard.shape[1]
-    copies = [1] * (PARTS - 1) + [lax.axis_size("group")]
-    shapes = [(pr, h_i + h_o + 3 * width), (pr, 3 * width), (copies[-1] * pr, 3 * width)]
+    copies = [lax.axis_size("group") if j else 1 for j in range(PARTS)]
+    shapes = [(copies[j] * pr, 3 * width if j else h_i + h_o + 3 * width) for j in parts]
 
     def kernel(ids_ref, in_ref, out_ref, gate_ref, up_ref, down_ref, *rest):
         outs, sems = rest[:-1], rest[-1]
         s = ids_ref[0]
         mine = pl.ds(pl.multiple_of(s * pr, pr), pr)
-        for j in range(PARTS):
-            dst = outs[j]
+        for j, dst in zip(parts, outs):
             at = 0
 
             def put(src, r0=0, n=pr, width_=None):
@@ -563,7 +562,7 @@
             half = dr - pr
             put(down_ref.at[pl.ds(top + pr, half), : width - h_d], n=half, width_=width - h_d)
             put(down_ref.at[pl.ds(top + pr, half), width - h_d :], r0=half, n=half, width_=width - h_d)
-        for j, dst in enumerate(outs):
+        for j, dst in zip(parts, outs):
             pltpu.make_async_copy(dst, dst, sems.at[j]).wait()
 
     return pl.pallas_call(
@@ -571,9 +570,9 @@
         name="own",
         out_shape=[sds(v, bf16) for v in shapes],
         in_specs=[smem_spec()] + [hbm_spec()] * 5,
-        out_specs=[vmem_spec()] * PARTS,
+        out_specs=[vmem_spec()] * len(parts),
         scratch_shapes=[pltpu.SemaphoreType.DMA((PARTS,))],
-        compiler_params=pltpu.CompilerParams(vmem_limit_bytes=6 * 2**20),
+        compiler_params=params(),
     )(ids, in_shard, out_shard, gate_shard, up_shard, down_shard)
 
 
@@ -656,7 +655,7 @@
     )(ids, *pieces, in_shard, x, gain1, taps, sel2, m1, m2, a_in, b_in)
 
 
-def join_call(ids, pieces, relay, out_shard, y, x, gain2, sel2, a_out, b_out, a_gate, a_up):
+def join_call(ids, pieces, relay, out_shard, y, x, dy, gain2, sel2, a_out, b_out, a_gate, a_up, b_down):
     rows, d = x.shape
     table = piece_table(relay)
     n_pieces = len(pieces)
@@ -667,17 +666,22 @@
     def kernel(*refs):
         ids_ref = refs[0]
         p_refs = refs[1 : 1 + n_pieces]
-        (out_ref, x_hbm, y_ref, g2_ref, sel_ref, a_out_ref, b_out_ref, a_gate_ref, a_up_ref) = refs[
-            1 + n_pieces : 10 + n_pieces
+        (out_ref, x_hbm, dy_hbm, y_ref, g2_ref, sel_ref, a_out_ref, b_out_ref, a_gate_ref, a_up_ref, b_down_ref) = refs[
+            1 + n_pieces : 12 + n_pieces
         ]
-        (zout_ref, hb_ref, n2_ref, zgu_ref, w_out_hbm, x_ref, h_ref, w_out, sem_out, sems) = refs[10 + n_pieces :]
+        (zout_ref, hb_ref, n2_ref, zgu_ref, dzd_ref, w_out_hbm, x_ref, dy_ref, h_ref, w_out, sem_out, sems) = refs[
+            12 + n_pieces :
+        ]
         gather_copies(ids_ref, p_refs, table, pr, w_out, sem_out, out_ref, lo)
-        [wait_x] = fetched([(x_hbm, x_ref)], sems)
+        wait_x, wait_dy = fetched([(x_hbm, x_ref), (dy_hbm, dy_ref)], sems)
         sel = sel_ref[...]
         zout_ref[...] = nn(y_ref[...], a_out_ref[...]).astype(bf16) * sel
         wait_x()
         pltpu.make_async_copy(w_out, w_out, sem_out).wait()
-        [wait_store] = fetched([(w_out, w_out_hbm)], sems)
+        store = pltpu.make_async_copy(w_out, w_out_hbm, sems.at[2])
+        store.start()
+        wait_dy()
+        dzd_ref[...] = (nt(dy_ref[...], b_down_ref[...]) * sel.astype(f32)).astype(bf16)
 
         def mid(j):
             o = nn(y_ref[...], w_out[:, col(j)]) + nn(zout_ref[...], b_out_ref[:, col(j)])
@@ -695,24 +699,24 @@
         loop(rows // ROWS, norm2)
         zgu_ref[:, :c] = nn(n2_ref[...], a_gate_ref[...]).astype(bf16) * sel
         zgu_ref[:, c:] = nn(n2_ref[...], a_up_ref[...]).astype(bf16) * sel
-        wait_store()
+        store.wait()
 
     return pl.pallas_call(
         kernel,
         name="join",
         out_shape=[
             sds((rows, c), bf16), sds((rows, d), bf16), sds((rows, d), bf16), sds((rows, 2 * c), bf16),
-            sds((d, d), bf16),
+            sds((rows, c), bf16), sds((d, d), bf16),
         ],
-        in_specs=[smem_spec()] + [any_spec()] * (n_pieces + 2) + [vmem_spec()] * 7,
-        out_specs=[vmem_spec()] * 4 + [any_spec()],
+        in_specs=[smem_spec()] + [any_spec()] * (n_pieces + 3) + [vmem_spec()] * 8,
+        out_specs=[vmem_spec()] * 5 + [any_spec()],
         scratch_shapes=[
-            pltpu.VMEM((rows, d), bf16), pltpu.VMEM((rows, d), f32), pltpu.VMEM((d, d), bf16),
-            pltpu.SemaphoreType.DMA, pltpu.SemaphoreType.DMA((1,)),
+            pltpu.VMEM((rows, d), bf16), pltpu.VMEM((rows, d), bf16), pltpu.VMEM((rows, d), f32), pltpu.VMEM((d, d), bf16),
+            pltpu.SemaphoreType.DMA, pltpu.SemaphoreType.DMA((3,)),
         ],
         compiler_params=params(),
         cost_estimate=cost(2.6 * rows * d * d),
-    )(ids, *pieces, out_shard, x, y, gain2, sel2, a_out, b_out, a_gate, a_up)
+    )(ids, *pieces, out_shard, x, dy, y, gain2, sel2, a_out, b_out, a_gate, a_up, b_down)
 
 
 def ffn_call(part, ids, pieces, relay, gate_shard, up_shard, down_shard, n2, dy, zgu, dzd,
@@ -1193,34 +1197,39 @@
         lengths[:, 0, :][s], adapter_ids[:, 0, :][s], rows, a_in.shape[1], ADAPTER_RANK
     )
     sel2 = sel * adapter_scale
-    packed = own_pieces(ids, in_weight, out_weight, gate_weight, up_weight, down_weight, dp_count)
+    shards = (in_weight, out_weight, gate_weight, up_weight, down_weight)
+    packed = own_pieces(ids, *shards, dp_count, (0,))
+    packed = [*packed, *own_pieces(after(ids, packed[0]), *shards, dp_count, tuple(range(1, PARTS)))]
     arrived = lax.all_to_all(cotangent, "dp", split_axis=0, concat_axis=0, tiled=True)
     io_width = in_weight.shape[1] + out_weight.shape[1]
     zs_io, *zs = from_planes(packed[0], [io_width, 3 * width])
     near_io = [swap_dp(zs_io, X_BIT), swap_dp(zs_io, Y_BIT)]
     near_io += far(*near_io, 1)
-    zs += from_planes(after(packed[1], zs_io), [3 * width])
     io = [zs_io, *near_io]
     io = io + core_copies(io)
     dy = lax.all_to_all(
-        picked(arrived, after(inverse_row, packed[0], sel2, after_one, after_two), dp_count), "dp", split_axis=0, concat_axis=0,
+        picked(arrived, after(inverse_row, packed[1], sel2, after_one, after_two), dp_count), "dp", split_axis=0, concat_axis=0,
         tiled=True,
     )
 
     gain1 = norm_gain[None, :]
     gain2 = ffn_gain[None, :]
+    groups = lax.axis_size("group")
+
+    def over_planes(pieces):
+        return others(ids, exchange(pieces.reshape(groups, -1, 3 * width), "group"))
+
+    zs.append(over_planes(after(packed[1], *near_io)))
     first = after(zs[0], dy, *near_io)
     nears = [swap_dp(first, X_BIT), swap_dp(first, Y_BIT)]
     n1, zin, mix, cv, y, w_in = front_call(
         after(ids, dy, zs[0]), io, 1, in_weight, tokens, gain1, conv_weight, sel2, after_one, after_two, a_in, b_in,
     )
     nears += far(*[after(v, zin) for v in nears], 2)
-    groups = lax.axis_size("group")
-    zs.append(others(ids, exchange(after(packed[2], zin).reshape(groups, -1, 3 * width), "group")))
-    zout, h, n2, zgu, w_out = join_call(
-        ids, io, 1, out_weight, y, tokens, gain2, sel2, a_out, b_out, a_gate, a_up,
-    )
-    dzd = (nt(dy, b_down) * sel2.astype(f32)).astype(bf16)
+    zs.append(over_planes(after(packed[2], zin, zs[1])))
+    zout, h, n2, zgu, dzd, w_out = join_call(
+        ids, io, 1, out_weight, y, tokens, dy, gain2, sel2, a_out, b_out, a_gate, a_up, b_down,
+    )
     state = (h,)
     previous = n2
     grads = []
@@ -1230,7 +1239,7 @@
         if j + 1 < PARTS:
             nears = near(after(zs[j + 1], previous, *nears))
         if j == PARTS - 1:
-            early = exchange(after(grads[-1], *arrays), "dp")
+            early = exchange(after(grads[-1], *nears), "dp")
         *state, g = ffn_call(
             j, after(ids, *zs[j + 1 : j + 2]), arrays, 2 if j == 0 else None, gate_weight, up_weight,
             down_weight, n2, dy, zgu, dzd, b_gate, b_up, a_down, grads[0] if j == 1 else None, *state,

time: 399 us -> 396 us (level)
  Pallas kernels: 198 us -> 208 us
  local copies, waits for them, and re-layouts: 18.7 us -> 10.6 us
  starting transfers between devices: 87.7 us -> 82.1 us
    unnamed x90 -> x64, local copies, waits for them, and re-layouts: 14.6 us -> 6.47 us
    ppermute x6 -> x3, starting transfers between devices: 13.2 us -> 5.57 us  [from_planes(): lax.ppermute(joined, 'group', [(i, (i + t) % groups) for i in range(group...]
    ppermute x46, waiting for transfers between devices: 50.9 us -> 57.7 us  [swap_dp(): lax.ppermute(values, 'dp', [(i, i ^ bit) for i in range(lax.axis_size('dp...]
    pallas_call x1 -> x2, Pallas kernels: 0.84 us -> 6.81 us  [own_pieces(): pl.pallas_call(kernel, name='own', out_shape=[sds(v, bf16) for v in shape...]
    all_to_all x5 -> x6, starting transfers between devices: 24 us -> 28.1 us  [exchange(): lax.all_to_all(flat, axis, split_axis=0, concat_axis=0, tiled=True)]
    ppermute x6 -> x3, waiting for transfers between devices: 14.4 us -> 11.4 us  [from_planes(): lax.ppermute(joined, 'group', [(i, (i + t) % groups) for i in range(group...]
  transfers between devices with their start and end apart: 65 -> 63, of which waited for: 17 -> 18; matrix products, arithmetic and copies ran while one was open for 2% -> 2% of each run, Pallas kernels for 50% -> 53%
where the time goes in v5:
time: 396 us; the launch traced here: 389 us
  Pallas kernels  208 us (53%)
  waiting for transfers between devices  82.5 us (21%)
  starting transfers between devices  82.1 us (21%)
  local copies, waits for them, and re-layouts  10.6 us (3%)
  other arithmetic  4.03 us (1%)
    pallas_call x3, Pallas kernels, ffn_call(): pl.pallas_call(kernel, name=f'ffn{part}', out_shape=[sds(*v) for v in sta...  111 us
    ppermute x46, waiting for transfers between devices, swap_dp(): lax.ppermute(values, 'dp', [(i, i ^ bit) for i in range(lax.axis_size('dp...  57.7 us
    ppermute x46, starting transfers between devices, swap_dp(): lax.ppermute(values, 'dp', [(i, i ^ bit) for i in range(lax.axis_size('dp...  29.1 us
    all_to_all x6, starting transfers between devices, exchange(): lax.all_to_all(flat, axis, split_axis=0, concat_axis=0, tiled=True)  28.1 us
    pallas_call x1, Pallas kernels, front_call(): pl.pallas_call(kernel, name='front', out_shape=[sds(wide[0], bf16), sds((...  17.4 us
    pallas_call x1, Pallas kernels, back_call(): pl.pallas_call(kernel, name='back', out_shape=[sds((rows, 3 * d), bf16),...  17.3 us
    pallas_call x1, Pallas kernels, last_call(): pl.pallas_call(kernel, name='last', out_shape=sds((rows, d), bf16), in_sp...  16.1 us
    pallas_call x1, Pallas kernels, join_call(): pl.pallas_call(kernel, name='join', out_shape=[sds((rows, c), bf16), sds(...  14.3 us
  transfers between devices with their start and end apart: 63, of which 18 were waited for; matrix products, arithmetic and copies ran while one was open for 2% of the time, Pallas kernels for 53%

profile of v5, /device:TPU:0, one launch (start us, length us, event | category | flops | bytes accessed | tf_op | source)
XLA Modules:
  0.0 388.8 jit_solution(11748200947825004901)
XLA Ops:
  0.6 5.2 %all-to-all-start = ((bf16[8,128,1024]{2,1,0:T(8,128)(2,1)}), bf16[8,128,1024]{2,1,0:T(8,128)(2,1)S(1)}, u32[]{:S(2)}, u32[]{:S(2)}) async-start(bf16[8,128,1024]{2,1,0:T(8,128)(2,1)} %bitcast.26), calls=%async_computation | async-start | bytes 4194304 | tf_op jit(solution)/shard_map/all_to_all | solution.py:1203
  6.4 2.7 own.2
  10.8 2.6 collective-permute-start.1
  17.1 2.1 compare_convert_fusion
  19.3 4.1 %own.3 = (bf16[512,1152]{1,0:T(8,128)(2,1)}, bf16[512,1152]{1,0:T(8,128)(2,1)}) custom-call(s32[2]{0:T(128)} %pad_add_fusion.ids_ref.refs_0_, bf16[1024,768]{1,0:T(8,128)(2,1)} %refs_11_.5, bf16[1024,256]{1,0:T(8,128)(2,1)} %refs_11_.6, bf16[1024,1152]{1,0:T(8,128)(2,1)} %refs_9_.3, bf16[1024,1152]{1,0:T(8,128)(2,1)} %refs_10_.3, bf16[4608,256]{1,0:T(8,128)(2,1)} %refs_11_.9), custom_call_target="tpu_custom_call" | custom-call | tf_op jit(solution)/shard_map/own/pallas_call | solution.py:568
  23.4 9.1 %all-to-all-done = bf16[8,128,1024]{2,1,0:T(8,128)(2,1)S(1)} async-done(((bf16[8,128,1024]{2,1,0:T(8,128)(2,1)}), bf16[8,128,1024]{2,1,0:T(8,128)(2,1)S(1)}, u32[]{:S(2)}, u32[]{:S(2)}) %all-to-all-start) | async-done | bytes 2097184 | tf_op jit(solution)/shard_map/all_to_all | solution.py:1203
  34.5 4.4 %all-to-all-start.1 = ((bf16[8,128,1024]{2,1,0:T(8,128)(2,1)}), bf16[8,128,1024]{2,1,0:T(8,128)(2,1)}, u32[]{:S(2)}, u32[]{:S(2)}) async-start(bf16[8,128,1024]{2,1,0:T(8,128)(2,1)} %bitcast.22), calls=%async_computation.1 | async-start | bytes 4194304 | tf_op jit(solution)/shard_map/all_to_all | solution.py:1210
  38.9 11.4 %collective-permute-done.1.refs_1_ = bf16[128,2176]{1,0:T(8,128)(2,1)S(1)} collective-permute-done((bf16[128,2176]{1,0:T(8,128)(2,1)}, bf16[128,2176]{1,0:T(8,128)(2,1)S(1)}, u32[]{:S(2)}, u32[]{:S(2)}) %collective-permute-start.1) | collective-permute-done | bytes 557088 | tf_op jit(solution)/shard_map/ppermute | solution.py:440
  54.5 26.8 %collective-permute-done.4.refs_3_ = bf16[384,1024]{1,0:T(8,128)(2,1)S(1)} collective-permute-done((bf16[384,1024]{1,0:T(8,128)(2,1)S(1)}, bf16[384,1024]{1,0:T(8,128)(2,1)S(1)}, u32[]{:S(2)}, u32[]{:S(2)}) %collective-permute-start.4) | collective-permute-done | bytes 786464 | tf_op jit(solution)/shard_map/ppermute | solution.py:339
  84.2 7.7 %collective-permute-done.5.refs_4_ = bf16[128,1024]{1,0:T(8,128)(2,1)S(1)} collective-permute-done((bf16[128,1024]{1,0:T(8,128)(2,1)S(1)}, bf16[128,1024]{1,0:T(8,128)(2,1)S(1)}, u32[]{:S(2)}, u32[]{:S(2)}) %collective-permute-start.5) | collective-permute-done | bytes 262176 | tf_op jit(solution)/shard_map/ppermute | solution.py:339
  91.8 3.4 collective-permute-done.6.refs_5_
  95.2 6.1 %all-to-all-start.2 = ((bf16[4,128,1152]{2,1,0:T(8,128)(2,1)}), bf16[4,128,1152]{2,1,0:T(8,128)(2,1)S(1)}, u32[]{:S(2)}, u32[]{:S(2)}) async-start(bf16[4,128,1152]{2,1,0:T(8,128)(2,1)} %bitcast.28), calls=%async_computation.2 | async-start | bytes 2359296 | tf_op jit(solution)/shard_map/all_to_all | solution.py:1161
  104.4 3.1 collective-permute-done.10.refs_9_
  110.4 17.4 %front.1 = (bf16[1024,1024]{1,0:T(8,128)(2,1)}, bf16[1024,128]{1,0:T(8,128)(2,1)}, bf16[1024,3072]{1,0:T(8,128)(2,1)}, bf16[1024,1024]{1,0:T(8,128)(2,1)}, bf16[...) custom-call(s32[2]{0:T(128)} %pad_add_fusion.ids_ref.refs_0_, bf16[384,1024]{1,0:T(8,128)(2,1)} %copy-done.1, ...), custom_call_target="tpu_custom_call" | custom-call | flops 2044723 | tf_op jit(solution)/shard_map/front/pallas_call | solution.py:645
  132.7 14.3 %join.1 = (bf16[1024,128]{1,0:T(8,128)(2,1)}, bf16[1024,1024]{1,0:T(8,128)(2,1)}, bf16[1024,1024]{1,0:T(8,128)(2,1)}, bf16[1024,256]{1,0:T(8,128)(2,1)}, bf16[10...) custom-call(s32[2]{0:T(128)} %pad_add_fusion.ids_ref.refs_0_, bf16[384,1024]{1,0:T(8,128)(2,1)} %copy-done.1, ...), custom_call_target="tpu_custom_call" | custom-call | flops 681574 | tf_op jit(solution)/shard_map/join/pallas_call | solution.py:704
  148.4 5.3 %all-to-all-start.3 = ((bf16[4,128,1152]{2,1,0:T(8,128)(2,1)}), bf16[4,128,1152]{2,1,0:T(8,128)(2,1)S(1)}, u32[]{:S(2)}, u32[]{:S(2)}) async-start(bf16[4,128,1152]{2,1,0:T(8,128)(2,1)} %bitcast.10), calls=%async_computation.3 | async-start | bytes 2359296 | tf_op jit(solution)/shard_map/all_to_all | solution.py:1161
  160.6 37.0 %ffn0.1 = (bf16[1024,1024]{1,0:T(8,128)(2,1)}, bf16[1024,1024]{1,0:T(8,128)(2,1)}, f32[1024,256]{1,0:T(8,128)}, f32[1024,128]{1,0:T(8,128)}, bf16[8,4,3,16,384]{4,3,2,1,0:T(8,128)(2,1)}) custom-call(s32[2]{0:T(128)} %pad_add_fusion.ids_ref.refs_0_, bf16[384,1152]{1,0:T(8,128)(2,1)} %stacked.2.refs_1_, bf16[384,1152]{1,0:T(8,128)(2,1)} %collective-permute-done.12.refs_2_, ...), custom_call_target="tpu_custom_call" | custom-call | flops 6134169 | tf_op jit(solution)/shard_map/ffn0/pallas_call | solution.py:893
  203.6 37.3 %ffn1.1 = (bf16[1024,1024]{1,0:T(8,128)(2,1)}, bf16[1024,1024]{1,0:T(8,128)(2,1)}, f32[1024,256]{1,0:T(8,128)}, f32[1024,128]{1,0:T(8,128)}, bf16[8,4,6,16,384]{4,3,2,1,0:T(8,128)(2,1)}) custom-call(s32[2]{0:T(128)} %pad_add_fusion.ids_ref.refs_0_, bf16[384,1152]{1,0:T(8,128)(2,1)} %copy-done.2, bf16[384,1152]{1,0:T(8,128)(2,1)} %collective-permute-done.21.refs_2_, ...), custom_call_target="tpu_custom_call" | custom-call | flops 6134169 | tf_op jit(solution)/shard_map/ffn1/pallas_call | solution.py:893
  242.5 4.1 %all-to-all-start.4 = ((bf16[8,384,384]{2,1,0:T(8,128)(2,1)}), bf16[8,384,384]{2,1,0:T(8,128)(2,1)S(1)}, u32[]{:S(2)}, u32[]{:S(2)}) async-start(bf16[8,384,384]{2,1,0:T(8,128)(2,1)} %bitcast.25), calls=%async_computation.4 | async-start | bytes 4718592 | tf_op jit(solution)/shard_map/all_to_all | solution.py:1161
  247.7 2.2 collective-permute-done.31.refs_5_
  253.4 37.0 %ffn2.1 = (bf16[1024,1024]{1,0:T(8,128)(2,1)}, bf16[1024,1024]{1,0:T(8,128)(2,1)}, f32[1024,256]{1,0:T(8,128)}, f32[1024,128]{1,0:T(8,128)}, bf16[8,4,3,16,384]{4,3,2,1,0:T(8,128)(2,1)}) custom-call(s32[2]{0:T(128)} %pad_add_fusion.ids_ref.refs_0_, bf16[384,1152]{1,0:T(8,128)(2,1)} %others.3.refs_1_, bf16[384,1152]{1,0:T(8,128)(2,1)} %copy-done.24, ...), custom_call_target="tpu_custom_call" | custom-call | flops 6134169 | tf_op jit(solution)/shard_map/ffn2/pallas_call | solution.py:893
  290.5 4.1 %all-to-all-start.5 = ((bf16[8,192,384]{2,1,0:T(8,128)(2,1)}), bf16[8,192,384]{2,1,0:T(8,128)(2,1)S(1)}, u32[]{:S(2)}, u32[]{:S(2)}) async-start(bf16[8,192,384]{2,1,0:T(8,128)(2,1)} %bitcast.29), calls=%async_computation.5 | async-start | bytes 2359296 | tf_op jit(solution)/shard_map/all_to_all | solution.py:1161
  294.6 12.4 %middle.1 = (bf16[1024,1024]{1,0:T(8,128)(2,1)}, bf16[1024,1024]{1,0:T(8,128)(2,1)}, bf16[1024,128]{1,0:T(8,128)(2,1)}, bf16[8,4,16,1280]{3,2,1,0:T(8,128)(2,1)}) custom-call(bf16[1024,1024]{1,0:T(8,128)(2,1)} %get-tuple-element.135.dn_hbm, bf16[1024,1024]{1,0:T(8,128)(2,1)} %get-tuple-element.107.refs_17_.refs_15_.n2_hbm, ...), custom_call_target="tpu_custom_call" | custom-call | flops 2097152 | tf_op jit(solution)/shard_map/middle/pallas_call | solution.py:984
  307.1 4.3 %all-to-all-done.5 = bf16[8,192,384]{2,1,0:T(8,128)(2,1)S(1)} async-done(((bf16[8,192,384]{2,1,0:T(8,128)(2,1)}), bf16[8,192,384]{2,1,0:T(8,128)(2,1)S(1)}, u32[]{:S(2)}, u32[]{:S(2)}) %all-to-all-start.5) | async-done | bytes 1179680 | tf_op jit(solution)/shard_map/all_to_all | solution.py:1161
  311.4 4.3 %all-to-all-start.6 = ((bf16[8,64,1280]{2,1,0:T(8,128)(2,1)}), bf16[8,64,1280]{2,1,0:T(8,128)(2,1)}, u32[]{:S(2)}, u32[]{:S(2)}) async-start(bf16[8,64,1280]{2,1,0:T(8,128)(2,1)} %bitcast.27), calls=%async_computation.6 | async-start | bytes 2621440 | tf_op jit(solution)/shard_map/all_to_all | solution.py:1161
  319.3 17.3 %back.1 = (bf16[1024,3072]{1,0:T(8,128)(2,1)}, bf16[1024,128]{1,0:T(8,128)(2,1)}, bf16[8,4,16,1024]{3,2,1,0:T(8,128)(2,1)}) custom-call(bf16[1024,1024]{1,0:T(8,128)(2,1)} %get-tuple-element.144.w_out_hbm, bf16[1024,1024]{1,0:T(8,128)(2,1)} %get-tuple-element.145.dhb_hbm.dh_hbm, bf16[1024,1024]{1,0:T(8,128)(2,1)} %get-tuple-element.146.cv_hbm, ...), custom_call_target="tpu_custom_call" | custom-call | flops 2097152 | tf_op jit(solution)/shard_map/back/pallas_call | solution.py:1043
  336.6 4.3 %all-to-all-start.7 = ((bf16[8,64,1024]{2,1,0:T(8,128)(2,1)}), bf16[8,64,1024]{2,1,0:T(8,128)(2,1)S(1)}, u32[]{:S(2)}, u32[]{:S(2)}) async-start(bf16[8,64,1024]{2,1,0:T(8,128)(2,1)} %bitcast.30), calls=%async_computation.7 | async-start | bytes 2097152 | tf_op jit(solution)/shard_map/all_to_all | solution.py:1161
  340.9 2.1 collective-permute-start.45
  342.9 2.4 collective-permute-start.46
  346.8 16.1 %last.1 = bf16[1024,1024]{1,0:T(8,128)(2,1)} custom-call(bf16[1024,3072]{1,0:T(8,128)(2,1)} %get-tuple-element.154.dp_hbm, bf16[1024,3072]{1,0:T(8,128)(2,1)} %get-tuple-element.155.w_in_hbm, bf16[1024,1024]{1,0:T(8,128)(2,1)} %get-tuple-element.145.dhb_hbm.dh_hbm, bf16[1024,1024]{1,0:T(8,128)(2,1)} %x_hbm.1, bf16[1024,128]{1,0:T(8,128)(2,1)} %get-tuple-element.156.dzi_ref, ...), custom_call_target="tpu_custom_call" | custom-call | flops 2097152 | tf_op jit(solution)/shard_map/last/pallas_call | solution.py:1090
  365.7 2.7 collective-permute-start.37
  372.0 2.4 collective-permute-start.50
  (193 shorter events, 72.0 us)
Async XLA Ops:
  0.6 31.8 %all-to-all-start = ((bf16[8,128,1024]{2,1,0:T(8,128)(2,1)}), bf16[8,128,1024]{2,1,0:T(8,128)(2,1)S(1)}, u32[]{:S(2)}, u32[]{:S(2)}) async-start(bf16[8,128,1024]{2,1,0:T(8,128)(2,1)} %bitcast.26), calls=%async_computation | async-start | bytes 4194304 | tf_op jit(solution)/shard_map/all_to_all | solution.py:1203
  9.1 29.8 %collective-permute-start = (bf16[128,2176]{1,0:T(8,128)(2,1)}, bf16[128,2176]{1,0:T(8,128)(2,1)S(1)}, u32[]{:S(2)}, u32[]{:S(2)}) collective-permute-start(bf16[128,2176]{1,0:T(8,128)(2,1)} %own.2), channel_id=1, source_target_pairs={{0,1},{1,2},{2,3},{3,0},{4,5},{5,6},{6,7},{7,4},{8,9},{9,10},{10,1... | collective-permute-start | bytes 1671176 | tf_op jit(solution)/shard_map/ppermute | solution.py:440
  10.8 39.5 %collective-permute-start.1 = (bf16[128,2176]{1,0:T(8,128)(2,1)}, bf16[128,2176]{1,0:T(8,128)(2,1)S(1)}, u32[]{:S(2)}, u32[]{:S(2)}) collective-permute-start(bf16[128,2176]{1,0:T(8,128)(2,1)} %own.2), channel_id=1, source_target_pairs={{0,2},{1,3},{2,0},{3,1},{4,6},{5,7},{6,4},{7,5},{8,10},{9,11},{10,... | collective-permute-start | bytes 1671176 | tf_op jit(solution)/shard_map/ppermute | solution.py:440
  13.3 36.9 %collective-permute-start.2 = (bf16[128,2176]{1,0:T(8,128)(2,1)}, bf16[128,2176]{1,0:T(8,128)(2,1)}, u32[]{:S(2)}, u32[]{:S(2)}) collective-permute-start(bf16[128,2176]{1,0:T(8,128)(2,1)} %own.2), channel_id=1, source_target_pairs={{0,3},{1,0},{2,1},{3,2},{4,7},{5,4},{6,5},{7,6},{8,11},{9,8},{10,9... | collective-permute-start | bytes 1671176 | tf_op jit(solution)/shard_map/ppermute | solution.py:440
  34.5 60.6 %all-to-all-start.1 = ((bf16[8,128,1024]{2,1,0:T(8,128)(2,1)}), bf16[8,128,1024]{2,1,0:T(8,128)(2,1)}, u32[]{:S(2)}, u32[]{:S(2)}) async-start(bf16[8,128,1024]{2,1,0:T(8,128)(2,1)} %bitcast.22), calls=%async_computation.1 | async-start | bytes 4194304 | tf_op jit(solution)/shard_map/all_to_all | solution.py:1210
  51.3 30.0 %collective-permute-start.4 = (bf16[384,1024]{1,0:T(8,128)(2,1)S(1)}, bf16[384,1024]{1,0:T(8,128)(2,1)S(1)}, u32[]{:S(2)}, u32[]{:S(2)}) collective-permute-start(bf16[384,1024]{1,0:T(8,128)(2,1)S(1)} %stacked.3.refs_1_), channel_id=1, source_target_pairs={{0,16},{4,20},{8,24},{12,28},{16,0},{20,4},{24,8},{28,12},{1,17},{... | collective-permute-start | bytes 2359304 | tf_op jit(solution)/shard_map/ppermute | solution.py:339
  53.1 29.8 %collective-permute-start.3 = (bf16[384,1024]{1,0:T(8,128)(2,1)S(1)}, bf16[384,1024]{1,0:T(8,128)(2,1)S(1)}, u32[]{:S(2)}, u32[]{:S(2)}) collective-permute-start(bf16[384,1024]{1,0:T(8,128)(2,1)S(1)} %stacked.3.refs_1_), channel_id=1, source_target_pairs={{0,8},{4,12},{8,0},{12,4},{16,24},{20,28},{24,16},{28,20},{1,9},{5... | collective-permute-start | bytes 2359304 | tf_op jit(solution)/shard_map/ppermute | solution.py:339
  81.4 13.8 %collective-permute-start.6 = (bf16[256,1024]{1,0:T(8,128)(2,1)S(1)}, bf16[256,1024]{1,0:T(8,128)(2,1)}, u32[]{:S(2)}, u32[]{:S(2)}) collective-permute-start(bf16[256,1024]{1,0:T(8,128)(2,1)S(1)} %slice.17), channel_id=1, source_target_pairs={{0,8},{4,12},{8,0},{12,4},{16,24},{20,28},{24,16},{28,20},{1,9},{5... | collective-permute-start | bytes 1572872 | tf_op jit(solution)/shard_map/ppermute | solution.py:339
  84.2 20.1 %collective-permute-start.7 = (bf16[384,1024]{1,0:T(8,128)(2,1)S(1)}, bf16[384,1024]{1,0:T(8,128)(2,1)}, u32[]{:S(2)}, u32[]{:S(2)}) collective-permute-start(bf16[384,1024]{1,0:T(8,128)(2,1)S(1)} %stacked.3.refs_1_), channel_id=1, source_target_pairs={{0,4},{4,0},{8,12},{12,8},{16,20},{20,16},{24,28},{28,24},{1,5},{5... | collective-permute-start | bytes 2359304 | tf_op jit(solution)/shard_map/ppermute | solution.py:339
  95.2 52.4 %all-to-all-start.2 = ((bf16[4,128,1152]{2,1,0:T(8,128)(2,1)}), bf16[4,128,1152]{2,1,0:T(8,128)(2,1)S(1)}, u32[]{:S(2)}, u32[]{:S(2)}) async-start(bf16[4,128,1152]{2,1,0:T(8,128)(2,1)} %bitcast.28), calls=%async_computation.2 | async-start | bytes 2359296 | tf_op jit(solution)/shard_map/all_to_all | solution.py:1161
  103.3 24.5 %collective-permute-start.12 = (bf16[384,1152]{1,0:T(8,128)(2,1)}, bf16[384,1152]{1,0:T(8,128)(2,1)}, u32[]{:S(2)}, u32[]{:S(2)}) collective-permute-start(bf16[384,1152]{1,0:T(8,128)(2,1)} %stacked.2.refs_1_), channel_id=1, source_target_pairs={{0,8},{4,12},{8,0},{12,4},{16,24},{20,28},{24,16},{28,20},{1,9},{5... | collective-permute-start | bytes 2654216 | tf_op jit(solution)/shard_map/ppermute | solution.py:339
  104.3 25.0 %collective-permute-start.13 = (bf16[384,1152]{1,0:T(8,128)(2,1)}, bf16[384,1152]{1,0:T(8,128)(2,1)}, u32[]{:S(2)}, u32[]{:S(2)}) collective-permute-start(bf16[384,1152]{1,0:T(8,128)(2,1)} %stacked.2.refs_1_), channel_id=1, source_target_pairs={{0,16},{4,20},{8,24},{12,28},{16,0},{20,4},{24,8},{28,12},{1,17},{... | collective-permute-start | bytes 2654216 | tf_op jit(solution)/shard_map/ppermute | solution.py:339
  128.9 24.8 %collective-permute-start.14 = (bf16[256,1152]{1,0:T(8,128)(2,1)S(1)}, bf16[256,1152]{1,0:T(8,128)(2,1)S(1)}, u32[]{:S(2)}, u32[]{:S(2)}) collective-permute-start(bf16[256,1152]{1,0:T(8,128)(2,1)S(1)} %slice.14), channel_id=1, source_target_pairs={{0,16},{4,20},{8,24},{12,28},{16,0},{20,4},{24,8},{28,12},{1,17},{... | collective-permute-start | bytes 1769480 | tf_op jit(solution)/shard_map/ppermute | solution.py:339
  129.1 26.2 %collective-permute-start.16 = (bf16[384,1152]{1,0:T(8,128)(2,1)}, bf16[384,1152]{1,0:T(8,128)(2,1)}, u32[]{:S(2)}, u32[]{:S(2)}) collective-permute-start(bf16[384,1152]{1,0:T(8,128)(2,1)} %stacked.2.refs_1_), channel_id=1, source_target_pairs={{0,4},{4,0},{8,12},{12,8},{16,20},{20,16},{24,28},{28,24},{1,5},{5... | collective-permute-start | bytes 2654216 | tf_op jit(solution)/shard_map/ppermute | solution.py:339
  130.9 22.8 %collective-permute-start.15 = (bf16[128,1152]{1,0:T(8,128)(2,1)}, bf16[128,1152]{1,0:T(8,128)(2,1)}, u32[]{:S(2)}, u32[]{:S(2)}) collective-permute-start(bf16[128,1152]{1,0:T(8,128)(2,1)} %slice.15), channel_id=1, source_target_pairs={{0,8},{4,12},{8,0},{12,4},{16,24},{20,28},{24,16},{28,20},{1,9},{5... | collective-permute-start | bytes 884744 | tf_op jit(solution)/shard_map/ppermute | solution.py:339
  147.0 11.3 %collective-permute-start.18 = (bf16[384,1152]{1,0:T(8,128)(2,1)}, bf16[384,1152]{1,0:T(8,128)(2,1)}, u32[]{:S(2)}, u32[]{:S(2)}) collective-permute-start(bf16[384,1152]{1,0:T(8,128)(2,1)} %collective-permute-done.13.refs_3_), channel_id=1, source_target_pairs={{0,4},{4,0},{8,12},{12,8},{16,20},{20,16},{24,28},{28,24},{1,5},{5... | collective-permute-start | bytes 2654216 | tf_op jit(solution)/shard_map/ppermute | solution.py:339
  147.2 11.1 %collective-permute-start.17 = (bf16[384,1152]{1,0:T(8,128)(2,1)}, bf16[384,1152]{1,0:T(8,128)(2,1)}, u32[]{:S(2)}, u32[]{:S(2)}) collective-permute-start(bf16[384,1152]{1,0:T(8,128)(2,1)} %collective-permute-done.12.refs_2_), channel_id=1, source_target_pairs={{0,4},{4,0},{8,12},{12,8},{16,20},{20,16},{24,28},{28,24},{1,5},{5... | collective-permute-start | bytes 2654216 | tf_op jit(solution)/shard_map/ppermute | solution.py:339
  148.4 50.0 %all-to-all-start.3 = ((bf16[4,128,1152]{2,1,0:T(8,128)(2,1)}), bf16[4,128,1152]{2,1,0:T(8,128)(2,1)S(1)}, u32[]{:S(2)}, u32[]{:S(2)}) async-start(bf16[4,128,1152]{2,1,0:T(8,128)(2,1)} %bitcast.10), calls=%async_computation.3 | async-start | bytes 2359296 | tf_op jit(solution)/shard_map/all_to_all | solution.py:1161
  153.7 43.9 %collective-permute-start.23 = (bf16[384,1152]{1,0:T(8,128)(2,1)S(1)}, bf16[384,1152]{1,0:T(8,128)(2,1)S(1)}, u32[]{:S(2)}, u32[]{:S(2)}) collective-permute-start(bf16[384,1152]{1,0:T(8,128)(2,1)S(1)} %others.2.refs_1_), channel_id=1, source_target_pairs={{0,24},{4,28},{8,16},{12,20},{16,8},{20,12},{24,0},{28,4},{1,25},{... | collective-permute-start | bytes 2654216 | tf_op jit(solution)/shard_map/ppermute | solution.py:339
  157.6 40.2 %collective-permute-start.22 = (bf16[384,1152]{1,0:T(8,128)(2,1)S(1)}, bf16[384,1152]{1,0:T(8,128)(2,1)}, u32[]{:S(2)}, u32[]{:S(2)}) collective-permute-start(bf16[384,1152]{1,0:T(8,128)(2,1)S(1)} %others.2.refs_1_), channel_id=1, source_target_pairs={{0,16},{4,20},{8,24},{12,28},{16,0},{20,4},{24,8},{28,12},{1,17},{... | collective-permute-start | bytes 2654216 | tf_op jit(solution)/shard_map/ppermute | solution.py:339
  158.3 42.5 %collective-permute-start.25 = (bf16[384,1152]{1,0:T(8,128)(2,1)S(1)}, bf16[384,1152]{1,0:T(8,128)(2,1)}, u32[]{:S(2)}, u32[]{:S(2)}) collective-permute-start(bf16[384,1152]{1,0:T(8,128)(2,1)S(1)} %others.2.refs_1_), channel_id=1, source_target_pairs={{0,4},{4,0},{8,12},{12,8},{16,20},{20,16},{24,28},{28,24},{1,5},{5... | collective-permute-start | bytes 2654216 | tf_op jit(solution)/shard_map/ppermute | solution.py:339
  158.3 39.9 %collective-permute-start.21 = (bf16[384,1152]{1,0:T(8,128)(2,1)S(1)}, bf16[384,1152]{1,0:T(8,128)(2,1)}, u32[]{:S(2)}, u32[]{:S(2)}) collective-permute-start(bf16[384,1152]{1,0:T(8,128)(2,1)S(1)} %others.2.refs_1_), channel_id=1, source_target_pairs={{0,8},{4,12},{8,0},{12,4},{16,24},{20,28},{24,16},{28,20},{1,9},{5... | collective-permute-start | bytes 2654216 | tf_op jit(solution)/shard_map/ppermute | solution.py:339
  200.0 40.9 %collective-permute-start.24 = (bf16[384,1152]{1,0:T(8,128)(2,1)}, bf16[384,1152]{1,0:T(8,128)(2,1)S(1)}, u32[]{:S(2)}, u32[]{:S(2)}) collective-permute-start(bf16[384,1152]{1,0:T(8,128)(2,1)} %others.3.refs_1_), channel_id=1, source_target_pairs={{0,8},{4,12},{8,0},{12,4},{16,24},{20,28},{24,16},{28,20},{1,9},{5... | collective-permute-start | bytes 2654216 | tf_op jit(solution)/shard_map/ppermute | solution.py:339
  200.8 40.2 %collective-permute-start.29 = (bf16[384,1152]{1,0:T(8,128)(2,1)}, bf16[384,1152]{1,0:T(8,128)(2,1)}, u32[]{:S(2)}, u32[]{:S(2)}) collective-permute-start(bf16[384,1152]{1,0:T(8,128)(2,1)} %others.3.refs_1_), channel_id=1, source_target_pairs={{0,16},{4,20},{8,24},{12,28},{16,0},{20,4},{24,8},{28,12},{1,17},{... | collective-permute-start | bytes 2654216 | tf_op jit(solution)/shard_map/ppermute | solution.py:339
  202.2 40.3 %collective-permute-start.30 = (bf16[384,1152]{1,0:T(8,128)(2,1)}, bf16[384,1152]{1,0:T(8,128)(2,1)}, u32[]{:S(2)}, u32[]{:S(2)}) collective-permute-start(bf16[384,1152]{1,0:T(8,128)(2,1)} %others.3.refs_1_), channel_id=1, source_target_pairs={{0,24},{4,28},{8,16},{12,20},{16,8},{20,12},{24,0},{28,4},{1,25},{... | collective-permute-start | bytes 2654216 | tf_op jit(solution)/shard_map/ppermute | solution.py:339
  242.5 48.0 %all-to-all-start.4 = ((bf16[8,384,384]{2,1,0:T(8,128)(2,1)}), bf16[8,384,384]{2,1,0:T(8,128)(2,1)S(1)}, u32[]{:S(2)}, u32[]{:S(2)}) async-start(bf16[8,384,384]{2,1,0:T(8,128)(2,1)} %bitcast.25), calls=%async_computation.4 | async-start | bytes 4718592 | tf_op jit(solution)/shard_map/all_to_all | solution.py:1161
  290.5 20.9 %all-to-all-start.5 = ((bf16[8,192,384]{2,1,0:T(8,128)(2,1)}), bf16[8,192,384]{2,1,0:T(8,128)(2,1)S(1)}, u32[]{:S(2)}, u32[]{:S(2)}) async-start(bf16[8,192,384]{2,1,0:T(8,128)(2,1)} %bitcast.29), calls=%async_computation.5 | async-start | bytes 2359296 | tf_op jit(solution)/shard_map/all_to_all | solution.py:1161
  311.4 25.2 %all-to-all-start.6 = ((bf16[8,64,1280]{2,1,0:T(8,128)(2,1)}), bf16[8,64,1280]{2,1,0:T(8,128)(2,1)}, u32[]{:S(2)}, u32[]{:S(2)}) async-start(bf16[8,64,1280]{2,1,0:T(8,128)(2,1)} %bitcast.27), calls=%async_computation.6 | async-start | bytes 2621440 | tf_op jit(solution)/shard_map/all_to_all | solution.py:1161
  336.6 26.3 %all-to-all-start.7 = ((bf16[8,64,1024]{2,1,0:T(8,128)(2,1)}), bf16[8,64,1024]{2,1,0:T(8,128)(2,1)S(1)}, u32[]{:S(2)}, u32[]{:S(2)}) async-start(bf16[8,64,1024]{2,1,0:T(8,128)(2,1)} %bitcast.30), calls=%async_computation.7 | async-start | bytes 2097152 | tf_op jit(solution)/shard_map/all_to_all | solution.py:1161
  340.9 24.3 %collective-permute-start.45 = (bf16[9,16,384]{2,1,0:T(8,128)(2,1)S(1)}, bf16[9,16,384]{2,1,0:T(8,128)(2,1)S(1)}, u32[]{:S(2)}, u32[]{:S(2)}) collective-permute-start(bf16[9,16,384]{2,1,0:T(8,128)(2,1)S(1)} %copy-done.13), channel_id=1, source_target_pairs={{0,1},{1,2},{2,3},{3,0},{4,5},{5,6},{6,7},{7,4},{8,9},{9,10},{10,1... | collective-permute-start | bytes 331784 | tf_op jit(solution)/shard_map/ppermute | solution.py:1167
  342.9 25.5 %collective-permute-start.46 = (bf16[9,16,384]{2,1,0:T(8,128)(2,1)S(1)}, bf16[9,16,384]{2,1,0:T(8,128)(2,1)S(1)}, u32[]{:S(2)}, u32[]{:S(2)}) collective-permute-start(bf16[9,16,384]{2,1,0:T(8,128)(2,1)S(1)} %copy-done.11), channel_id=1, source_target_pairs={{0,2},{1,3},{2,0},{3,1},{4,6},{5,7},{6,4},{7,5},{8,10},{9,11},{10,... | collective-permute-start | bytes 331784 | tf_op jit(solution)/shard_map/ppermute | solution.py:1167
  345.3 23.1 %collective-permute-start.47 = (bf16[9,16,384]{2,1,0:T(8,128)(2,1)S(1)}, bf16[9,16,384]{2,1,0:T(8,128)(2,1)S(1)}, u32[]{:S(2)}, u32[]{:S(2)}) collective-permute-start(bf16[9,16,384]{2,1,0:T(8,128)(2,1)S(1)} %copy-done.9), channel_id=1, source_target_pairs={{0,3},{1,0},{2,1},{3,2},{4,7},{5,4},{6,5},{7,6},{8,11},{9,8},{10,9... | collective-permute-start | bytes 331784 | tf_op jit(solution)/shard_map/ppermute | solution.py:1167
  (63 other events, 438.4 us)

commit v6 on v5

--- a/solution.py
+++ b/solution.py
@@ -1221,11 +1221,10 @@
 
     zs.append(over_planes(after(packed[1], *near_io)))
     first = after(zs[0], dy, *near_io)
-    nears = [swap_dp(first, X_BIT), swap_dp(first, Y_BIT)]
+    nears = near(first)
     n1, zin, mix, cv, y, w_in = front_call(
         after(ids, dy, zs[0]), io, 1, in_weight, tokens, gain1, conv_weight, sel2, after_one, after_two, a_in, b_in,
     )
-    nears += far(*[after(v, zin) for v in nears], 2)
     zs.append(over_planes(after(packed[2], zin, zs[1])))
     zout, h, n2, zgu, dzd, w_out = join_call(
         ids, io, 1, out_weight, y, tokens, dy, gain2, sel2, a_out, b_out, a_gate, a_up, b_down,
@@ -1241,7 +1240,7 @@
         if j == PARTS - 1:
             early = exchange(after(grads[-1], *nears), "dp")
         *state, g = ffn_call(
-            j, after(ids, *zs[j + 1 : j + 2]), arrays, 2 if j == 0 else None, gate_weight, up_weight,
+            j, after(ids, *zs[j + 1 : j + 2]), arrays, None, gate_weight, up_weight,
             down_weight, n2, dy, zgu, dzd, b_gate, b_up, a_down, grads[0] if j == 1 else None, *state,
         )
         previous = state[2]

time: 396 us -> 391 us (0.987)
    ppermute x46 -> x44, waiting for transfers between devices: 57.7 us -> 54.9 us  [swap_dp(): lax.ppermute(values, 'dp', [(i, i ^ bit) for i in range(lax.axis_size('dp...]
    ppermute x46 -> x44, starting transfers between devices: 29.1 us -> 30.3 us  [swap_dp(): lax.ppermute(values, 'dp', [(i, i ^ bit) for i in range(lax.axis_size('dp...]
  transfers between devices with their start and end apart: 63 -> 61, of which waited for: 18 -> 19; matrix products, arithmetic and copies ran while one was open for 2% -> 1% of each run, Pallas kernels for 53% -> 54%
where the time goes in v6:
time: 391 us; the launch traced here: 383 us
  Pallas kernels  208 us (53%)
  starting transfers between devices  83.3 us (21%)
  waiting for transfers between devices  79.7 us (20%)
  local copies, waits for them, and re-layouts  6.96 us (2%)
  other arithmetic  4.03 us (1%)
    pallas_call x3, Pallas kernels, ffn_call(): pl.pallas_call(kernel, name=f'ffn{part}', out_shape=[sds(*v) for v in sta...  111 us
    ppermute x44, waiting for transfers between devices, swap_dp(): lax.ppermute(values, 'dp', [(i, i ^ bit) for i in range(lax.axis_size('dp...  54.9 us
    ppermute x44, starting transfers between devices, swap_dp(): lax.ppermute(values, 'dp', [(i, i ^ bit) for i in range(lax.axis_size('dp...  30.3 us
    all_to_all x6, starting transfers between devices, exchange(): lax.all_to_all(flat, axis, split_axis=0, concat_axis=0, tiled=True)  28.1 us
    pallas_call x1, Pallas kernels, front_call(): pl.pallas_call(kernel, name='front', out_shape=[sds(wide[0], bf16), sds((...  17.4 us
    pallas_call x1, Pallas kernels, back_call(): pl.pallas_call(kernel, name='back', out_shape=[sds((rows, 3 * d), bf16),...  17.3 us
    pallas_call x1, Pallas kernels, last_call(): pl.pallas_call(kernel, name='last', out_shape=sds((rows, d), bf16), in_sp...  16.2 us
    pallas_call x1, Pallas kernels, join_call(): pl.pallas_call(kernel, name='join', out_shape=[sds((rows, c), bf16), sds(...  14.4 us
  transfers between devices with their start and end apart: 61, of which 19 were waited for; matrix products, arithmetic and copies ran while one was open for 1% of the time, Pallas kernels for 54%

profile of v6, /device:TPU:0, one launch (start us, length us, event | category | flops | bytes accessed | tf_op | source)
XLA Modules:
  0.0 383.5 jit_solution(15892150512338690500)
XLA Ops:
  0.6 5.2 %all-to-all-start = ((bf16[8,128,1024]{2,1,0:T(8,128)(2,1)}), bf16[8,128,1024]{2,1,0:T(8,128)(2,1)S(1)}, u32[]{:S(2)}, u32[]{:S(2)}) async-start(bf16[8,128,1024]{2,1,0:T(8,128)(2,1)} %bitcast.26), calls=%async_computation | async-start | bytes 4194304 | tf_op jit(solution)/shard_map/all_to_all | solution.py:1203
  6.4 2.7 own.2
  10.8 2.6 collective-permute-start.1
  17.1 2.1 compare_convert_fusion
  19.3 4.1 %own.3 = (bf16[512,1152]{1,0:T(8,128)(2,1)}, bf16[512,1152]{1,0:T(8,128)(2,1)}) custom-call(s32[2]{0:T(128)} %pad_add_fusion.ids_ref.refs_0_, bf16[1024,768]{1,0:T(8,128)(2,1)} %refs_11_.5, bf16[1024,256]{1,0:T(8,128)(2,1)} %refs_11_.6, bf16[1024,1152]{1,0:T(8,128)(2,1)} %refs_9_.5, bf16[1024,1152]{1,0:T(8,128)(2,1)} %refs_10_.5, bf16[4608,256]{1,0:T(8,128)(2,1)} %refs_11_.9), custom_call_target="tpu_custom_call" | custom-call | tf_op jit(solution)/shard_map/own/pallas_call | solution.py:568
  23.4 9.1 %all-to-all-done = bf16[8,128,1024]{2,1,0:T(8,128)(2,1)S(1)} async-done(((bf16[8,128,1024]{2,1,0:T(8,128)(2,1)}), bf16[8,128,1024]{2,1,0:T(8,128)(2,1)S(1)}, u32[]{:S(2)}, u32[]{:S(2)}) %all-to-all-start) | async-done | bytes 2097184 | tf_op jit(solution)/shard_map/all_to_all | solution.py:1203
  34.5 4.4 %all-to-all-start.1 = ((bf16[8,128,1024]{2,1,0:T(8,128)(2,1)}), bf16[8,128,1024]{2,1,0:T(8,128)(2,1)}, u32[]{:S(2)}, u32[]{:S(2)}) async-start(bf16[8,128,1024]{2,1,0:T(8,128)(2,1)} %bitcast.22), calls=%async_computation.1 | async-start | bytes 4194304 | tf_op jit(solution)/shard_map/all_to_all | solution.py:1210
  38.9 11.4 %collective-permute-done.1.refs_1_ = bf16[128,2176]{1,0:T(8,128)(2,1)S(1)} collective-permute-done((bf16[128,2176]{1,0:T(8,128)(2,1)}, bf16[128,2176]{1,0:T(8,128)(2,1)S(1)}, u32[]{:S(2)}, u32[]{:S(2)}) %collective-permute-start.1) | collective-permute-done | bytes 557088 | tf_op jit(solution)/shard_map/ppermute | solution.py:440
  54.5 26.8 %collective-permute-done.4.refs_3_ = bf16[384,1024]{1,0:T(8,128)(2,1)S(1)} collective-permute-done((bf16[384,1024]{1,0:T(8,128)(2,1)S(1)}, bf16[384,1024]{1,0:T(8,128)(2,1)S(1)}, u32[]{:S(2)}, u32[]{:S(2)}) %collective-permute-start.4) | collective-permute-done | bytes 786464 | tf_op jit(solution)/shard_map/ppermute | solution.py:339
  84.2 7.7 %collective-permute-done.5.refs_4_ = bf16[128,1024]{1,0:T(8,128)(2,1)S(1)} collective-permute-done((bf16[128,1024]{1,0:T(8,128)(2,1)S(1)}, bf16[128,1024]{1,0:T(8,128)(2,1)S(1)}, u32[]{:S(2)}, u32[]{:S(2)}) %collective-permute-start.5) | collective-permute-done | bytes 262176 | tf_op jit(solution)/shard_map/ppermute | solution.py:339
  91.9 3.3 collective-permute-done.6.refs_5_
  95.2 6.1 %all-to-all-start.2 = ((bf16[4,128,1152]{2,1,0:T(8,128)(2,1)}), bf16[4,128,1152]{2,1,0:T(8,128)(2,1)S(1)}, u32[]{:S(2)}, u32[]{:S(2)}) async-start(bf16[4,128,1152]{2,1,0:T(8,128)(2,1)} %bitcast.28), calls=%async_computation.2 | async-start | bytes 2359296 | tf_op jit(solution)/shard_map/all_to_all | solution.py:1161
  101.8 2.0 stacked.2.refs_1_
  111.5 17.4 %front.1 = (bf16[1024,1024]{1,0:T(8,128)(2,1)}, bf16[1024,128]{1,0:T(8,128)(2,1)}, bf16[1024,3072]{1,0:T(8,128)(2,1)}, bf16[1024,1024]{1,0:T(8,128)(2,1)}, bf16[...) custom-call(s32[2]{0:T(128)} %pad_add_fusion.ids_ref.refs_0_, bf16[384,1024]{1,0:T(8,128)(2,1)} %copy-done.1, ...), custom_call_target="tpu_custom_call" | custom-call | flops 2044723 | tf_op jit(solution)/shard_map/front/pallas_call | solution.py:645
  129.0 14.4 %join.1 = (bf16[1024,128]{1,0:T(8,128)(2,1)}, bf16[1024,1024]{1,0:T(8,128)(2,1)}, bf16[1024,1024]{1,0:T(8,128)(2,1)}, bf16[1024,256]{1,0:T(8,128)(2,1)}, bf16[10...) custom-call(s32[2]{0:T(128)} %pad_add_fusion.ids_ref.refs_0_, bf16[384,1024]{1,0:T(8,128)(2,1)} %copy-done.1, ...), custom_call_target="tpu_custom_call" | custom-call | flops 681574 | tf_op jit(solution)/shard_map/join/pallas_call | solution.py:704
  146.6 5.3 %all-to-all-start.3 = ((bf16[4,128,1152]{2,1,0:T(8,128)(2,1)}), bf16[4,128,1152]{2,1,0:T(8,128)(2,1)S(1)}, u32[]{:S(2)}, u32[]{:S(2)}) async-start(bf16[4,128,1152]{2,1,0:T(8,128)(2,1)} %bitcast.10), calls=%async_computation.3 | async-start | bytes 2359296 | tf_op jit(solution)/shard_map/all_to_all | solution.py:1161
  155.5 37.0 %ffn0.1 = (bf16[1024,1024]{1,0:T(8,128)(2,1)}, bf16[1024,1024]{1,0:T(8,128)(2,1)}, f32[1024,256]{1,0:T(8,128)}, f32[1024,128]{1,0:T(8,128)}, bf16[8,4,3,16,384]{4,3,2,1,0:T(8,128)(2,1)}) custom-call(s32[2]{0:T(128)} %pad_add_fusion.ids_ref.refs_0_, bf16[384,1152]{1,0:T(8,128)(2,1)} %stacked.2.refs_1_, bf16[384,1152]{1,0:T(8,128)(2,1)} %collective-permute-done.12.refs_2_, ...), custom_call_target="tpu_custom_call" | custom-call | flops 6134169 | tf_op jit(solution)/shard_map/ffn0/pallas_call | solution.py:893
  198.9 37.2 %ffn1.1 = (bf16[1024,1024]{1,0:T(8,128)(2,1)}, bf16[1024,1024]{1,0:T(8,128)(2,1)}, f32[1024,256]{1,0:T(8,128)}, f32[1024,128]{1,0:T(8,128)}, bf16[8,4,6,16,384]{4,3,2,1,0:T(8,128)(2,1)}) custom-call(s32[2]{0:T(128)} %pad_add_fusion.ids_ref.refs_0_, bf16[384,1152]{1,0:T(8,128)(2,1)} %copy-done.2, bf16[384,1152]{1,0:T(8,128)(2,1)} %collective-permute-done.19.refs_2_, ...), custom_call_target="tpu_custom_call" | custom-call | flops 6134169 | tf_op jit(solution)/shard_map/ffn1/pallas_call | solution.py:893
  237.2 4.1 %all-to-all-start.4 = ((bf16[8,384,384]{2,1,0:T(8,128)(2,1)}), bf16[8,384,384]{2,1,0:T(8,128)(2,1)S(1)}, u32[]{:S(2)}, u32[]{:S(2)}) async-start(bf16[8,384,384]{2,1,0:T(8,128)(2,1)} %bitcast.25), calls=%async_computation.4 | async-start | bytes 4718592 | tf_op jit(solution)/shard_map/all_to_all | solution.py:1161
  242.4 2.2 collective-permute-done.29.refs_5_
  248.2 37.0 %ffn2.1 = (bf16[1024,1024]{1,0:T(8,128)(2,1)}, bf16[1024,1024]{1,0:T(8,128)(2,1)}, f32[1024,256]{1,0:T(8,128)}, f32[1024,128]{1,0:T(8,128)}, bf16[8,4,3,16,384]{4,3,2,1,0:T(8,128)(2,1)}) custom-call(s32[2]{0:T(128)} %pad_add_fusion.ids_ref.refs_0_, bf16[384,1152]{1,0:T(8,128)(2,1)} %others.3.refs_1_, bf16[384,1152]{1,0:T(8,128)(2,1)} %copy-done.24, ...), custom_call_target="tpu_custom_call" | custom-call | flops 6134169 | tf_op jit(solution)/shard_map/ffn2/pallas_call | solution.py:893
  285.2 4.2 %all-to-all-start.5 = ((bf16[8,192,384]{2,1,0:T(8,128)(2,1)}), bf16[8,192,384]{2,1,0:T(8,128)(2,1)S(1)}, u32[]{:S(2)}, u32[]{:S(2)}) async-start(bf16[8,192,384]{2,1,0:T(8,128)(2,1)} %bitcast.29), calls=%async_computation.5 | async-start | bytes 2359296 | tf_op jit(solution)/shard_map/all_to_all | solution.py:1161
  289.4 12.5 %middle.1 = (bf16[1024,1024]{1,0:T(8,128)(2,1)}, bf16[1024,1024]{1,0:T(8,128)(2,1)}, bf16[1024,128]{1,0:T(8,128)(2,1)}, bf16[8,4,16,1280]{3,2,1,0:T(8,128)(2,1)}) custom-call(bf16[1024,1024]{1,0:T(8,128)(2,1)} %get-tuple-element.129.dn_hbm, bf16[1024,1024]{1,0:T(8,128)(2,1)} %get-tuple-element.104.refs_15_.n2_hbm, ...), custom_call_target="tpu_custom_call" | custom-call | flops 2097152 | tf_op jit(solution)/shard_map/middle/pallas_call | solution.py:984
  301.9 4.3 %all-to-all-done.5 = bf16[8,192,384]{2,1,0:T(8,128)(2,1)S(1)} async-done(((bf16[8,192,384]{2,1,0:T(8,128)(2,1)}), bf16[8,192,384]{2,1,0:T(8,128)(2,1)S(1)}, u32[]{:S(2)}, u32[]{:S(2)}) %all-to-all-start.5) | async-done | bytes 1179680 | tf_op jit(solution)/shard_map/all_to_all | solution.py:1161
  306.1 4.3 %all-to-all-start.6 = ((bf16[8,64,1280]{2,1,0:T(8,128)(2,1)}), bf16[8,64,1280]{2,1,0:T(8,128)(2,1)}, u32[]{:S(2)}, u32[]{:S(2)}) async-start(bf16[8,64,1280]{2,1,0:T(8,128)(2,1)} %bitcast.27), calls=%async_computation.6 | async-start | bytes 2621440 | tf_op jit(solution)/shard_map/all_to_all | solution.py:1161
  314.0 17.3 %back.1 = (bf16[1024,3072]{1,0:T(8,128)(2,1)}, bf16[1024,128]{1,0:T(8,128)(2,1)}, bf16[8,4,16,1024]{3,2,1,0:T(8,128)(2,1)}) custom-call(bf16[1024,1024]{1,0:T(8,128)(2,1)} %get-tuple-element.138.w_out_hbm, bf16[1024,1024]{1,0:T(8,128)(2,1)} %get-tuple-element.139.dhb_hbm.dh_hbm, bf16[1024,1024]{1,0:T(8,128)(2,1)} %get-tuple-element.140.cv_hbm, ...), custom_call_target="tpu_custom_call" | custom-call | flops 2097152 | tf_op jit(solution)/shard_map/back/pallas_call | solution.py:1043
  331.3 4.2 %all-to-all-start.7 = ((bf16[8,64,1024]{2,1,0:T(8,128)(2,1)}), bf16[8,64,1024]{2,1,0:T(8,128)(2,1)S(1)}, u32[]{:S(2)}, u32[]{:S(2)}) async-start(bf16[8,64,1024]{2,1,0:T(8,128)(2,1)} %bitcast.30), calls=%async_computation.7 | async-start | bytes 2097152 | tf_op jit(solution)/shard_map/all_to_all | solution.py:1161
  337.6 2.4 collective-permute-start.44
  341.4 16.2 %last.1 = bf16[1024,1024]{1,0:T(8,128)(2,1)} custom-call(bf16[1024,3072]{1,0:T(8,128)(2,1)} %get-tuple-element.148.dp_hbm, bf16[1024,3072]{1,0:T(8,128)(2,1)} %get-tuple-element.149.w_in_hbm, bf16[1024,1024]{1,0:T(8,128)(2,1)} %get-tuple-element.139.dhb_hbm.dh_hbm, bf16[1024,1024]{1,0:T(8,128)(2,1)} %x_hbm.1, bf16[1024,128]{1,0:T(8,128)(2,1)} %get-tuple-element.150.dzi_ref, ...), custom_call_target="tpu_custom_call" | custom-call | flops 2097152 | tf_op jit(solution)/shard_map/last/pallas_call | solution.py:1090
  360.5 2.7 collective-permute-start.35
  363.2 2.0 collective-permute-start.46
  366.8 2.4 collective-permute-start.48
  (181 shorter events, 67.9 us)
Async XLA Ops:
  0.6 31.8 %all-to-all-start = ((bf16[8,128,1024]{2,1,0:T(8,128)(2,1)}), bf16[8,128,1024]{2,1,0:T(8,128)(2,1)S(1)}, u32[]{:S(2)}, u32[]{:S(2)}) async-start(bf16[8,128,1024]{2,1,0:T(8,128)(2,1)} %bitcast.26), calls=%async_computation | async-start | bytes 4194304 | tf_op jit(solution)/shard_map/all_to_all | solution.py:1203
  9.1 29.8 %collective-permute-start = (bf16[128,2176]{1,0:T(8,128)(2,1)}, bf16[128,2176]{1,0:T(8,128)(2,1)S(1)}, u32[]{:S(2)}, u32[]{:S(2)}) collective-permute-start(bf16[128,2176]{1,0:T(8,128)(2,1)} %own.2), channel_id=1, source_target_pairs={{0,1},{1,2},{2,3},{3,0},{4,5},{5,6},{6,7},{7,4},{8,9},{9,10},{10,1... | collective-permute-start | bytes 1671176 | tf_op jit(solution)/shard_map/ppermute | solution.py:440
  10.8 39.5 %collective-permute-start.1 = (bf16[128,2176]{1,0:T(8,128)(2,1)}, bf16[128,2176]{1,0:T(8,128)(2,1)S(1)}, u32[]{:S(2)}, u32[]{:S(2)}) collective-permute-start(bf16[128,2176]{1,0:T(8,128)(2,1)} %own.2), channel_id=1, source_target_pairs={{0,2},{1,3},{2,0},{3,1},{4,6},{5,7},{6,4},{7,5},{8,10},{9,11},{10,... | collective-permute-start | bytes 1671176 | tf_op jit(solution)/shard_map/ppermute | solution.py:440
  13.3 36.9 %collective-permute-start.2 = (bf16[128,2176]{1,0:T(8,128)(2,1)}, bf16[128,2176]{1,0:T(8,128)(2,1)}, u32[]{:S(2)}, u32[]{:S(2)}) collective-permute-start(bf16[128,2176]{1,0:T(8,128)(2,1)} %own.2), channel_id=1, source_target_pairs={{0,3},{1,0},{2,1},{3,2},{4,7},{5,4},{6,5},{7,6},{8,11},{9,8},{10,9... | collective-permute-start | bytes 1671176 | tf_op jit(solution)/shard_map/ppermute | solution.py:440
  34.5 60.6 %all-to-all-start.1 = ((bf16[8,128,1024]{2,1,0:T(8,128)(2,1)}), bf16[8,128,1024]{2,1,0:T(8,128)(2,1)}, u32[]{:S(2)}, u32[]{:S(2)}) async-start(bf16[8,128,1024]{2,1,0:T(8,128)(2,1)} %bitcast.22), calls=%async_computation.1 | async-start | bytes 4194304 | tf_op jit(solution)/shard_map/all_to_all | solution.py:1210
  51.3 30.0 %collective-permute-start.4 = (bf16[384,1024]{1,0:T(8,128)(2,1)S(1)}, bf16[384,1024]{1,0:T(8,128)(2,1)S(1)}, u32[]{:S(2)}, u32[]{:S(2)}) collective-permute-start(bf16[384,1024]{1,0:T(8,128)(2,1)S(1)} %stacked.3.refs_1_), channel_id=1, source_target_pairs={{0,16},{4,20},{8,24},{12,28},{16,0},{20,4},{24,8},{28,12},{1,17},{... | collective-permute-start | bytes 2359304 | tf_op jit(solution)/shard_map/ppermute | solution.py:339
  53.1 29.8 %collective-permute-start.3 = (bf16[384,1024]{1,0:T(8,128)(2,1)S(1)}, bf16[384,1024]{1,0:T(8,128)(2,1)S(1)}, u32[]{:S(2)}, u32[]{:S(2)}) collective-permute-start(bf16[384,1024]{1,0:T(8,128)(2,1)S(1)} %stacked.3.refs_1_), channel_id=1, source_target_pairs={{0,8},{4,12},{8,0},{12,4},{16,24},{20,28},{24,16},{28,20},{1,9},{5... | collective-permute-start | bytes 2359304 | tf_op jit(solution)/shard_map/ppermute | solution.py:339
  81.4 13.8 %collective-permute-start.6 = (bf16[256,1024]{1,0:T(8,128)(2,1)S(1)}, bf16[256,1024]{1,0:T(8,128)(2,1)}, u32[]{:S(2)}, u32[]{:S(2)}) collective-permute-start(bf16[256,1024]{1,0:T(8,128)(2,1)S(1)} %slice.9), channel_id=1, source_target_pairs={{0,8},{4,12},{8,0},{12,4},{16,24},{20,28},{24,16},{28,20},{1,9},{5... | collective-permute-start | bytes 1572872 | tf_op jit(solution)/shard_map/ppermute | solution.py:339
  95.2 50.6 %all-to-all-start.2 = ((bf16[4,128,1152]{2,1,0:T(8,128)(2,1)}), bf16[4,128,1152]{2,1,0:T(8,128)(2,1)S(1)}, u32[]{:S(2)}, u32[]{:S(2)}) async-start(bf16[4,128,1152]{2,1,0:T(8,128)(2,1)} %bitcast.28), calls=%async_computation.2 | async-start | bytes 2359296 | tf_op jit(solution)/shard_map/all_to_all | solution.py:1161
  103.9 39.6 %collective-permute-start.14 = (bf16[384,1152]{1,0:T(8,128)(2,1)}, bf16[384,1152]{1,0:T(8,128)(2,1)}, u32[]{:S(2)}, u32[]{:S(2)}) collective-permute-start(bf16[384,1152]{1,0:T(8,128)(2,1)} %stacked.2.refs_1_), channel_id=1, source_target_pairs={{0,24},{4,28},{8,16},{12,20},{16,8},{20,12},{24,0},{28,4},{1,25},{... | collective-permute-start | bytes 2654216 | tf_op jit(solution)/shard_map/ppermute | solution.py:339
  103.9 41.3 %collective-permute-start.13 = (bf16[384,1152]{1,0:T(8,128)(2,1)}, bf16[384,1152]{1,0:T(8,128)(2,1)}, u32[]{:S(2)}, u32[]{:S(2)}) collective-permute-start(bf16[384,1152]{1,0:T(8,128)(2,1)} %stacked.2.refs_1_), channel_id=1, source_target_pairs={{0,16},{4,20},{8,24},{12,28},{16,0},{20,4},{24,8},{28,12},{1,17},{... | collective-permute-start | bytes 2654216 | tf_op jit(solution)/shard_map/ppermute | solution.py:339
  105.7 39.6 %collective-permute-start.12 = (bf16[384,1152]{1,0:T(8,128)(2,1)}, bf16[384,1152]{1,0:T(8,128)(2,1)}, u32[]{:S(2)}, u32[]{:S(2)}) collective-permute-start(bf16[384,1152]{1,0:T(8,128)(2,1)} %stacked.2.refs_1_), channel_id=1, source_target_pairs={{0,8},{4,12},{8,0},{12,4},{16,24},{20,28},{24,16},{28,20},{1,9},{5... | collective-permute-start | bytes 2654216 | tf_op jit(solution)/shard_map/ppermute | solution.py:339
  109.9 43.2 %collective-permute-start.15 = (bf16[384,1152]{1,0:T(8,128)(2,1)}, bf16[384,1152]{1,0:T(8,128)(2,1)}, u32[]{:S(2)}, u32[]{:S(2)}) collective-permute-start(bf16[384,1152]{1,0:T(8,128)(2,1)} %stacked.2.refs_1_), channel_id=1, source_target_pairs={{0,4},{4,0},{8,12},{12,8},{16,20},{20,16},{24,28},{28,24},{1,5},{5... | collective-permute-start | bytes 2654216 | tf_op jit(solution)/shard_map/ppermute | solution.py:339
  143.4 11.1 %collective-permute-start.18 = (bf16[384,1152]{1,0:T(8,128)(2,1)}, bf16[384,1152]{1,0:T(8,128)(2,1)}, u32[]{:S(2)}, u32[]{:S(2)}) collective-permute-start(bf16[384,1152]{1,0:T(8,128)(2,1)} %collective-permute-done.14.refs_4_), channel_id=1, source_target_pairs={{0,4},{4,0},{8,12},{12,8},{16,20},{20,16},{24,28},{28,24},{1,5},{5... | collective-permute-start | bytes 2654216 | tf_op jit(solution)/shard_map/ppermute | solution.py:339
  145.3 9.3 %collective-permute-start.17 = (bf16[384,1152]{1,0:T(8,128)(2,1)}, bf16[384,1152]{1,0:T(8,128)(2,1)}, u32[]{:S(2)}, u32[]{:S(2)}) collective-permute-start(bf16[384,1152]{1,0:T(8,128)(2,1)} %collective-permute-done.13.refs_3_), channel_id=1, source_target_pairs={{0,4},{4,0},{8,12},{12,8},{16,20},{20,16},{24,28},{28,24},{1,5},{5... | collective-permute-start | bytes 2654216 | tf_op jit(solution)/shard_map/ppermute | solution.py:339
  145.3 10.2 %collective-permute-start.16 = (bf16[384,1152]{1,0:T(8,128)(2,1)}, bf16[384,1152]{1,0:T(8,128)(2,1)}, u32[]{:S(2)}, u32[]{:S(2)}) collective-permute-start(bf16[384,1152]{1,0:T(8,128)(2,1)} %collective-permute-done.12.refs_2_), channel_id=1, source_target_pairs={{0,4},{4,0},{8,12},{12,8},{16,20},{20,16},{24,28},{28,24},{1,5},{5... | collective-permute-start | bytes 2654216 | tf_op jit(solution)/shard_map/ppermute | solution.py:339
  146.6 47.1 %all-to-all-start.3 = ((bf16[4,128,1152]{2,1,0:T(8,128)(2,1)}), bf16[4,128,1152]{2,1,0:T(8,128)(2,1)S(1)}, u32[]{:S(2)}, u32[]{:S(2)}) async-start(bf16[4,128,1152]{2,1,0:T(8,128)(2,1)} %bitcast.10), calls=%async_computation.3 | async-start | bytes 2359296 | tf_op jit(solution)/shard_map/all_to_all | solution.py:1161
  151.9 40.7 %collective-permute-start.21 = (bf16[384,1152]{1,0:T(8,128)(2,1)S(1)}, bf16[384,1152]{1,0:T(8,128)(2,1)S(1)}, u32[]{:S(2)}, u32[]{:S(2)}) collective-permute-start(bf16[384,1152]{1,0:T(8,128)(2,1)S(1)} %others.2.refs_1_), channel_id=1, source_target_pairs={{0,24},{4,28},{8,16},{12,20},{16,8},{20,12},{24,0},{28,4},{1,25},{... | collective-permute-start | bytes 2654216 | tf_op jit(solution)/shard_map/ppermute | solution.py:339
  153.1 40.1 %collective-permute-start.20 = (bf16[384,1152]{1,0:T(8,128)(2,1)S(1)}, bf16[384,1152]{1,0:T(8,128)(2,1)}, u32[]{:S(2)}, u32[]{:S(2)}) collective-permute-start(bf16[384,1152]{1,0:T(8,128)(2,1)S(1)} %others.2.refs_1_), channel_id=1, source_target_pairs={{0,16},{4,20},{8,24},{12,28},{16,0},{20,4},{24,8},{28,12},{1,17},{... | collective-permute-start | bytes 2654216 | tf_op jit(solution)/shard_map/ppermute | solution.py:339
  154.5 42.1 %collective-permute-start.23 = (bf16[384,1152]{1,0:T(8,128)(2,1)S(1)}, bf16[384,1152]{1,0:T(8,128)(2,1)}, u32[]{:S(2)}, u32[]{:S(2)}) collective-permute-start(bf16[384,1152]{1,0:T(8,128)(2,1)S(1)} %others.2.refs_1_), channel_id=1, source_target_pairs={{0,4},{4,0},{8,12},{12,8},{16,20},{20,16},{24,28},{28,24},{1,5},{5... | collective-permute-start | bytes 2654216 | tf_op jit(solution)/shard_map/ppermute | solution.py:339
  154.5 38.7 %collective-permute-start.19 = (bf16[384,1152]{1,0:T(8,128)(2,1)S(1)}, bf16[384,1152]{1,0:T(8,128)(2,1)}, u32[]{:S(2)}, u32[]{:S(2)}) collective-permute-start(bf16[384,1152]{1,0:T(8,128)(2,1)S(1)} %others.2.refs_1_), channel_id=1, source_target_pairs={{0,8},{4,12},{8,0},{12,4},{16,24},{20,28},{24,16},{28,20},{1,9},{5... | collective-permute-start | bytes 2654216 | tf_op jit(solution)/shard_map/ppermute | solution.py:339
  195.4 40.8 %collective-permute-start.22 = (bf16[384,1152]{1,0:T(8,128)(2,1)}, bf16[384,1152]{1,0:T(8,128)(2,1)S(1)}, u32[]{:S(2)}, u32[]{:S(2)}) collective-permute-start(bf16[384,1152]{1,0:T(8,128)(2,1)} %others.3.refs_1_), channel_id=1, source_target_pairs={{0,8},{4,12},{8,0},{12,4},{16,24},{20,28},{24,16},{28,20},{1,9},{5... | collective-permute-start | bytes 2654216 | tf_op jit(solution)/shard_map/ppermute | solution.py:339
  196.6 39.6 %collective-permute-start.27 = (bf16[384,1152]{1,0:T(8,128)(2,1)}, bf16[384,1152]{1,0:T(8,128)(2,1)}, u32[]{:S(2)}, u32[]{:S(2)}) collective-permute-start(bf16[384,1152]{1,0:T(8,128)(2,1)} %others.3.refs_1_), channel_id=1, source_target_pairs={{0,16},{4,20},{8,24},{12,28},{16,0},{20,4},{24,8},{28,12},{1,17},{... | collective-permute-start | bytes 2654216 | tf_op jit(solution)/shard_map/ppermute | solution.py:339
  197.2 40.0 %collective-permute-start.28 = (bf16[384,1152]{1,0:T(8,128)(2,1)}, bf16[384,1152]{1,0:T(8,128)(2,1)}, u32[]{:S(2)}, u32[]{:S(2)}) collective-permute-start(bf16[384,1152]{1,0:T(8,128)(2,1)} %others.3.refs_1_), channel_id=1, source_target_pairs={{0,24},{4,28},{8,16},{12,20},{16,8},{20,12},{24,0},{28,4},{1,25},{... | collective-permute-start | bytes 2654216 | tf_op jit(solution)/shard_map/ppermute | solution.py:339
  237.2 48.0 %all-to-all-start.4 = ((bf16[8,384,384]{2,1,0:T(8,128)(2,1)}), bf16[8,384,384]{2,1,0:T(8,128)(2,1)S(1)}, u32[]{:S(2)}, u32[]{:S(2)}) async-start(bf16[8,384,384]{2,1,0:T(8,128)(2,1)} %bitcast.25), calls=%async_computation.4 | async-start | bytes 4718592 | tf_op jit(solution)/shard_map/all_to_all | solution.py:1161
  285.2 20.9 %all-to-all-start.5 = ((bf16[8,192,384]{2,1,0:T(8,128)(2,1)}), bf16[8,192,384]{2,1,0:T(8,128)(2,1)S(1)}, u32[]{:S(2)}, u32[]{:S(2)}) async-start(bf16[8,192,384]{2,1,0:T(8,128)(2,1)} %bitcast.29), calls=%async_computation.5 | async-start | bytes 2359296 | tf_op jit(solution)/shard_map/all_to_all | solution.py:1161
  306.1 25.2 %all-to-all-start.6 = ((bf16[8,64,1280]{2,1,0:T(8,128)(2,1)}), bf16[8,64,1280]{2,1,0:T(8,128)(2,1)}, u32[]{:S(2)}, u32[]{:S(2)}) async-start(bf16[8,64,1280]{2,1,0:T(8,128)(2,1)} %bitcast.27), calls=%async_computation.6 | async-start | bytes 2621440 | tf_op jit(solution)/shard_map/all_to_all | solution.py:1161
  331.3 26.3 %all-to-all-start.7 = ((bf16[8,64,1024]{2,1,0:T(8,128)(2,1)}), bf16[8,64,1024]{2,1,0:T(8,128)(2,1)S(1)}, u32[]{:S(2)}, u32[]{:S(2)}) async-start(bf16[8,64,1024]{2,1,0:T(8,128)(2,1)} %bitcast.30), calls=%async_computation.7 | async-start | bytes 2097152 | tf_op jit(solution)/shard_map/all_to_all | solution.py:1161
  335.6 24.3 %collective-permute-start.43 = (bf16[9,16,384]{2,1,0:T(8,128)(2,1)S(1)}, bf16[9,16,384]{2,1,0:T(8,128)(2,1)S(1)}, u32[]{:S(2)}, u32[]{:S(2)}) collective-permute-start(bf16[9,16,384]{2,1,0:T(8,128)(2,1)S(1)} %copy-done.13), channel_id=1, source_target_pairs={{0,1},{1,2},{2,3},{3,0},{4,5},{5,6},{6,7},{7,4},{8,9},{9,10},{10,1... | collective-permute-start | bytes 331784 | tf_op jit(solution)/shard_map/ppermute | solution.py:1167
  337.6 25.6 %collective-permute-start.44 = (bf16[9,16,384]{2,1,0:T(8,128)(2,1)S(1)}, bf16[9,16,384]{2,1,0:T(8,128)(2,1)S(1)}, u32[]{:S(2)}, u32[]{:S(2)}) collective-permute-start(bf16[9,16,384]{2,1,0:T(8,128)(2,1)S(1)} %copy-done.11), channel_id=1, source_target_pairs={{0,2},{1,3},{2,0},{3,1},{4,6},{5,7},{6,4},{7,5},{8,10},{9,11},{10,... | collective-permute-start | bytes 331784 | tf_op jit(solution)/shard_map/ppermute | solution.py:1167
  339.9 23.2 %collective-permute-start.45 = (bf16[9,16,384]{2,1,0:T(8,128)(2,1)S(1)}, bf16[9,16,384]{2,1,0:T(8,128)(2,1)S(1)}, u32[]{:S(2)}, u32[]{:S(2)}) collective-permute-start(bf16[9,16,384]{2,1,0:T(8,128)(2,1)S(1)} %copy-done.9), channel_id=1, source_target_pairs={{0,3},{1,0},{2,1},{3,2},{4,7},{5,4},{6,5},{7,6},{8,11},{9,8},{10,9... | collective-permute-start | bytes 331784 | tf_op jit(solution)/shard_map/ppermute | solution.py:1167
  359.9 9.2 %collective-permute-start.34 = (bf16[16,2304]{1,0:T(8,128)(2,1)S(1)}, bf16[16,2304]{1,0:T(8,128)(2,1)S(1)}, u32[]{:S(2)}, u32[]{:S(2)}) collective-permute-start(bf16[16,2304]{1,0:T(8,128)(2,1)S(1)} %get-tuple-element.156), channel_id=1, source_target_pairs={{0,2},{1,3},{2,0},{3,1},{4,6},{5,7},{6,4},{7,5},{8,10},{9,11},{10,... | collective-permute-start | bytes 221192 | tf_op jit(solution)/shard_map/ppermute | solution.py:1167
  (58 other events, 426.1 us)

commit v7 on v6

--- a/solution.py
+++ b/solution.py
@@ -1007,19 +1007,23 @@
 
     def kernel(w_out_hbm, dhb_hbm, cv_hbm, mix_hbm, n1_hbm, dzo, zin_ref, sel_ref, m1_ref, m2_ref, taps_ref,
                a_out_ref, b_in_ref, dp_out, dzi_ref, gi_ref, w_out_ref, dhb, cv_ref, mix_ref, n1_ref, dp_ref, sems):
-        wait_w, wait_dhb, wait_cv, wait_mix, wait_n1 = fetched(
-            [(w_out_hbm, w_out_ref), (dhb_hbm, dhb), (cv_hbm, cv_ref), (mix_hbm, mix_ref), (n1_hbm, n1_ref)], sems
-        )
+        wanted = [(w_out_hbm, w_out_ref), (dhb_hbm, dhb)]
+        for j in range(blocks):
+            wanted.append((cv_hbm.at[:, col(j)], cv_ref.at[:, col(j)]))
+            for k in (1, 2, 0):
+                cc = col(k * blocks + j)
+                wanted.append((mix_hbm.at[:, cc], mix_ref.at[:, cc]))
+        wait_w, wait_dhb, *wait_block, wait_n1 = fetched([*wanted, (n1_hbm, n1_ref)], sems)
         sel_f = sel_ref[...].astype(f32)
         m1 = m1_ref[...]
         m2 = m2_ref[...]
         wait_w()
         wait_dhb()
-        wait_cv()
-        wait_mix()
 
         def conv(j):
             dyc = nt(dhb[...], w_out_ref[col(j), :]) + nt(dzo[...], a_out_ref[col(j), :])
+            for wait in wait_block[4 * j : 4 * j + 4]:
+                wait()
             dp_ref[:, col(blocks + j)] = (dyc * cv_ref[:, col(j)].astype(f32)).astype(bf16)
             dcv = dyc * mix_ref[:, col(blocks + j)].astype(f32)
             dbx = (
@@ -1030,8 +1034,9 @@
             dp_ref[:, col(j)] = (dbx * mix_ref[:, col(2 * blocks + j)].astype(f32)).astype(bf16)
             dp_ref[:, col(2 * blocks + j)] = (dbx * mix_ref[:, col(j)].astype(f32)).astype(bf16)
 
-        loop(blocks, conv)
-        store = pltpu.make_async_copy(dp_ref, dp_out, sems.at[5])
+        for j in range(blocks):
+            conv(j)
+        store = pltpu.make_async_copy(dp_ref, dp_out, sems.at[4 * blocks + 3])
         store.start()
         dzi_ref[...] = (nt(dp_ref[...], b_in_ref[...]) * sel_f).astype(bf16)
         spread(gi_ref, 0, nn(zin_ref[...].T, dp_ref[...]))
@@ -1048,7 +1053,7 @@
         ],
         in_specs=[any_spec()] * 5 + [vmem_spec()] * 8,
         out_specs=[any_spec()] + [vmem_spec()] * 2,
-        scratch_shapes=[pltpu.VMEM((d, d), bf16), wide, wide, long, wide, long, pltpu.SemaphoreType.DMA((6,))],
+        scratch_shapes=[pltpu.VMEM((d, d), bf16), wide, wide, long, wide, long, pltpu.SemaphoreType.DMA((4 * blocks + 4,))],
         compiler_params=params(),
         cost_estimate=cost(2 * rows * d * 4 * d),
     )(w_out, dhb, cv, mix, n1, dzo, zin, sel2, m1, m2, taps, a_out, b_in)

time: 391 us -> 393 us (level)
  no operation moved by 1% of the time
where the time goes in v7:
time: 393 us; the launch traced here: 386 us
  Pallas kernels  210 us (53%)
  starting transfers between devices  83 us (21%)
  waiting for transfers between devices  79.5 us (20%)
  local copies, waits for them, and re-layouts  7.02 us (2%)
  other arithmetic  4.03 us (1%)
    pallas_call x3, Pallas kernels, ffn_call(): pl.pallas_call(kernel, name=f'ffn{part}', out_shape=[sds(*v) for v in sta...  111 us
    ppermute x44, waiting for transfers between devices, swap_dp(): lax.ppermute(values, 'dp', [(i, i ^ bit) for i in range(lax.axis_size('dp...  54.8 us
    ppermute x44, starting transfers between devices, swap_dp(): lax.ppermute(values, 'dp', [(i, i ^ bit) for i in range(lax.axis_size('dp...  30.4 us
    all_to_all x6, starting transfers between devices, exchange(): lax.all_to_all(flat, axis, split_axis=0, concat_axis=0, tiled=True)  27.9 us
    pallas_call x1, Pallas kernels, back_call(): pl.pallas_call(kernel, name='back', out_shape=[sds((rows, 3 * d), bf16),...  19.1 us
    pallas_call x1, Pallas kernels, front_call(): pl.pallas_call(kernel, name='front', out_shape=[sds(wide[0], bf16), sds((...  17.4 us
    pallas_call x1, Pallas kernels, last_call(): pl.pallas_call(kernel, name='last', out_shape=sds((rows, d), bf16), in_sp...  16.4 us
    pallas_call x1, Pallas kernels, join_call(): pl.pallas_call(kernel, name='join', out_shape=[sds((rows, c), bf16), sds(...  14.4 us
  transfers between devices with their start and end apart: 61, of which 19 were waited for; matrix products, arithmetic and copies ran while one was open for 1% of the time, Pallas kernels for 54%

profile of v7, /device:TPU:0, one launch (start us, length us, event | category | flops | bytes accessed | tf_op | source)
XLA Modules:
  0.0 385.6 jit_solution(3715797444873655836)
XLA Ops:
  0.6 5.2 %all-to-all-start = ((bf16[8,128,1024]{2,1,0:T(8,128)(2,1)}), bf16[8,128,1024]{2,1,0:T(8,128)(2,1)S(1)}, u32[]{:S(2)}, u32[]{:S(2)}) async-start(bf16[8,128,1024]{2,1,0:T(8,128)(2,1)} %bitcast.26), calls=%async_computation | async-start | bytes 4194304 | tf_op jit(solution)/shard_map/all_to_all | solution.py:1208
  6.4 2.7 own.2
  10.8 2.6 collective-permute-start.1
  17.1 2.1 compare_convert_fusion
  19.3 4.1 %own.3 = (bf16[512,1152]{1,0:T(8,128)(2,1)}, bf16[512,1152]{1,0:T(8,128)(2,1)}) custom-call(s32[2]{0:T(128)} %pad_add_fusion.ids_ref.refs_0_, bf16[1024,768]{1,0:T(8,128)(2,1)} %refs_11_.5, bf16[1024,256]{1,0:T(8,128)(2,1)} %refs_11_.6, bf16[1024,1152]{1,0:T(8,128)(2,1)} %refs_9_.5, bf16[1024,1152]{1,0:T(8,128)(2,1)} %refs_10_.5, bf16[4608,256]{1,0:T(8,128)(2,1)} %refs_11_.9), custom_call_target="tpu_custom_call" | custom-call | tf_op jit(solution)/shard_map/own/pallas_call | solution.py:568
  23.4 9.1 %all-to-all-done = bf16[8,128,1024]{2,1,0:T(8,128)(2,1)S(1)} async-done(((bf16[8,128,1024]{2,1,0:T(8,128)(2,1)}), bf16[8,128,1024]{2,1,0:T(8,128)(2,1)S(1)}, u32[]{:S(2)}, u32[]{:S(2)}) %all-to-all-start) | async-done | bytes 2097184 | tf_op jit(solution)/shard_map/all_to_all | solution.py:1208
  34.5 4.4 %all-to-all-start.1 = ((bf16[8,128,1024]{2,1,0:T(8,128)(2,1)}), bf16[8,128,1024]{2,1,0:T(8,128)(2,1)}, u32[]{:S(2)}, u32[]{:S(2)}) async-start(bf16[8,128,1024]{2,1,0:T(8,128)(2,1)} %bitcast.22), calls=%async_computation.1 | async-start | bytes 4194304 | tf_op jit(solution)/shard_map/all_to_all | solution.py:1215
  38.9 11.4 %collective-permute-done.1.refs_1_ = bf16[128,2176]{1,0:T(8,128)(2,1)S(1)} collective-permute-done((bf16[128,2176]{1,0:T(8,128)(2,1)}, bf16[128,2176]{1,0:T(8,128)(2,1)S(1)}, u32[]{:S(2)}, u32[]{:S(2)}) %collective-permute-start.1) | collective-permute-done | bytes 557088 | tf_op jit(solution)/shard_map/ppermute | solution.py:440
  54.5 26.8 %collective-permute-done.4.refs_3_ = bf16[384,1024]{1,0:T(8,128)(2,1)S(1)} collective-permute-done((bf16[384,1024]{1,0:T(8,128)(2,1)S(1)}, bf16[384,1024]{1,0:T(8,128)(2,1)S(1)}, u32[]{:S(2)}, u32[]{:S(2)}) %collective-permute-start.4) | collective-permute-done | bytes 786464 | tf_op jit(solution)/shard_map/ppermute | solution.py:339
  84.2 7.7 %collective-permute-done.5.refs_4_ = bf16[128,1024]{1,0:T(8,128)(2,1)S(1)} collective-permute-done((bf16[128,1024]{1,0:T(8,128)(2,1)S(1)}, bf16[128,1024]{1,0:T(8,128)(2,1)S(1)}, u32[]{:S(2)}, u32[]{:S(2)}) %collective-permute-start.5) | collective-permute-done | bytes 262176 | tf_op jit(solution)/shard_map/ppermute | solution.py:339
  91.9 3.3 collective-permute-done.6.refs_5_
  95.2 6.1 %all-to-all-start.2 = ((bf16[4,128,1152]{2,1,0:T(8,128)(2,1)}), bf16[4,128,1152]{2,1,0:T(8,128)(2,1)S(1)}, u32[]{:S(2)}, u32[]{:S(2)}) async-start(bf16[4,128,1152]{2,1,0:T(8,128)(2,1)} %bitcast.28), calls=%async_computation.2 | async-start | bytes 2359296 | tf_op jit(solution)/shard_map/all_to_all | solution.py:1166
  101.8 2.0 stacked.2.refs_1_
  111.5 17.4 %front.1 = (bf16[1024,1024]{1,0:T(8,128)(2,1)}, bf16[1024,128]{1,0:T(8,128)(2,1)}, bf16[1024,3072]{1,0:T(8,128)(2,1)}, bf16[1024,1024]{1,0:T(8,128)(2,1)}, bf16[...) custom-call(s32[2]{0:T(128)} %pad_add_fusion.ids_ref.refs_0_, bf16[384,1024]{1,0:T(8,128)(2,1)} %copy-done.1, ...), custom_call_target="tpu_custom_call" | custom-call | flops 2044723 | tf_op jit(solution)/shard_map/front/pallas_call | solution.py:645
  129.0 14.4 %join.1 = (bf16[1024,128]{1,0:T(8,128)(2,1)}, bf16[1024,1024]{1,0:T(8,128)(2,1)}, bf16[1024,1024]{1,0:T(8,128)(2,1)}, bf16[1024,256]{1,0:T(8,128)(2,1)}, bf16[10...) custom-call(s32[2]{0:T(128)} %pad_add_fusion.ids_ref.refs_0_, bf16[384,1024]{1,0:T(8,128)(2,1)} %copy-done.1, ...), custom_call_target="tpu_custom_call" | custom-call | flops 681574 | tf_op jit(solution)/shard_map/join/pallas_call | solution.py:704
  146.6 5.3 %all-to-all-start.3 = ((bf16[4,128,1152]{2,1,0:T(8,128)(2,1)}), bf16[4,128,1152]{2,1,0:T(8,128)(2,1)S(1)}, u32[]{:S(2)}, u32[]{:S(2)}) async-start(bf16[4,128,1152]{2,1,0:T(8,128)(2,1)} %bitcast.10), calls=%async_computation.3 | async-start | bytes 2359296 | tf_op jit(solution)/shard_map/all_to_all | solution.py:1166
  155.5 37.0 %ffn0.1 = (bf16[1024,1024]{1,0:T(8,128)(2,1)}, bf16[1024,1024]{1,0:T(8,128)(2,1)}, f32[1024,256]{1,0:T(8,128)}, f32[1024,128]{1,0:T(8,128)}, bf16[8,4,3,16,384]{4,3,2,1,0:T(8,128)(2,1)}) custom-call(s32[2]{0:T(128)} %pad_add_fusion.ids_ref.refs_0_, bf16[384,1152]{1,0:T(8,128)(2,1)} %stacked.2.refs_1_, bf16[384,1152]{1,0:T(8,128)(2,1)} %collective-permute-done.12.refs_2_, ...), custom_call_target="tpu_custom_call" | custom-call | flops 6134169 | tf_op jit(solution)/shard_map/ffn0/pallas_call | solution.py:893
  198.9 37.4 %ffn1.1 = (bf16[1024,1024]{1,0:T(8,128)(2,1)}, bf16[1024,1024]{1,0:T(8,128)(2,1)}, f32[1024,256]{1,0:T(8,128)}, f32[1024,128]{1,0:T(8,128)}, bf16[8,4,6,16,384]{4,3,2,1,0:T(8,128)(2,1)}) custom-call(s32[2]{0:T(128)} %pad_add_fusion.ids_ref.refs_0_, bf16[384,1152]{1,0:T(8,128)(2,1)} %copy-done.2, bf16[384,1152]{1,0:T(8,128)(2,1)} %collective-permute-done.19.refs_2_, ...), custom_call_target="tpu_custom_call" | custom-call | flops 6134169 | tf_op jit(solution)/shard_map/ffn1/pallas_call | solution.py:893
  237.3 3.8 all-to-all-start.4
  242.2 2.2 collective-permute-done.29.refs_5_
  247.9 37.0 %ffn2.1 = (bf16[1024,1024]{1,0:T(8,128)(2,1)}, bf16[1024,1024]{1,0:T(8,128)(2,1)}, f32[1024,256]{1,0:T(8,128)}, f32[1024,128]{1,0:T(8,128)}, bf16[8,4,3,16,384]{4,3,2,1,0:T(8,128)(2,1)}) custom-call(s32[2]{0:T(128)} %pad_add_fusion.ids_ref.refs_0_, bf16[384,1152]{1,0:T(8,128)(2,1)} %others.3.refs_1_, bf16[384,1152]{1,0:T(8,128)(2,1)} %copy-done.24, ...), custom_call_target="tpu_custom_call" | custom-call | flops 6134169 | tf_op jit(solution)/shard_map/ffn2/pallas_call | solution.py:893
  285.0 3.9 %all-to-all-start.5 = ((bf16[8,192,384]{2,1,0:T(8,128)(2,1)}), bf16[8,192,384]{2,1,0:T(8,128)(2,1)S(1)}, u32[]{:S(2)}, u32[]{:S(2)}) async-start(bf16[8,192,384]{2,1,0:T(8,128)(2,1)} %bitcast.29), calls=%async_computation.5 | async-start | bytes 2359296 | tf_op jit(solution)/shard_map/all_to_all | solution.py:1166
  288.9 12.5 %middle.1 = (bf16[1024,1024]{1,0:T(8,128)(2,1)}, bf16[1024,1024]{1,0:T(8,128)(2,1)}, bf16[1024,128]{1,0:T(8,128)(2,1)}, bf16[8,4,16,1280]{3,2,1,0:T(8,128)(2,1)}) custom-call(bf16[1024,1024]{1,0:T(8,128)(2,1)} %get-tuple-element.129.dn_hbm, bf16[1024,1024]{1,0:T(8,128)(2,1)} %get-tuple-element.104.refs_15_.n2_hbm, ...), custom_call_target="tpu_custom_call" | custom-call | flops 2097152 | tf_op jit(solution)/shard_map/middle/pallas_call | solution.py:984
  301.4 4.3 %all-to-all-done.5 = bf16[8,192,384]{2,1,0:T(8,128)(2,1)S(1)} async-done(((bf16[8,192,384]{2,1,0:T(8,128)(2,1)}), bf16[8,192,384]{2,1,0:T(8,128)(2,1)S(1)}, u32[]{:S(2)}, u32[]{:S(2)}) %all-to-all-start.5) | async-done | bytes 1179680 | tf_op jit(solution)/shard_map/all_to_all | solution.py:1166
  305.7 4.5 %all-to-all-start.6 = ((bf16[8,64,1280]{2,1,0:T(8,128)(2,1)}), bf16[8,64,1280]{2,1,0:T(8,128)(2,1)}, u32[]{:S(2)}, u32[]{:S(2)}) async-start(bf16[8,64,1280]{2,1,0:T(8,128)(2,1)} %bitcast.27), calls=%async_computation.6 | async-start | bytes 2621440 | tf_op jit(solution)/shard_map/all_to_all | solution.py:1166
  313.8 19.1 %back.1 = (bf16[1024,3072]{1,0:T(8,128)(2,1)}, bf16[1024,128]{1,0:T(8,128)(2,1)}, bf16[8,4,16,1024]{3,2,1,0:T(8,128)(2,1)}) custom-call(bf16[1024,1024]{1,0:T(8,128)(2,1)} %get-tuple-element.138.w_out_hbm, bf16[1024,1024]{1,0:T(8,128)(2,1)} %get-tuple-element.139.dhb_hbm.dh_hbm, bf16[1024,1024]{1,0:T(8,128)(2,1)} %get-tuple-element.140.cv_hbm, ...), custom_call_target="tpu_custom_call" | custom-call | flops 2097152 | tf_op jit(solution)/shard_map/back/pallas_call | solution.py:1048
  332.9 4.3 %all-to-all-start.7 = ((bf16[8,64,1024]{2,1,0:T(8,128)(2,1)}), bf16[8,64,1024]{2,1,0:T(8,128)(2,1)S(1)}, u32[]{:S(2)}, u32[]{:S(2)}) async-start(bf16[8,64,1024]{2,1,0:T(8,128)(2,1)} %bitcast.30), calls=%async_computation.7 | async-start | bytes 2097152 | tf_op jit(solution)/shard_map/all_to_all | solution.py:1166
  339.2 2.4 collective-permute-start.44
  343.0 16.4 %last.1 = bf16[1024,1024]{1,0:T(8,128)(2,1)} custom-call(bf16[1024,3072]{1,0:T(8,128)(2,1)} %get-tuple-element.148.dp_hbm, bf16[1024,3072]{1,0:T(8,128)(2,1)} %get-tuple-element.149.w_in_hbm, bf16[1024,1024]{1,0:T(8,128)(2,1)} %get-tuple-element.139.dhb_hbm.dh_hbm, bf16[1024,1024]{1,0:T(8,128)(2,1)} %x_hbm.1, bf16[1024,128]{1,0:T(8,128)(2,1)} %get-tuple-element.150.dzi_ref, ...), custom_call_target="tpu_custom_call" | custom-call | flops 2097152 | tf_op jit(solution)/shard_map/last/pallas_call | solution.py:1095
  362.3 2.7 collective-permute-start.35
  365.1 2.0 collective-permute-start.46
  368.6 2.4 collective-permute-start.48
  (181 shorter events, 67.7 us)
Async XLA Ops:
  0.6 31.8 %all-to-all-start = ((bf16[8,128,1024]{2,1,0:T(8,128)(2,1)}), bf16[8,128,1024]{2,1,0:T(8,128)(2,1)S(1)}, u32[]{:S(2)}, u32[]{:S(2)}) async-start(bf16[8,128,1024]{2,1,0:T(8,128)(2,1)} %bitcast.26), calls=%async_computation | async-start | bytes 4194304 | tf_op jit(solution)/shard_map/all_to_all | solution.py:1208
  9.1 29.8 %collective-permute-start = (bf16[128,2176]{1,0:T(8,128)(2,1)}, bf16[128,2176]{1,0:T(8,128)(2,1)S(1)}, u32[]{:S(2)}, u32[]{:S(2)}) collective-permute-start(bf16[128,2176]{1,0:T(8,128)(2,1)} %own.2), channel_id=1, source_target_pairs={{0,1},{1,2},{2,3},{3,0},{4,5},{5,6},{6,7},{7,4},{8,9},{9,10},{10,1... | collective-permute-start | bytes 1671176 | tf_op jit(solution)/shard_map/ppermute | solution.py:440
  10.8 39.5 %collective-permute-start.1 = (bf16[128,2176]{1,0:T(8,128)(2,1)}, bf16[128,2176]{1,0:T(8,128)(2,1)S(1)}, u32[]{:S(2)}, u32[]{:S(2)}) collective-permute-start(bf16[128,2176]{1,0:T(8,128)(2,1)} %own.2), channel_id=1, source_target_pairs={{0,2},{1,3},{2,0},{3,1},{4,6},{5,7},{6,4},{7,5},{8,10},{9,11},{10,... | collective-permute-start | bytes 1671176 | tf_op jit(solution)/shard_map/ppermute | solution.py:440
  13.3 36.9 %collective-permute-start.2 = (bf16[128,2176]{1,0:T(8,128)(2,1)}, bf16[128,2176]{1,0:T(8,128)(2,1)}, u32[]{:S(2)}, u32[]{:S(2)}) collective-permute-start(bf16[128,2176]{1,0:T(8,128)(2,1)} %own.2), channel_id=1, source_target_pairs={{0,3},{1,0},{2,1},{3,2},{4,7},{5,4},{6,5},{7,6},{8,11},{9,8},{10,9... | collective-permute-start | bytes 1671176 | tf_op jit(solution)/shard_map/ppermute | solution.py:440
  34.5 60.6 %all-to-all-start.1 = ((bf16[8,128,1024]{2,1,0:T(8,128)(2,1)}), bf16[8,128,1024]{2,1,0:T(8,128)(2,1)}, u32[]{:S(2)}, u32[]{:S(2)}) async-start(bf16[8,128,1024]{2,1,0:T(8,128)(2,1)} %bitcast.22), calls=%async_computation.1 | async-start | bytes 4194304 | tf_op jit(solution)/shard_map/all_to_all | solution.py:1215
  51.3 30.0 %collective-permute-start.4 = (bf16[384,1024]{1,0:T(8,128)(2,1)S(1)}, bf16[384,1024]{1,0:T(8,128)(2,1)S(1)}, u32[]{:S(2)}, u32[]{:S(2)}) collective-permute-start(bf16[384,1024]{1,0:T(8,128)(2,1)S(1)} %stacked.3.refs_1_), channel_id=1, source_target_pairs={{0,16},{4,20},{8,24},{12,28},{16,0},{20,4},{24,8},{28,12},{1,17},{... | collective-permute-start | bytes 2359304 | tf_op jit(solution)/shard_map/ppermute | solution.py:339
  53.1 29.8 %collective-permute-start.3 = (bf16[384,1024]{1,0:T(8,128)(2,1)S(1)}, bf16[384,1024]{1,0:T(8,128)(2,1)S(1)}, u32[]{:S(2)}, u32[]{:S(2)}) collective-permute-start(bf16[384,1024]{1,0:T(8,128)(2,1)S(1)} %stacked.3.refs_1_), channel_id=1, source_target_pairs={{0,8},{4,12},{8,0},{12,4},{16,24},{20,28},{24,16},{28,20},{1,9},{5... | collective-permute-start | bytes 2359304 | tf_op jit(solution)/shard_map/ppermute | solution.py:339
  81.4 13.8 %collective-permute-start.6 = (bf16[256,1024]{1,0:T(8,128)(2,1)S(1)}, bf16[256,1024]{1,0:T(8,128)(2,1)}, u32[]{:S(2)}, u32[]{:S(2)}) collective-permute-start(bf16[256,1024]{1,0:T(8,128)(2,1)S(1)} %slice.9), channel_id=1, source_target_pairs={{0,8},{4,12},{8,0},{12,4},{16,24},{20,28},{24,16},{28,20},{1,9},{5... | collective-permute-start | bytes 1572872 | tf_op jit(solution)/shard_map/ppermute | solution.py:339
  95.2 50.6 %all-to-all-start.2 = ((bf16[4,128,1152]{2,1,0:T(8,128)(2,1)}), bf16[4,128,1152]{2,1,0:T(8,128)(2,1)S(1)}, u32[]{:S(2)}, u32[]{:S(2)}) async-start(bf16[4,128,1152]{2,1,0:T(8,128)(2,1)} %bitcast.28), calls=%async_computation.2 | async-start | bytes 2359296 | tf_op jit(solution)/shard_map/all_to_all | solution.py:1166
  103.9 39.5 %collective-permute-start.14 = (bf16[384,1152]{1,0:T(8,128)(2,1)}, bf16[384,1152]{1,0:T(8,128)(2,1)}, u32[]{:S(2)}, u32[]{:S(2)}) collective-permute-start(bf16[384,1152]{1,0:T(8,128)(2,1)} %stacked.2.refs_1_), channel_id=1, source_target_pairs={{0,24},{4,28},{8,16},{12,20},{16,8},{20,12},{24,0},{28,4},{1,25},{... | collective-permute-start | bytes 2654216 | tf_op jit(solution)/shard_map/ppermute | solution.py:339
  103.9 41.3 %collective-permute-start.13 = (bf16[384,1152]{1,0:T(8,128)(2,1)}, bf16[384,1152]{1,0:T(8,128)(2,1)}, u32[]{:S(2)}, u32[]{:S(2)}) collective-permute-start(bf16[384,1152]{1,0:T(8,128)(2,1)} %stacked.2.refs_1_), channel_id=1, source_target_pairs={{0,16},{4,20},{8,24},{12,28},{16,0},{20,4},{24,8},{28,12},{1,17},{... | collective-permute-start | bytes 2654216 | tf_op jit(solution)/shard_map/ppermute | solution.py:339
  105.7 39.6 %collective-permute-start.12 = (bf16[384,1152]{1,0:T(8,128)(2,1)}, bf16[384,1152]{1,0:T(8,128)(2,1)}, u32[]{:S(2)}, u32[]{:S(2)}) collective-permute-start(bf16[384,1152]{1,0:T(8,128)(2,1)} %stacked.2.refs_1_), channel_id=1, source_target_pairs={{0,8},{4,12},{8,0},{12,4},{16,24},{20,28},{24,16},{28,20},{1,9},{5... | collective-permute-start | bytes 2654216 | tf_op jit(solution)/shard_map/ppermute | solution.py:339
  109.9 43.2 %collective-permute-start.15 = (bf16[384,1152]{1,0:T(8,128)(2,1)}, bf16[384,1152]{1,0:T(8,128)(2,1)}, u32[]{:S(2)}, u32[]{:S(2)}) collective-permute-start(bf16[384,1152]{1,0:T(8,128)(2,1)} %stacked.2.refs_1_), channel_id=1, source_target_pairs={{0,4},{4,0},{8,12},{12,8},{16,20},{20,16},{24,28},{28,24},{1,5},{5... | collective-permute-start | bytes 2654216 | tf_op jit(solution)/shard_map/ppermute | solution.py:339
  143.4 11.1 %collective-permute-start.18 = (bf16[384,1152]{1,0:T(8,128)(2,1)}, bf16[384,1152]{1,0:T(8,128)(2,1)}, u32[]{:S(2)}, u32[]{:S(2)}) collective-permute-start(bf16[384,1152]{1,0:T(8,128)(2,1)} %collective-permute-done.14.refs_4_), channel_id=1, source_target_pairs={{0,4},{4,0},{8,12},{12,8},{16,20},{20,16},{24,28},{28,24},{1,5},{5... | collective-permute-start | bytes 2654216 | tf_op jit(solution)/shard_map/ppermute | solution.py:339
  145.3 9.3 %collective-permute-start.17 = (bf16[384,1152]{1,0:T(8,128)(2,1)}, bf16[384,1152]{1,0:T(8,128)(2,1)}, u32[]{:S(2)}, u32[]{:S(2)}) collective-permute-start(bf16[384,1152]{1,0:T(8,128)(2,1)} %collective-permute-done.13.refs_3_), channel_id=1, source_target_pairs={{0,4},{4,0},{8,12},{12,8},{16,20},{20,16},{24,28},{28,24},{1,5},{5... | collective-permute-start | bytes 2654216 | tf_op jit(solution)/shard_map/ppermute | solution.py:339
  145.3 10.2 %collective-permute-start.16 = (bf16[384,1152]{1,0:T(8,128)(2,1)}, bf16[384,1152]{1,0:T(8,128)(2,1)}, u32[]{:S(2)}, u32[]{:S(2)}) collective-permute-start(bf16[384,1152]{1,0:T(8,128)(2,1)} %collective-permute-done.12.refs_2_), channel_id=1, source_target_pairs={{0,4},{4,0},{8,12},{12,8},{16,20},{20,16},{24,28},{28,24},{1,5},{5... | collective-permute-start | bytes 2654216 | tf_op jit(solution)/shard_map/ppermute | solution.py:339
  146.6 47.1 %all-to-all-start.3 = ((bf16[4,128,1152]{2,1,0:T(8,128)(2,1)}), bf16[4,128,1152]{2,1,0:T(8,128)(2,1)S(1)}, u32[]{:S(2)}, u32[]{:S(2)}) async-start(bf16[4,128,1152]{2,1,0:T(8,128)(2,1)} %bitcast.10), calls=%async_computation.3 | async-start | bytes 2359296 | tf_op jit(solution)/shard_map/all_to_all | solution.py:1166
  151.9 40.7 %collective-permute-start.21 = (bf16[384,1152]{1,0:T(8,128)(2,1)S(1)}, bf16[384,1152]{1,0:T(8,128)(2,1)S(1)}, u32[]{:S(2)}, u32[]{:S(2)}) collective-permute-start(bf16[384,1152]{1,0:T(8,128)(2,1)S(1)} %others.2.refs_1_), channel_id=1, source_target_pairs={{0,24},{4,28},{8,16},{12,20},{16,8},{20,12},{24,0},{28,4},{1,25},{... | collective-permute-start | bytes 2654216 | tf_op jit(solution)/shard_map/ppermute | solution.py:339
  153.1 40.1 %collective-permute-start.20 = (bf16[384,1152]{1,0:T(8,128)(2,1)S(1)}, bf16[384,1152]{1,0:T(8,128)(2,1)}, u32[]{:S(2)}, u32[]{:S(2)}) collective-permute-start(bf16[384,1152]{1,0:T(8,128)(2,1)S(1)} %others.2.refs_1_), channel_id=1, source_target_pairs={{0,16},{4,20},{8,24},{12,28},{16,0},{20,4},{24,8},{28,12},{1,17},{... | collective-permute-start | bytes 2654216 | tf_op jit(solution)/shard_map/ppermute | solution.py:339
  154.5 42.1 %collective-permute-start.23 = (bf16[384,1152]{1,0:T(8,128)(2,1)S(1)}, bf16[384,1152]{1,0:T(8,128)(2,1)}, u32[]{:S(2)}, u32[]{:S(2)}) collective-permute-start(bf16[384,1152]{1,0:T(8,128)(2,1)S(1)} %others.2.refs_1_), channel_id=1, source_target_pairs={{0,4},{4,0},{8,12},{12,8},{16,20},{20,16},{24,28},{28,24},{1,5},{5... | collective-permute-start | bytes 2654216 | tf_op jit(solution)/shard_map/ppermute | solution.py:339
  154.5 38.7 %collective-permute-start.19 = (bf16[384,1152]{1,0:T(8,128)(2,1)S(1)}, bf16[384,1152]{1,0:T(8,128)(2,1)}, u32[]{:S(2)}, u32[]{:S(2)}) collective-permute-start(bf16[384,1152]{1,0:T(8,128)(2,1)S(1)} %others.2.refs_1_), channel_id=1, source_target_pairs={{0,8},{4,12},{8,0},{12,4},{16,24},{20,28},{24,16},{28,20},{1,9},{5... | collective-permute-start | bytes 2654216 | tf_op jit(solution)/shard_map/ppermute | solution.py:339
  195.4 41.0 %collective-permute-start.22 = (bf16[384,1152]{1,0:T(8,128)(2,1)}, bf16[384,1152]{1,0:T(8,128)(2,1)S(1)}, u32[]{:S(2)}, u32[]{:S(2)}) collective-permute-start(bf16[384,1152]{1,0:T(8,128)(2,1)} %others.3.refs_1_), channel_id=1, source_target_pairs={{0,8},{4,12},{8,0},{12,4},{16,24},{20,28},{24,16},{28,20},{1,9},{5... | collective-permute-start | bytes 2654216 | tf_op jit(solution)/shard_map/ppermute | solution.py:339
  196.6 39.7 %collective-permute-start.27 = (bf16[384,1152]{1,0:T(8,128)(2,1)}, bf16[384,1152]{1,0:T(8,128)(2,1)}, u32[]{:S(2)}, u32[]{:S(2)}) collective-permute-start(bf16[384,1152]{1,0:T(8,128)(2,1)} %others.3.refs_1_), channel_id=1, source_target_pairs={{0,16},{4,20},{8,24},{12,28},{16,0},{20,4},{24,8},{28,12},{1,17},{... | collective-permute-start | bytes 2654216 | tf_op jit(solution)/shard_map/ppermute | solution.py:339
  197.2 40.0 %collective-permute-start.28 = (bf16[384,1152]{1,0:T(8,128)(2,1)}, bf16[384,1152]{1,0:T(8,128)(2,1)}, u32[]{:S(2)}, u32[]{:S(2)}) collective-permute-start(bf16[384,1152]{1,0:T(8,128)(2,1)} %others.3.refs_1_), channel_id=1, source_target_pairs={{0,24},{4,28},{8,16},{12,20},{16,8},{20,12},{24,0},{28,4},{1,25},{... | collective-permute-start | bytes 2654216 | tf_op jit(solution)/shard_map/ppermute | solution.py:339
  237.3 47.7 %all-to-all-start.4 = ((bf16[8,384,384]{2,1,0:T(8,128)(2,1)}), bf16[8,384,384]{2,1,0:T(8,128)(2,1)S(1)}, u32[]{:S(2)}, u32[]{:S(2)}) async-start(bf16[8,384,384]{2,1,0:T(8,128)(2,1)} %bitcast.25), calls=%async_computation.4 | async-start | bytes 4718592 | tf_op jit(solution)/shard_map/all_to_all | solution.py:1166
  285.0 20.8 %all-to-all-start.5 = ((bf16[8,192,384]{2,1,0:T(8,128)(2,1)}), bf16[8,192,384]{2,1,0:T(8,128)(2,1)S(1)}, u32[]{:S(2)}, u32[]{:S(2)}) async-start(bf16[8,192,384]{2,1,0:T(8,128)(2,1)} %bitcast.29), calls=%async_computation.5 | async-start | bytes 2359296 | tf_op jit(solution)/shard_map/all_to_all | solution.py:1166
  305.7 27.2 %all-to-all-start.6 = ((bf16[8,64,1280]{2,1,0:T(8,128)(2,1)}), bf16[8,64,1280]{2,1,0:T(8,128)(2,1)}, u32[]{:S(2)}, u32[]{:S(2)}) async-start(bf16[8,64,1280]{2,1,0:T(8,128)(2,1)} %bitcast.27), calls=%async_computation.6 | async-start | bytes 2621440 | tf_op jit(solution)/shard_map/all_to_all | solution.py:1166
  332.9 26.5 %all-to-all-start.7 = ((bf16[8,64,1024]{2,1,0:T(8,128)(2,1)}), bf16[8,64,1024]{2,1,0:T(8,128)(2,1)S(1)}, u32[]{:S(2)}, u32[]{:S(2)}) async-start(bf16[8,64,1024]{2,1,0:T(8,128)(2,1)} %bitcast.30), calls=%async_computation.7 | async-start | bytes 2097152 | tf_op jit(solution)/shard_map/all_to_all | solution.py:1166
  337.2 24.5 %collective-permute-start.43 = (bf16[9,16,384]{2,1,0:T(8,128)(2,1)S(1)}, bf16[9,16,384]{2,1,0:T(8,128)(2,1)S(1)}, u32[]{:S(2)}, u32[]{:S(2)}) collective-permute-start(bf16[9,16,384]{2,1,0:T(8,128)(2,1)S(1)} %copy-done.13), channel_id=1, source_target_pairs={{0,1},{1,2},{2,3},{3,0},{4,5},{5,6},{6,7},{7,4},{8,9},{9,10},{10,1... | collective-permute-start | bytes 331784 | tf_op jit(solution)/shard_map/ppermute | solution.py:1172
  339.2 25.8 %collective-permute-start.44 = (bf16[9,16,384]{2,1,0:T(8,128)(2,1)S(1)}, bf16[9,16,384]{2,1,0:T(8,128)(2,1)S(1)}, u32[]{:S(2)}, u32[]{:S(2)}) collective-permute-start(bf16[9,16,384]{2,1,0:T(8,128)(2,1)S(1)} %copy-done.11), channel_id=1, source_target_pairs={{0,2},{1,3},{2,0},{3,1},{4,6},{5,7},{6,4},{7,5},{8,10},{9,11},{10,... | collective-permute-start | bytes 331784 | tf_op jit(solution)/shard_map/ppermute | solution.py:1172
  341.5 23.5 %collective-permute-start.45 = (bf16[9,16,384]{2,1,0:T(8,128)(2,1)S(1)}, bf16[9,16,384]{2,1,0:T(8,128)(2,1)S(1)}, u32[]{:S(2)}, u32[]{:S(2)}) collective-permute-start(bf16[9,16,384]{2,1,0:T(8,128)(2,1)S(1)} %copy-done.9), channel_id=1, source_target_pairs={{0,3},{1,0},{2,1},{3,2},{4,7},{5,4},{6,5},{7,6},{8,11},{9,8},{10,9... | collective-permute-start | bytes 331784 | tf_op jit(solution)/shard_map/ppermute | solution.py:1172
  361.7 9.2 %collective-permute-start.34 = (bf16[16,2304]{1,0:T(8,128)(2,1)S(1)}, bf16[16,2304]{1,0:T(8,128)(2,1)S(1)}, u32[]{:S(2)}, u32[]{:S(2)}) collective-permute-start(bf16[16,2304]{1,0:T(8,128)(2,1)S(1)} %get-tuple-element.156), channel_id=1, source_target_pairs={{0,2},{1,3},{2,0},{3,1},{4,6},{5,7},{6,4},{7,5},{8,10},{9,11},{10,... | collective-permute-start | bytes 221192 | tf_op jit(solution)/shard_map/ppermute | solution.py:1172
  (58 other events, 426.3 us)
